TPU v7x, 256 devices: a whole 4x4x8 slice. The times are simulated.
256 devices in a mesh: stn: 8 (over x, z_lo), tm: 32 (over z_hi, y, core).
Axes of the slice: x: 4, y: 4, z: 8 (z_hi: 4, z_lo: 2; z = z_hi * 2 + z_lo), core: 2. Of those that a mesh axis runs over, the one named last changes fastest.
Arguments:
- spectra: bfloat16 [16, 8, 128, 2, 4096], P('stn', None, 'tm'), may hold values from -6 to 6
- flags: int32 [16, 8, 128, 32], P('stn', None, 'tm'), may hold values from 0 to 1, as said below
- poly_index: int32 [16, 8, 128], P('stn', None, 'tm'), may hold values from 0 to 63
- delay_model: float32 [64, 3], replicated, may hold values from -48 to 48
- partner_order: int32 [16], replicated, may hold values from 0 to 15, each once
Outputs:
- fringe: float32 [2, 256, 8, 256], P(None, ('stn', 'tm'))
Inputs may be any that keep to these rules, and one draw needn't show every extreme that they name: `flags`: 1 marks a flagged block; whole blocks of a station can be flagged for the full window. `partner_order`: each station appears once.
All inputs are finite; a program needn't handle non-finite values.
Results may differ from a plain program's by a relative error of at most 0.003.
Values may be sent and summed in bfloat16 or wider, within the bound.
No kernel may reach another device: no remote copies, remote signals or barrier semaphores. Data moves between devices by JAX's collectives and lax.ppermute only.
A program may use at most 128 MiB of HBM per device.

v0:
```python
import math

import jax
import jax.numpy as jnp
from jax import lax
from jax.sharding import Mesh
from jax.sharding import PartitionSpec as P

LAGS = 256
STN = ("stn_0", "stn_1")
STN_TM = ("stn_0", "stn_1", "tm")


def sent_to_all(shard, axis):
    copies = jnp.broadcast_to(shard, (lax.axis_size(axis), *shard.shape))
    return lax.all_to_all(copies, axis, split_axis=0, concat_axis=0, tiled=True)


def laid_out(pieces, dim):
    pieces = jnp.moveaxis(pieces, 0, dim)
    dims = pieces.shape
    return pieces.reshape(*dims[:dim], dims[dim] * dims[dim + 1], *dims[dim + 2 :])


def gathered_copies(shard, axis, dim):
    pieces = sent_to_all(shard, axis)
    return laid_out(pieces, dim)


def whole_of(shard, axes, dim):
    result = shard
    for number in range(len(axes) - 1, -1, -1):
        result = lax.all_gather(result, axes[number], axis=dim, tiled=True)
    return result


def split_up(shard, dim, size):
    dims = shard.shape
    pieces = shard.reshape(*dims[:dim], size, dims[dim] // size, *dims[dim + 1 :])
    return jnp.moveaxis(pieces, dim, 0)


def summed_on_arrival(shard, axis, dim):
    pieces = split_up(shard, dim, lax.axis_size(axis))
    arrived = lax.all_to_all(pieces, axis, split_axis=0, concat_axis=0, tiled=True)
    return arrived.astype(jnp.float32).sum(axis=0)


def rotate(spectra, flags, coeffs, times, total_time):
    channels = spectra.shape[-1]
    blocks = flags.shape[-1]
    moment = times / total_time
    delay = coeffs[..., 0] + coeffs[..., 1] * moment + coeffs[..., 2] * moment * moment
    freq = jnp.arange(channels, dtype=jnp.int32).astype(jnp.float32) * (math.pi / channels)
    phase = delay[..., None] * freq
    cosine = jnp.cos(phase)
    sine = jnp.sin(phase)
    real = spectra[..., 0, :].astype(jnp.float32)
    imag = spectra[..., 1, :].astype(jnp.float32)
    weight = 1.0 - flags.astype(jnp.float32)
    weight = jnp.broadcast_to(weight[..., None], weight.shape + (channels // blocks,)).reshape(
        real.shape
    )
    new_real = weight * (real * cosine + imag * sine)
    new_imag = weight * (imag * cosine - real * sine)
    return jnp.stack([new_real, new_imag], axis=-2).astype(jnp.bfloat16)


def transform(vis, counts, lags):
    rows, periods, _, channels = vis.shape
    blocks = counts.shape[-1]
    scale = 1.0 / jnp.sqrt(jnp.maximum(counts, 1.0))
    normed = vis.reshape(rows, periods, 2, blocks, channels // blocks) * scale[:, :, None, :, None]
    normed = normed.reshape(rows, periods, 2, channels)
    index = jnp.arange(lags, dtype=jnp.int32)
    middle = lags // 2
    delays = jnp.where(index < middle, index - middle, index - middle + 1)
    turns = jnp.arange(channels, dtype=jnp.int32)[:, None] * delays[None, :] % channels
    angle = turns.astype(jnp.float32) * (2.0 * math.pi / channels)
    cosine = jnp.cos(angle)
    sine = jnp.sin(angle)
    highest = lax.Precision.HIGHEST
    real = normed[:, :, 0].reshape(rows * periods, channels)
    imag = normed[:, :, 1].reshape(rows * periods, channels)
    part_real = jnp.dot(real, cosine, precision=highest) + jnp.dot(imag, sine, precision=highest)
    part_imag = jnp.dot(imag, cosine, precision=highest) - jnp.dot(real, sine, precision=highest)
    part_real = part_real.reshape(rows, periods, lags)
    part_imag = part_imag.reshape(rows, periods, lags)
    pidx = jnp.arange(periods, dtype=jnp.int32)
    pturn = pidx[:, None] * pidx[None, :] % periods
    pangle = pturn.astype(jnp.float32) * (2.0 * math.pi / periods)
    pcos = jnp.cos(pangle)
    psin = jnp.sin(pangle)
    out_real = jnp.einsum("rp,npl->nrl", pcos, part_real, precision=highest) + jnp.einsum(
        "rp,npl->nrl", psin, part_imag, precision=highest
    )
    out_imag = jnp.einsum("rp,npl->nrl", pcos, part_imag, precision=highest) - jnp.einsum(
        "rp,npl->nrl", psin, part_real, precision=highest
    )
    factor = 1.0 / math.sqrt(periods * channels)
    return jnp.stack([out_real, out_imag]) * factor


def correlate(mine, theirs):
    mine_real = mine[:, :, :, 0].astype(jnp.float32)[:, None]
    mine_imag = mine[:, :, :, 1].astype(jnp.float32)[:, None]
    their_real = theirs[:, :, :, 0].astype(jnp.float32)[None]
    their_imag = theirs[:, :, :, 1].astype(jnp.float32)[None]
    real = jnp.sum(mine_real * their_real + mine_imag * their_imag, axis=3)
    imag = jnp.sum(mine_imag * their_real - mine_real * their_imag, axis=3)
    return jnp.stack([real, imag], axis=3)


def per_device(spectra, flags, poly_index, delay_model, partner_order):
    local_count, periods, depth, _, channels = spectra.shape
    cycle_size = lax.axis_size(STN)
    time_width = lax.axis_size("tm")
    stations = local_count * cycle_size
    total_time = float(periods * depth * time_width)
    first_time = lax.axis_index("tm") * depth
    times = (
        jnp.arange(periods, dtype=jnp.int32)[:, None] * (depth * time_width)
        + first_time
        + jnp.arange(depth, dtype=jnp.int32)[None, :]
    ).astype(jnp.float32)
    table_rows = delay_model.shape[0]
    onehot = (poly_index[..., None] == jnp.arange(table_rows, dtype=jnp.int32)).astype(jnp.float32)
    coeffs = jnp.dot(onehot.reshape(-1, table_rows), delay_model, precision=lax.Precision.HIGHEST)
    coeffs = coeffs.reshape(local_count, periods, depth, 3)
    rotated = rotate(spectra, flags, coeffs, times, total_time)
    all_flags = gathered_copies(flags, STN, 0)
    local_weight = 1.0 - flags.astype(jnp.float32)
    all_weight = 1.0 - all_flags.astype(jnp.float32)
    counts = jnp.einsum(
        "apkx,bpkx->abpx", local_weight, all_weight, precision=lax.Precision.HIGHEST
    )
    working = lax.all_to_all(rotated, "tm", split_axis=4, concat_axis=2, tiled=True)
    band = working.shape[-1]
    block = correlate(working, whole_of(working, STN, 0))
    vis_rows = jnp.take(block, partner_order, axis=1).reshape(
        local_count * stations, periods, 2, band
    )
    count_rows = jnp.take(counts, partner_order, axis=1).reshape(
        local_count * stations, periods, counts.shape[-1]
    )
    owned_counts = summed_on_arrival(count_rows.astype(jnp.bfloat16), "tm", 0)
    owned_vis = lax.all_to_all(vis_rows, "tm", split_axis=0, concat_axis=3, tiled=True)
    return transform(owned_vis, owned_counts, LAGS)


def solution(mesh):
    finer = Mesh(mesh.devices.reshape(4, 2, mesh.shape["tm"]), ("stn_0", "stn_1", "tm"))
    return jax.shard_map(
        per_device,
        mesh=finer,
        in_specs=(
            P(STN, None, "tm", None, None),
            P(STN, None, "tm", None),
            P(STN, None, "tm"),
            P(),
            P(),
        ),
        out_specs=P(None, STN_TM, None, None),
        check_vma=False,
    )
```

profile of v0, /device:TPU:1, one launch (start us, length us, event | category | flops | bytes accessed | tf_op | source)
XLA Modules:
  0.0 385.3 jit_solution(1203339314235424996)
XLA Ops:
  6.6 0.9 convert_subtract_fusion.1
  8.0 3.2 fusion.100
  11.6 7.0 %fusion.32 = (bf16[2,8,4,1,4096]{4,1,2,0,3:T(8,128)(2,1)S(1)}, bf16[2,8,4,1,4096]{4,1,2,0,3:T(8,128)(2,1)S(1)}) fusion(f32[2,8,4,1,4096]{4,1,2,0,3:T(8,128)S(1)} %reshape.199, f32[4096]{0:T(1024)S(1)} %convert_multiply_fusion, f32[2,8,4]{1,2,0:T(4,128)S(1)} %bitcast.102, bf16[2,8,4,1,4096]{4,3,2,1,0:T(2,128)(2,1)} %get-tuple-element.14, ...), kind=kLoop, calls=%fused_computation.38 | loop fusion | flops 3407872 | bytes 3162368 | tf_op jit(solution)/shard_map/convert.4
  18.8 17.0 %copy.95 = bf16[2,8,4,2,4096]{1,2,3,0,4:T(4,128)(2,1)} copy(bf16[2,8,4,2,4096]{4,1,2,0,3:T(8,128)(2,1)S(1)} %pad_maximum_fusion) | data formatting | bytes 2097152 | tf_op jit(solution)/shard_map/stack | solution.py:66
  35.8 19.8 %reshape.224 = bf16[32,2,8192]{2,1,0:T(2,128)(2,1)S(1)} reshape(bf16[4096,2,2,4,8]{4,3,2,1,0:T(4,128)(2,1)} %bitcast.91) | data formatting | bytes 2097152
  55.6 40.2 %all_to_all.43 = bf16[32,2,8192]{2,1,0:T(2,128)(2,1)S(1)} all-to-all(bf16[32,2,8192]{2,1,0:T(2,128)(2,1)S(1)} %reshape.224), channel_id=1, replica_groups=mesh['stn_0'=4,'stn_1'=2,'tm'=32] {'tm'}, dimensions={0} | all-to-all | bytes 2097152 | tf_op jit(solution)/shard_map/all_to_all | solution.py:137
  95.8 20.8 %reshape.225 = bf16[4096,2,2,4,8]{4,3,2,1,0:T(4,128)(2,1)} reshape(bf16[32,2,8192]{2,1,0:T(2,128)(2,1)S(1)} %all_to_all.43) | data formatting | bytes 2097152
  116.6 19.3 %copy.113 = bf16[2,8,4,2,32,128]{5,1,3,2,4,0:T(8,128)(2,1)S(1)} copy(bf16[2,8,4,2,32,128]{1,2,3,0,5,4:T(4,128)(2,1)} %bitcast.92) | data formatting | bytes 2097152 | tf_op jit(solution)/shard_map/all_to_all | solution.py:137
  135.9 1.2 copy.99
  137.2 35.9 %all-gather.3.cloned.1.call-done = bf16[4,8,128,2,128]{4,2,3,1,0:T(8,128)(2,1)} async-done(((bf16[2,8,128,2,128]{4,2,3,1,0:T(8,128)(2,1)}), bf16[4,8,128,2,128]{4,2,3,1,0:T(8,128)(2,1)}) %all-gather.3.cloned.1.call-update) | async-done | bytes 2097168 | tf_op jit(solution)/shard_map/all_gather | solution.py:33
  173.9 4.0 %all-to-all-start.2 = ((s32[8,1,2048]{2,1,0:T(1,128)}), s32[8,1,2048]{2,1,0:T(1,128)S(1)}, u32[]{:S(2)}, u32[]{:S(2)}) async-start(s32[8,1,2048]{2,1,0:T(1,128)} %reshape.226), calls=%async_computation.2 | async-start | bytes 131072 | tf_op jit(solution)/shard_map/all_to_all | solution.py:16
  178.2 4.9 %all-to-all-done.2 = s32[8,1,2048]{2,1,0:T(1,128)S(1)} async-done(((s32[8,1,2048]{2,1,0:T(1,128)}), s32[8,1,2048]{2,1,0:T(1,128)S(1)}, u32[]{:S(2)}, u32[]{:S(2)}) %all-to-all-start.2) | async-done | bytes 65568 | tf_op jit(solution)/shard_map/all_to_all | solution.py:16
  184.9 1.8 convolution_bitcast_fusion
  188.3 23.2 %all-to-all-start.3 = ((bf16[32,2,128]{2,1,0:T(2,128)(2,1)}), bf16[32,2,128]{2,1,0:T(2,128)(2,1)S(1)}, u32[]{:S(2)}, u32[]{:S(2)}) async-start(bf16[32,2,128]{2,1,0:T(2,128)(2,1)} %reshape.228), calls=%async_computation.3 | async-start | bytes 32768 | tf_op jit(solution)/shard_map/all_to_all | solution.py:45
  212.1 48.9 %all-gather.5.cloned.1.call-done = bf16[16,8,128,2,128]{4,2,3,1,0:T(8,128)(2,1)} async-done(((bf16[4,8,128,2,128]{4,2,3,1,0:T(8,128)(2,1)}), bf16[16,8,128,2,128]{4,2,3,1,0:T(8,128)(2,1)}) %all-gather.5.cloned.1.call-update) | async-done | bytes 8388624 | tf_op jit(solution)/shard_map/all_gather | solution.py:33
  261.0 11.3 %fusion.4 = (f32[16,8,128,128]{3,2,1,0:T(8,128)}, f32[16,8,128,128]{3,2,1,0:T(8,128)}) fusion(bf16[16,8,128,2,128]{4,2,3,1,0:T(8,128)(2,1)} %all-gather.5.cloned.1.call-done), kind=kLoop, calls=%fused_computation.13 | loop fusion | flops 4194304 | bytes 25165824 | tf_op jit(solution)/shard_map/convert_element_type | solution.py:107
  272.3 10.1 %add_reduce_fusion = (f32[2,16,8,128]{3,2,1,0:T(8,128)S(1)}, f32[2,16,8,128]{3,2,1,0:T(8,128)S(1)}) fusion(f32[16,8,128,128]{3,2,1,0:T(8,128)} %get-tuple-element.8, f32[2,8,128,128]{3,2,1,0:T(8,128)S(1)} %copy.100, f32[16,8,128,128]{3,2,1,0:T(8,128)} %get-tuple-element.7, f32[2,8,128,128]{3,2,1,0:T(8,128)S(1)} %copy.98), kind=kLoop, calls=%fused_computation.3 | loop fusion | flops 33488896 | bytes 19136512 | tf_op jit(solution)/shard_map/reduce_sum | solution.py:109
  283.1 0.8 bitcast_select_fusion
  283.9 10.3 %all-to-all-start.1 = ((f32[32,8,2,128]{3,1,2,0:T(8,128)}), f32[32,8,2,128]{3,1,2,0:T(8,128)S(1)}, u32[]{:S(2)}, u32[]{:S(2)}) async-start(f32[32,8,2,128]{3,1,2,0:T(8,128)} %bitcast_select_fusion), calls=%async_computation.1 | async-start | bytes 524288 | tf_op jit(solution)/shard_map/all_to_all | solution.py:147
  294.4 12.8 %all-to-all-done.1 = f32[32,8,2,128]{3,1,2,0:T(8,128)S(1)} async-done(((f32[32,8,2,128]{3,1,2,0:T(8,128)}), f32[32,8,2,128]{3,1,2,0:T(8,128)S(1)}, u32[]{:S(2)}, u32[]{:S(2)}) %all-to-all-start.1) | async-done | bytes 262176 | tf_op jit(solution)/shard_map/all_to_all | solution.py:147
  307.5 17.4 %fusion.12 = f32[8,256]{1,0:T(8,128)S(1)} fusion(s32[256]{0:T(256)S(1)} %fusion.67, f32[1,8,1,4096]{3,0,2,1:T(1,128)S(1)} %get-tuple-element.15), kind=kOutput, calls=%fused_computation.20 | convolution fusion | flops 115343360 | bytes 140288 | tf_op jit(solution)/shard_map/dot_general | solution.py:85
  324.8 17.1 %fusion.10 = f32[8,256]{1,0:T(8,128)S(1)} fusion(s32[256]{0:T(256)S(1)} %fusion.67, f32[1,8,1,4096]{3,0,2,1:T(1,128)S(1)} %get-tuple-element.16), kind=kOutput, calls=%fused_computation.19 | convolution fusion | flops 115343360 | bytes 140288 | tf_op jit(solution)/shard_map/dot_general | solution.py:86
  342.0 17.7 %fusion.24 = f32[8,256]{1,0:T(8,128)S(1)} fusion(f32[8,256]{1,0:T(8,128)S(1)} %fusion.12, s32[256]{0:T(256)S(1)} %fusion.67, f32[1,8,1,4096]{3,0,2,1:T(1,128)S(1)} %get-tuple-element.16), kind=kOutput, calls=%fused_computation.34 | convolution fusion | flops 115345408 | bytes 148480 | tf_op jit(solution)/shard_map/dot_general | solution.py:85
  359.9 17.3 %fusion.27 = f32[8,256]{1,0:T(8,128)S(1)} fusion(f32[8,256]{1,0:T(8,128)S(1)} %fusion.10, s32[256]{0:T(256)S(1)} %fusion.67, f32[1,8,1,4096]{3,0,2,1:T(1,128)S(1)} %get-tuple-element.15), kind=kOutput, calls=%fused_computation.35 | convolution fusion | flops 115345408 | bytes 148480 | tf_op jit(solution)/shard_map/dot_general | solution.py:86
  (64 shorter events, 8.5 us)
Async XLA Ops:
  6.5 4.7 %copy-start = (f32[64,3]{0,1:T(4,128)S(1)}, f32[64,3]{0,1:T(4,128)}, u32[]{:S(2)}) copy-start(f32[64,3]{0,1:T(4,128)} %param.8) | copy-start | bytes 2308
  6.5 1.4 copy-start.2
  6.5 4.7 %copy-start.4 = (s32[2,8,4]{1,2,0:T(4,128)S(1)}, s32[2,8,4]{1,2,0:T(4,128)}, u32[]{:S(2)}) copy-start(s32[2,8,4]{1,2,0:T(4,128)} %param.7) | copy-start | bytes 772
  6.5 166.5 %all-gather.3.cloned.1.call-start = ((), (), s32[]{:S(2)}) async-start(), calls=%async_computation.4 | async-start | bytes 3145728 | tf_op jit(solution)/shard_map/all_gather | solution.py:33
  135.9 37.2 %copy-start.3 = (s32[2,8,4,32]{3,2,1,0:T(4,128)S(1)}, s32[2,8,4,32]{3,2,1,0:T(4,128)}, u32[]{:S(2)}) copy-start(s32[2,8,4,32]{3,2,1,0:T(4,128)} %param.6) | copy-start | bytes 24580
  135.9 42.0 %copy-start.5 = (s32[16]{0:T(128)S(1)}, s32[16]{0:T(128)}, u32[]{:S(2)}) copy-start(s32[16]{0:T(128)} %param.9) | copy-start | bytes 196
  137.1 123.8 %all-gather.5.cloned.1.call-start = ((), (), s32[]{:S(2)}) async-start(), calls=%async_computation.5 | async-start | bytes 10485760 | tf_op jit(solution)/shard_map/all_gather | solution.py:33
  173.9 9.2 %all-to-all-start.2 = ((s32[8,1,2048]{2,1,0:T(1,128)}), s32[8,1,2048]{2,1,0:T(1,128)S(1)}, u32[]{:S(2)}, u32[]{:S(2)}) async-start(s32[8,1,2048]{2,1,0:T(1,128)} %reshape.226), calls=%async_computation.2 | async-start | bytes 131072 | tf_op jit(solution)/shard_map/all_to_all | solution.py:16
  188.3 95.6 %all-to-all-start.3 = ((bf16[32,2,128]{2,1,0:T(2,128)(2,1)}), bf16[32,2,128]{2,1,0:T(2,128)(2,1)S(1)}, u32[]{:S(2)}, u32[]{:S(2)}) async-start(bf16[32,2,128]{2,1,0:T(2,128)(2,1)} %reshape.228), calls=%async_computation.3 | async-start | bytes 32768 | tf_op jit(solution)/shard_map/all_to_all | solution.py:45
  283.9 23.4 %all-to-all-start.1 = ((f32[32,8,2,128]{3,1,2,0:T(8,128)}), f32[32,8,2,128]{3,1,2,0:T(8,128)S(1)}, u32[]{:S(2)}, u32[]{:S(2)}) async-start(f32[32,8,2,128]{3,1,2,0:T(8,128)} %bitcast_select_fusion), calls=%async_computation.1 | async-start | bytes 524288 | tf_op jit(solution)/shard_map/all_to_all | solution.py:147
  359.9 18.5 %copy-start.1 = (f32[64,3]{0,1:T(4,128)S(1)}, f32[64,3]{0,1:T(4,128)}, u32[]{:S(2)}) copy-start(f32[64,3]{0,1:T(4,128)} %param.8) | copy-start | bytes 2308
Sparse Core Ops, SparseCore 0:
  137.3 35.7 all-gather.2
  174.9 86.0 all-gather.4
where the time goes:
time: 393 us; the launch traced here: 385 us
  waiting for transfers between devices  102 us (26%)
  local copies, waits for them, and re-layouts  86.6 us (22%)
  matrix products  72.5 us (18%)
  blocking collectives  40.2 us (10%)
  starting transfers between devices  37.6 us (10%)
  other arithmetic  32.1 us (8%)
  between operations  13.9 us (4%)
    all_gather x2, waiting for transfers between devices, whole_of(): result = lax.all_gather(result, axes[number], axis=dim, tiled=True)  84.7 us
    unnamed x20, local copies, waits for them, and re-layouts  42.3 us
    all_to_all x1, blocking collectives, per_device(): lax.all_to_all(rotated, 'tm', split_axis=4, concat_axis=2, tiled=True)  40.2 us
    all_to_all x1, starting transfers between devices, summed_on_arrival(): lax.all_to_all(pieces, axis, split_axis=0, concat_axis=0, tiled=True)  23.2 us
    all_to_all x2, local copies, waits for them, and re-layouts, per_device(): lax.all_to_all(rotated, 'tm', split_axis=4, concat_axis=2, tiled=True)  20.5 us
    dot_general x1, matrix products, transform(): jnp.dot(imag, sine, precision=highest)  17.7 us
    dot_general x1, matrix products, transform(): jnp.dot(real, cosine, precision=highest)  17.4 us
    dot_general x1, matrix products, transform(): jnp.dot(real, sine, precision=highest)  17.3 us
  transfers between devices with their start and end apart: 5, of which 4 were waited for; matrix products, arithmetic and copies ran while one was open for 8% of the time, Pallas kernels for 0%

commit v1 on v0

v1 whole, which is shorter than its diff:
```python
import math

import jax
import jax.numpy as jnp
import numpy as np
from jax import lax
from jax.experimental import pallas as pl
from jax.experimental.pallas import tpu as pltpu
from jax.sharding import PartitionSpec as P

S = 16
C = 4096
PERIODS = 8
LAGS = 256
SPP = 128
CB = 32
STN = 8
TM = 32
K = 4
ROWS = 24
LANES = 128
HALF = LAGS // 2
HIGHEST = lax.Precision.HIGHEST


def rows_of(shape):
    return lax.broadcasted_iota(jnp.int32, shape, len(shape) - 2)


def lanes_of(shape):
    return lax.broadcasted_iota(jnp.int32, shape, len(shape) - 1)


def rotate_kernel(first_ref, poly_ref, model_ref, flags_ref, x_ref, out_ref):
    p = pl.program_id(0)
    row = rows_of((8, LANES))
    even = row % 2 == 0
    which = row // 2
    lane = lanes_of((8, LANES)).astype(jnp.float32)
    sign = jnp.where(even, 1.0, -1.0)
    for s in range(2):
        delay = jnp.zeros((8, LANES), jnp.float32)
        weight = jnp.zeros((8, CB), jnp.float32)
        for k in range(K):
            index = poly_ref[s, p, k]
            time = p * SPP + first_ref[0] + k
            moment = time.astype(jnp.float32) * (1.0 / (PERIODS * SPP))
            value = (
                model_ref[index, 0]
                + model_ref[index, 1] * moment
                + model_ref[index, 2] * moment * moment
            )
            delay = jnp.where(which == k, value, delay)
            flag = flags_ref[s, 0, k : k + 1, :].astype(jnp.float32)
            weight = jnp.where(
                which[:, :CB] == k, jnp.broadcast_to(1.0 - flag, (8, CB)), weight
            )
        fine = delay * (lane * (math.pi / C))
        fine_cos = jnp.cos(fine)
        fine_sin = jnp.sin(fine)
        signed_cos = sign * fine_cos
        signed_sin = sign * fine_sin
        coarse = delay[:, :CB] * (lane[:, :CB] * (math.pi * LANES / C))
        coarse_cos = weight * jnp.cos(coarse)
        coarse_sin = weight * jnp.sin(coarse)
        for q in range(CB):
            x = x_ref[s, 0, :, q * LANES : (q + 1) * LANES].astype(jnp.float32)
            a_cos = jnp.broadcast_to(coarse_cos[:, q : q + 1], (8, LANES))
            a_sin = jnp.broadcast_to(coarse_sin[:, q : q + 1], (8, LANES))
            cosine = a_cos * fine_cos - a_sin * fine_sin
            sine = a_sin * signed_cos + a_cos * signed_sin
            other = jnp.where(even, pltpu.roll(x, 7, 0), pltpu.roll(x, 1, 0))
            turned = x * cosine + other * sine
            out_ref[q, s * 8 : s * 8 + 8, :] = turned.astype(jnp.bfloat16)
    for q in range(CB):
        tile = jnp.zeros((8, LANES), jnp.float32)
        for s in range(2):
            for k in range(K):
                flag = flags_ref[s, 0, k : k + 1, q : q + 1].astype(jnp.float32)
                tile = jnp.where(
                    row == s * K + k, jnp.broadcast_to(1.0 - flag, (8, LANES)), tile
                )
        out_ref[q, 16:24, :] = tile.astype(jnp.bfloat16)


def rotated_chunks(spectra, flags, poly_index, delay_model, first):
    tiles = spectra.reshape(2, PERIODS, 2 * K, C)
    return pl.pallas_call(
        rotate_kernel,
        grid=(PERIODS,),
        in_specs=[
            pl.BlockSpec(memory_space=pltpu.SMEM),
            pl.BlockSpec(memory_space=pltpu.SMEM),
            pl.BlockSpec(memory_space=pltpu.SMEM),
            pl.BlockSpec((2, 1, K, CB), lambda p: (0, p, 0, 0)),
            pl.BlockSpec((2, 1, 2 * K, C), lambda p: (0, p, 0, 0)),
        ],
        out_specs=pl.BlockSpec((CB, ROWS, LANES), lambda p: (p, 0, 0)),
        out_shape=jax.ShapeDtypeStruct((PERIODS * CB, ROWS, LANES), jnp.bfloat16),
        name="rotate",
    )(first, poly_index, delay_model, flags, tiles)


def row_sums(values):
    row = rows_of((8, LANES))
    upper = row < 4
    stage = [
        jnp.where(upper, values[i], values[i + 4])
        + pltpu.roll(jnp.where(upper, values[i + 4], values[i]), 4, 0)
        for i in range(4)
    ]
    for distance in (2, 1):
        first = row % (2 * distance) < distance
        stage = [
            jnp.where(first, stage[i], stage[i + distance])
            + jnp.where(
                first,
                pltpu.roll(stage[i], 8 - distance, 0),
                pltpu.roll(stage[i + distance], distance, 0),
            )
            for i in range(distance)
        ]
    return stage[0]


def correlate_kernel(order_ref, y_ref, out_ref, wide, turned, weights, scales, held):
    row = rows_of((8, LANES))
    even = row % 2 == 0
    lane = lanes_of((8, LANES))

    def unpack(t, carry):
        total = jnp.zeros((8, LANES), jnp.float32)
        for n in range(STN):
            for s in range(2):
                x = y_ref[n, t, s * 8 : s * 8 + 8, :].astype(jnp.float32)
                wide[2 * n + s, t] = x
                turned[2 * n + s, t] = jnp.where(
                    even, -pltpu.roll(x, 7, 0), pltpu.roll(x, 1, 0)
                )
            w = y_ref[n, t, 16:24, :].astype(jnp.float32)
            total = jnp.where(lane // 8 == 2 * n, w, total)
            total = jnp.where(lane // 8 == 2 * n + 1, pltpu.roll(w, 4, 0), total)
        weights[pl.ds(pl.multiple_of(t * 8, 8), 8), :] = jnp.where(row < K, total, 0.0)
        return carry

    lax.fori_loop(0, TM, unpack, 0)
    counts = lax.dot_general(
        weights[...].astype(jnp.bfloat16),
        weights[...].astype(jnp.bfloat16),
        (((0,), (0,)), ((), ())),
        preferred_element_type=jnp.float32,
    )
    scales[...] = 1.0 / jnp.sqrt(jnp.maximum(counts, 1.0))

    def place(b, block, tile):
        rows = jnp.concatenate(
            [scales[8 * (4 * block + i) : 8 * (4 * block + i) + 2, :] for i in range(4)]
        )
        held[b, block] = tile * jnp.broadcast_to(rows[:, 8 * b : 8 * b + 1], (8, LANES))

    for block_a in range(4):
        for block_b in range(block_a, 4):
            pairs = [
                (i, j)
                for i in range(4)
                for j in range(4)
                if block_a != block_b or i <= j
            ]

            def add(t, sums, block_a=block_a, block_b=block_b, pairs=pairs):
                mine = [wide[4 * block_a + i, t] for i in range(4)]
                theirs = [wide[4 * block_b + j, t] for j in range(4)]
                crossed = [turned[4 * block_b + j, t] for j in range(4)]
                return tuple(
                    (re + mine[i] * theirs[j], im + mine[i] * crossed[j])
                    for (re, im), (i, j) in zip(sums, pairs)
                )

            zero = jnp.zeros((8, LANES), jnp.float32)
            sums = lax.fori_loop(0, TM, add, tuple((zero, zero) for _ in pairs))
            vis = dict(zip(pairs, sums))
            if block_a == block_b:
                for i in range(4):
                    vis[i, i] = (vis[i, i][0], zero)
                    for j in range(i):
                        vis[i, j] = (vis[j, i][0], -vis[j, i][1])
            for j in range(4):
                place(
                    4 * block_b + j,
                    block_a,
                    row_sums([vis[i, j][part] for i in range(4) for part in range(2)]),
                )
            if block_a != block_b:
                for i in range(4):
                    place(
                        4 * block_a + i,
                        block_b,
                        row_sums(
                            [
                                vis[i, j][part] if part == 0 else -vis[i, j][part]
                                for j in range(4)
                                for part in range(2)
                            ]
                        ),
                    )
    for j in range(S):
        b = order_ref[j]
        for block in range(4):
            tile = held[b, block]
            for i in range(4):
                out_ref[(4 * block + i) * S + j] = tile[2 * i : 2 * i + 2, :]


def correlated(order, arrived):
    return pl.pallas_call(
        correlate_kernel,
        in_specs=[
            pl.BlockSpec(memory_space=pltpu.SMEM),
            pl.BlockSpec(memory_space=pltpu.VMEM),
        ],
        out_specs=pl.BlockSpec(memory_space=pltpu.VMEM),
        out_shape=jax.ShapeDtypeStruct((S * S, 2, LANES), jnp.float32),
        scratch_shapes=[
            pltpu.VMEM((S, TM, 8, LANES), jnp.float32),
            pltpu.VMEM((S, TM, 8, LANES), jnp.float32),
            pltpu.VMEM((TM * 8, LANES), jnp.float32),
            pltpu.VMEM((LANES, LANES), jnp.float32),
            pltpu.VMEM((S, 4, 8, LANES), jnp.float32),
        ],
        compiler_params=pltpu.CompilerParams(vmem_limit_bytes=32 * 2**20),
        name="correlate",
    )(order, arrived.reshape(STN, TM, ROWS, LANES))


def fringe_tables():
    lag = np.arange(1, HALF + 1)
    fine = 2.0 * np.pi * ((np.arange(LANES)[:, None] * lag) % C) / C
    coarse = 2.0 * np.pi * ((np.arange(CB)[:, None] * lag) % CB) / CB
    period = 2.0 * np.pi * ((np.arange(PERIODS)[:, None] * np.arange(PERIODS)) % PERIODS)
    period = period / PERIODS
    factor = 1.0 / math.sqrt(PERIODS * C)
    flip = np.eye(HALF)[::-1]
    return [
        np.ascontiguousarray(table, np.float32)
        for table in (
            np.concatenate([np.cos(fine), np.sin(fine)], axis=1),
            np.stack([np.cos(coarse), np.sin(coarse)]),
            np.stack([np.cos(period), np.sin(period)]) * factor,
            flip,
        )
    ]


def fringe_kernel(z_ref, fine_ref, coarse_ref, period_ref, flip_ref, out_ref):
    fine = fine_ref[...]
    re = jnp.dot(z_ref[0], fine, precision=HIGHEST, preferred_element_type=jnp.float32)
    im = jnp.dot(z_ref[1], fine, precision=HIGHEST, preferred_element_type=jnp.float32)
    parts = [[], [], [], []]
    for p in range(PERIODS):
        sums = [jnp.zeros((8, LANES), jnp.float32)] * 4
        for g in range(CB // 8):
            at = slice(p * CB + g * 8, p * CB + g * 8 + 8)
            re_cos, re_sin = re[at, :HALF], re[at, HALF:]
            im_cos, im_sin = im[at, :HALF], im[at, HALF:]
            cosine = coarse_ref[0, g * 8 : g * 8 + 8, :]
            sine = coarse_ref[1, g * 8 : g * 8 + 8, :]
            plus_re, plus_im = re_cos + im_sin, im_cos - re_sin
            minus_re, minus_im = re_cos - im_sin, im_cos + re_sin
            terms = (
                cosine * minus_re - sine * minus_im,
                cosine * minus_im + sine * minus_re,
                cosine * plus_re + sine * plus_im,
                cosine * plus_im - sine * plus_re,
            )
            sums = [total + term for total, term in zip(sums, terms)]
        for part, total in zip(parts, sums):
            part.append(total)
    minus_re, minus_im, plus_re, plus_im = (row_sums(part) for part in parts)
    reversed_ = jnp.dot(
        jnp.concatenate([minus_re, minus_im]),
        flip_ref[...],
        precision=HIGHEST,
        preferred_element_type=jnp.float32,
    )
    real = jnp.concatenate([reversed_[:8], plus_re], axis=1)
    imag = jnp.concatenate([reversed_[8:], plus_im], axis=1)
    cosine, sine = period_ref[0], period_ref[1]

    def turn(a, b):
        return jnp.dot(a, b, precision=HIGHEST, preferred_element_type=jnp.float32)

    out_ref[0, 0] = turn(cosine, real) + turn(sine, imag)
    out_ref[1, 0] = turn(cosine, imag) - turn(sine, real)


def fringed(normed):
    return pl.pallas_call(
        fringe_kernel,
        in_specs=[pl.BlockSpec(memory_space=pltpu.VMEM)] * 5,
        out_specs=pl.BlockSpec(memory_space=pltpu.VMEM),
        out_shape=jax.ShapeDtypeStruct((2, 1, PERIODS, LAGS), jnp.float32),
        compiler_params=pltpu.CompilerParams(vmem_limit_bytes=32 * 2**20),
        name="fringe",
    )(normed, *fringe_tables())


def per_device(spectra, flags, poly_index, delay_model, partner_order):
    axes = ("stn", "tm")
    first = (lax.axis_index("tm") * K).astype(jnp.int32).reshape(1)
    chunks = rotated_chunks(spectra, flags, poly_index, delay_model, first)
    arrived = lax.all_to_all(chunks, axes, split_axis=0, concat_axis=0, tiled=True)
    rows = correlated(partner_order, arrived)
    owned = lax.all_to_all(rows, axes, split_axis=0, concat_axis=0, tiled=True)
    return fringed(jnp.moveaxis(owned, 1, 0))


def solution(mesh):
    return jax.shard_map(
        per_device,
        mesh=mesh,
        in_specs=(
            P("stn", None, "tm", None, None),
            P("stn", None, "tm", None),
            P("stn", None, "tm"),
            P(),
            P(),
        ),
        out_specs=P(None, ("stn", "tm"), None, None),
        check_vma=False,
    )
```

time: 393 us -> 104 us (0.26); the launches traced: 385 us -> 103 us
  waiting for transfers between devices: 102 us -> 0 us
  local copies, waits for them, and re-layouts: 86.6 us -> 5.02 us
  matrix products: 72.5 us -> 0 us
  blocking collectives: 40.2 us -> 79.6 us
  starting transfers between devices: 37.6 us -> 0 us
  other arithmetic: 32.1 us -> 0 us
  Pallas kernels: 0 us -> 18.5 us
  between operations: 13.9 us -> 0.06 us
    all_gather x2 -> x0, waiting for transfers between devices: 84.7 us -> none  [whole_of(): result = lax.all_gather(result, axes[number], axis=dim, tiled=True)]
    dot_general x10 -> x0, matrix products: 72.5 us -> none  [the longest x1 17.7 us: transform(): jnp.dot(imag, sine, precision=highest)]
    unnamed x20 -> x12, local copies, waits for them, and re-layouts: 42.3 us -> 2.76 us
    all_to_all x1 -> x2, blocking collectives: 40.2 us -> 79.6 us  [the longest x1 57 us: per_device(): lax.all_to_all(chunks, axes, split_axis=0, concat_axis=0, tiled=True)]
    all_to_all x3 -> x0, starting transfers between devices: 37.5 us -> none  [the longest x1 23.2 us: summed_on_arrival(): lax.all_to_all(pieces, axis, split_axis=0, concat_axis=0, tiled=True)]
    all_to_all x3 -> x1, local copies, waits for them, and re-layouts: 21 us -> 0.02 us  [per_device(): owned = lax.all_to_all(rows, axes, split_axis=0, concat_axis=0, tiled=True)]
    pallas_call x0 -> x3, Pallas kernels: none -> 18.5 us  [the longest x1 8.85 us: rotated_chunks(): pl.pallas_call(rotate_kernel, grid=(PERIODS,), in_specs=[pl.BlockSpec(mem...]
    all_to_all x3 -> x0, waiting for transfers between devices: 17.7 us -> none  [the longest x1 12.8 us: per_device(): lax.all_to_all(vis_rows, 'tm', split_axis=0, concat_axis=3, tiled=True)]
  transfers between devices with their start and end apart: 5 -> 0, of which waited for: 4 -> 0; matrix products, arithmetic and copies ran while one was open for 8% -> 0% of each run, Pallas kernels for 0% -> 0%
where the time goes in v1:
time: 104 us; the launch traced here: 103 us
  blocking collectives  79.6 us (77%)
  Pallas kernels  18.5 us (18%)
  local copies, waits for them, and re-layouts  5.02 us (5%)
    all_to_all x1, blocking collectives, per_device(): lax.all_to_all(chunks, axes, split_axis=0, concat_axis=0, tiled=True)  57 us
    all_to_all x1, blocking collectives, per_device(): owned = lax.all_to_all(rows, axes, split_axis=0, concat_axis=0, tiled=True)  22.6 us
    pallas_call x1, Pallas kernels, rotated_chunks(): pl.pallas_call(rotate_kernel, grid=(PERIODS,), in_specs=[pl.BlockSpec(mem...  8.85 us
    pallas_call x1, Pallas kernels, correlated(): pl.pallas_call(correlate_kernel, in_specs=[pl.BlockSpec(memory_space=pltp...  8.01 us
    unnamed x12, local copies, waits for them, and re-layouts  2.76 us
    reshape x1, local copies, waits for them, and re-layouts, rotated_chunks(): tiles = spectra.reshape(2, PERIODS, 2 * K, C)  2.24 us

profile of v1, /device:TPU:1, one launch (start us, length us, event | category | flops | bytes accessed | tf_op | source)
XLA Modules:
  0.0 103.2 jit_solution(1911571569790440179)
XLA Ops:
  0.0 1.4 %copy.13.poly_ref = s32[2,8,4]{2,1,0:T(8,128)} copy(s32[2,8,4]{1,2,0:T(4,128)} %param.11) | data formatting | bytes 512 | tf_op args[2]
  1.4 1.4 %copy.14.model_ref = f32[64,3]{1,0:T(8,128)} copy(f32[64,3]{0,1:T(4,128)} %param.12) | data formatting | bytes 1536 | tf_op args[3]
  2.7 2.2 %reshape.10.x_ref = bf16[2,8,8,4096]{3,2,1,0:T(8,128)(2,1)} reshape(bf16[2,8,4,2,4096]{4,3,2,1,0:T(2,128)(2,1)} %param.9) | data formatting | bytes 2097152 | tf_op jit(solution)/shard_map/reshape | solution.py:87
  5.0 8.8 %rotate.1 = bf16[256,24,128]{2,1,0:T(8,128)(2,1)} custom-call(s32[1]{0:T(128)} %bitcast.first_ref, s32[2,8,4]{2,1,0:T(8,128)} %copy.13.poly_ref, f32[64,3]{1,0:T(8,128)} %copy.14.model_ref, s32[2,8,4,32]{3,2,1,0:T(4,128)} %flags_ref.1, bf16[2,8,8,4096]{3,2,1,0:T(8,128)(2,1)} %reshape.10.x_ref), custom_call_target="tpu_custom_call" | custom-call | tf_op jit(solution)/shard_map/rotate/pallas_call | solution.py:88
  13.8 0.0 copy-start.4
  13.8 57.0 %all_to_all.10 = bf16[256,24,128]{2,1,0:T(8,128)(2,1)S(1)} all-to-all(bf16[256,24,128]{2,1,0:T(8,128)(2,1)} %rotate.1), channel_id=1, replica_groups=mesh['stn'=8,'tm'=32] {'stn','tm'}, dimensions={0} | all-to-all | bytes 3145728 | tf_op jit(solution)/shard_map/all_to_all | solution.py:311
  70.8 0.0 copy-start
  70.8 0.0 copy-start.1
  70.8 0.0 copy-start.2
  70.8 0.0 copy-start.3
  70.8 0.0 copy-done.4
  70.8 8.0 %correlate.1 = f32[256,2,128]{2,1,0:T(2,128)S(1)} custom-call(s32[16]{0:T(128)S(1)} %copy-done.4, bf16[8,32,24,128]{3,2,1,0:T(8,128)(2,1)S(1)} %bitcast.5), custom_call_target="tpu_custom_call" | custom-call | tf_op jit(solution)/shard_map/correlate/pallas_call | solution.py:215
  78.8 22.6 %all_to_all.11 = f32[256,2,128]{2,1,0:T(2,128)S(1)} all-to-all(f32[256,2,128]{2,1,0:T(2,128)S(1)} %correlate.1), channel_id=1, replica_groups=mesh['stn'=8,'tm'=32] {'stn','tm'}, dimensions={0} | all-to-all | bytes 524288 | tf_op jit(solution)/shard_map/all_to_all | solution.py:313
  101.5 0.0 copy-done
  101.5 0.0 copy-done.1
  101.5 0.0 copy-done.2
  101.5 0.0 copy-done.3
  101.5 1.6 %fringe.1 = f32[2,1,8,256]{3,2,1,0:T(8,128)} custom-call(f32[2,256,128]{2,1,0:T(8,128)S(1)} %bitcast.6, f32[128,256]{1,0:T(8,128)S(1)} %copy-done, f32[2,32,128]{2,1,0:T(8,128)S(1)} %copy-done.2, f32[2,8,8]{2,1,0:T(8,128)S(1)} %copy-done.3, f32[128,128]{1,0:T(8,128)S(1)} %copy-done.1), custom_call_target="tpu_custom_call" | custom-call | tf_op jit(solution)/shard_map/fringe/pallas_call | solution.py:297
  (1 shorter events, 0.0 us)
Async XLA Ops:
  13.8 57.0 %copy-start.4 = (s32[16]{0:T(128)S(1)}, s32[16]{0:T(128)}, u32[]{:S(2)}) copy-start(s32[16]{0:T(128)} %order_ref.1) | copy-start | bytes 196
  70.8 30.7 %copy-start = (f32[128,256]{1,0:T(8,128)S(1)}, f32[128,256]{1,0:T(8,128)}, u32[]{:S(2)}) copy-start(f32[128,256]{1,0:T(8,128)} %constant.14.clone.fine_ref) | copy-start | bytes 393220
  70.8 30.7 %copy-start.1 = (f32[128,128]{1,0:T(8,128)S(1)}, f32[128,128]{1,0:T(8,128)}, u32[]{:S(2)}) copy-start(f32[128,128]{1,0:T(8,128)} %constant.17.clone.flip_ref) | copy-start | bytes 196612
  70.8 30.7 %copy-start.2 = (f32[2,32,128]{2,1,0:T(8,128)S(1)}, f32[2,32,128]{2,1,0:T(8,128)}, u32[]{:S(2)}) copy-start(f32[2,32,128]{2,1,0:T(8,128)} %constant.15.clone.coarse_ref) | copy-start | bytes 98308
  70.8 30.7 %copy-start.3 = (f32[2,8,8]{2,1,0:T(8,128)S(1)}, f32[2,8,8]{2,1,0:T(8,128)}, u32[]{:S(2)}) copy-start(f32[2,8,8]{2,1,0:T(8,128)} %constant.16.clone.period_ref) | copy-start | bytes 1540

commit v2 on v1

v2 whole, which is shorter than its diff:
```python
import math

import jax
import jax.numpy as jnp
import numpy as np
from jax import lax
from jax.experimental import pallas as pl
from jax.experimental.pallas import tpu as pltpu
from jax.sharding import PartitionSpec as P

S = 16
C = 4096
PERIODS = 8
LAGS = 256
SPP = 128
CB = 32
STN = 8
TM = 32
K = 4
SPECTRA = 2 * K
LANES = 128
HALF = LAGS // 2
HIGHEST = lax.Precision.HIGHEST


def rows_of(shape):
    return lax.broadcasted_iota(jnp.int32, shape, len(shape) - 2)


def lanes_of(shape):
    return lax.broadcasted_iota(jnp.int32, shape, len(shape) - 1)


def rotate_kernel(first_ref, poly_ref, model_ref, flags_ref, x_hbm, out_ref, x_ref, turned_re, turned_im, sems):
    def fetch(p):
        return pltpu.make_async_copy(x_hbm.at[:, p], x_ref.at[p], sems.at[p])

    for p in range(PERIODS):
        fetch(p).start()
    row = rows_of((8, LANES))
    lane = lanes_of((8, LANES))
    across = jnp.zeros((8, LANES), jnp.float32)
    down = []
    for p in range(PERIODS):
        column = jnp.zeros((8, LANES), jnp.float32)
        for s in range(2):
            for k in range(K):
                index = poly_ref[s, k, p]
                time = p * SPP + first_ref[0] + k
                moment = time.astype(jnp.float32) * (1.0 / (PERIODS * SPP))
                delay = (
                    model_ref[0, index]
                    + model_ref[1, index] * moment
                    + model_ref[2, index] * moment * moment
                )
                column = jnp.where(row == s * K + k, delay, column)
                across = jnp.where(lane == p * SPECTRA + s * K + k, delay, across)
        down.append(column)
    fine = [d * (lane.astype(jnp.float32) * (math.pi / C)) for d in down]
    fine_cos = [jnp.cos(f) for f in fine]
    fine_sin = [jnp.sin(f) for f in fine]
    weight = 1.0 - flags_ref[...].reshape(2 * PERIODS * K, CB).astype(jnp.float32)
    weight = weight.astype(jnp.bfloat16)
    source = rows_of((2 * PERIODS * K, LANES))
    source_s, source_p, source_k = source // (PERIODS * K), source // K % PERIODS, source % K
    target = lanes_of((2 * PERIODS * K, LANES))

    def spread(chosen):
        return lax.dot_general(
            weight,
            chosen.astype(jnp.bfloat16),
            (((0,), (0,)), ((), ())),
            preferred_element_type=jnp.float32,
        )

    spectrum = source_s * K + source_k
    coarse_weight = spread(
        jnp.where(target == source_p * SPECTRA + spectrum, 1.0, 0.0)
    )
    block = rows_of((CB, LANES)).astype(jnp.float32)
    coarse = jnp.tile(across, (CB // 8, 1)) * (block * (math.pi * LANES / C))
    coarse_cos = coarse_weight * jnp.cos(coarse)
    coarse_sin = coarse_weight * jnp.sin(coarse)
    for p in range(PERIODS):
        mark = jnp.where((source_p == p) & (target % SPECTRA == spectrum), 1.0, 0.0)
        sent = spread(mark).astype(jnp.bfloat16)
        fetch(p).wait()
        for s in range(2):
            for k in range(K):
                r = s * K + k
                x = x_ref[p, s, k].astype(jnp.float32)
                re = x[0:1].reshape(CB, LANES)
                im = x[1:2].reshape(CB, LANES)
                at = p * SPECTRA + r
                a_cos = jnp.broadcast_to(coarse_cos[:, at : at + 1], (CB, LANES))
                a_sin = jnp.broadcast_to(coarse_sin[:, at : at + 1], (CB, LANES))
                b_cos = jnp.broadcast_to(fine_cos[p][r : r + 1], (CB, LANES))
                b_sin = jnp.broadcast_to(fine_sin[p][r : r + 1], (CB, LANES))
                cosine = a_cos * b_cos - a_sin * b_sin
                sine = a_sin * b_cos + a_cos * b_sin
                turned_re[p % 2, pl.ds(r, CB, stride=SPECTRA), :] = re * cosine + im * sine
                turned_im[p % 2, pl.ds(r, CB, stride=SPECTRA), :] = im * cosine - re * sine
        for q in range(CB):
            at = slice(q * SPECTRA, (q + 1) * SPECTRA)
            both = jnp.concatenate([turned_re[p % 2, at], turned_im[p % 2, at]])
            out_ref[p * CB + q, 0:SPECTRA] = both.astype(jnp.bfloat16).reshape(SPECTRA, 2, LANES)
        out_ref[p * CB : (p + 1) * CB, SPECTRA] = jnp.broadcast_to(
            sent[:, None, :], (CB, 2, LANES)
        )


def rotated_chunks(spectra, flags, poly_index, delay_model, first):
    return pl.pallas_call(
        rotate_kernel,
        in_specs=[
            pl.BlockSpec(memory_space=pltpu.SMEM),
            pl.BlockSpec(memory_space=pltpu.SMEM),
            pl.BlockSpec(memory_space=pltpu.SMEM),
            pl.BlockSpec(memory_space=pltpu.VMEM),
            pl.BlockSpec(memory_space=pltpu.HBM),
        ],
        out_specs=pl.BlockSpec(memory_space=pltpu.VMEM),
        out_shape=jax.ShapeDtypeStruct((PERIODS * CB, SPECTRA + 1, 2, LANES), jnp.bfloat16),
        scratch_shapes=[
            pltpu.VMEM((PERIODS, 2, K, 2, C), jnp.bfloat16),
            pltpu.VMEM((2, CB * SPECTRA, LANES), jnp.float32),
            pltpu.VMEM((2, CB * SPECTRA, LANES), jnp.float32),
            pltpu.SemaphoreType.DMA((PERIODS,)),
        ],
        compiler_params=pltpu.CompilerParams(vmem_limit_bytes=32 * 2**20),
        name="rotate",
    )(first, poly_index.transpose(0, 2, 1), delay_model.T, flags, spectra)


def group_sums(values, group):
    row = rows_of((8, LANES))
    stage = list(values)
    distance = group // 2
    while distance:
        first = row % (2 * distance) < distance
        if 2 * distance == 8:
            stage = [
                jnp.where(first, stage[i], stage[i + distance])
                + pltpu.roll(jnp.where(first, stage[i + distance], stage[i]), 4, 0)
                for i in range(distance)
            ]
        else:
            stage = [
                jnp.where(first, stage[i], stage[i + distance])
                + jnp.where(
                    first,
                    pltpu.roll(stage[i], 8 - distance, 0),
                    pltpu.roll(stage[i + distance], distance, 0),
                )
                for i in range(distance)
            ]
        distance //= 2
    return stage[0]


def pair_scales(y_ref):
    lane = lanes_of((TM, LANES))
    seen = jnp.zeros((TM, LANES), jnp.float32)
    for n in range(STN):
        seen = jnp.where(
            lane // SPECTRA == n, y_ref[n, :, SPECTRA].astype(jnp.float32)[:, 0, :], seen
        )
    seen = seen.astype(jnp.bfloat16)
    together = lax.dot_general(
        seen, seen, (((0,), (0,)), ((), ())), preferred_element_type=jnp.float32
    )
    i, j = rows_of((LANES, LANES)), lanes_of((LANES, LANES))
    together = jnp.where(i % K == j % K, together, 0.0).astype(jnp.bfloat16)
    partner = jnp.where(i // K == j, 1.0, 0.0).astype(jnp.bfloat16)
    summed = jnp.dot(together, partner, preferred_element_type=jnp.float32)
    a, b = rows_of((STN * 8, LANES)), lanes_of((STN * 8, LANES))
    station = jnp.where(a // 4 == b // K, 1.0, 0.0).astype(jnp.bfloat16)
    counts = jnp.dot(
        station, summed.astype(jnp.bfloat16), preferred_element_type=jnp.float32
    )
    return 1.0 / jnp.sqrt(jnp.maximum(counts, 1.0))


def correlate_kernel(order_ref, y_ref, out_ref, mine_ref, theirs_ref, crossed_ref, scales, place_ref):
    for j in range(S):
        place_ref[order_ref[j]] = j
    row = rows_of((8, LANES))
    scales[...] = pair_scales(y_ref)

    def unpack(t, carry):
        for n in range(STN):
            x = y_ref[n, t, 0:SPECTRA].reshape(2 * SPECTRA, LANES).astype(jnp.float32)
            re, im = x[:SPECTRA], x[SPECTRA:]
            total, gap = re + im, im - re
            for part, value in enumerate((re, im, total)):
                mine_ref[n, part, t] = value
            for part, value in enumerate((total, gap)):
                theirs_ref[n, part, t] = value
            for part, value in enumerate((re, total, gap)):
                crossed_ref[n, part, t] = pltpu.roll(value, 4, 0)
        return carry

    lax.fori_loop(0, TM, unpack, 0)
    conjugate = jnp.where(row % 2 == 0, 1.0, -1.0)
    zero = jnp.zeros((8, LANES), jnp.float32)

    def finish(n, m, sums):
        values = []
        for number, (first, second, third) in enumerate((sums[:3], sums[3:])):
            real = first + third
            imag = zero if n == m and number == 0 else first - second
            values += [real, imag]
        tile = group_sums(values, 4)
        scale = scales[n * 8 : n * 8 + 8, :]
        even = jnp.broadcast_to(scale[:, 2 * m : 2 * m + 1], (8, LANES))
        odd = jnp.broadcast_to(scale[:, 2 * m + 1 : 2 * m + 2], (8, LANES))
        tile = tile * jnp.where((row < 2) | (row >= 6), even, odd)
        other = tile * conjugate
        for pair in range(4):
            h = pair // 2
            a = 2 * n + h
            b = 2 * m + (h if pair % 2 == 0 else 1 - h)
            at = slice(2 * pair, 2 * pair + 2)
            out_ref[a * S + place_ref[b]] = tile[at]
            if n != m:
                out_ref[b * S + place_ref[a]] = other[at]

    for block_n in range(0, STN, 2):
        for block_m in range(block_n, STN, 2):
            pairs = [
                (n, m)
                for n in range(block_n, block_n + 2)
                for m in range(block_m, block_m + 2)
                if n <= m
            ]

            def add(t, sums, pairs=pairs, block_n=block_n, block_m=block_m):
                mine = {
                    n: [mine_ref[n, part, t] for part in range(3)]
                    for n in range(block_n, block_n + 2)
                }
                theirs = {
                    m: [
                        mine_ref[m, 0, t],
                        theirs_ref[m, 0, t],
                        theirs_ref[m, 1, t],
                        *(crossed_ref[m, part, t] for part in range(3)),
                    ]
                    for m in range(block_m, block_m + 2)
                }
                result = []
                for (n, m), total in zip(pairs, sums):
                    re, im, both = mine[n]
                    factors = (both, re, im, both, re, im)
                    result.append(
                        tuple(
                            t0 + f * o for t0, f, o in zip(total, factors, theirs[m])
                        )
                    )
                return tuple(result)

            sums = lax.fori_loop(
                0, TM, add, tuple((zero,) * 6 for _ in pairs), unroll=4
            )
            for (n, m), total in zip(pairs, sums):
                finish(n, m, total)


def correlated(order, arrived):
    return pl.pallas_call(
        correlate_kernel,
        in_specs=[
            pl.BlockSpec(memory_space=pltpu.SMEM),
            pl.BlockSpec(memory_space=pltpu.VMEM),
        ],
        out_specs=pl.BlockSpec(memory_space=pltpu.VMEM),
        out_shape=jax.ShapeDtypeStruct((S * S, 2, LANES), jnp.float32),
        scratch_shapes=[
            pltpu.VMEM((STN, 3, TM, 8, LANES), jnp.float32),
            pltpu.VMEM((STN, 2, TM, 8, LANES), jnp.float32),
            pltpu.VMEM((STN, 3, TM, 8, LANES), jnp.float32),
            pltpu.VMEM((STN * 8, LANES), jnp.float32),
            pltpu.SMEM((S,), jnp.int32),
        ],
        compiler_params=pltpu.CompilerParams(vmem_limit_bytes=48 * 2**20),
        name="correlate",
    )(order, arrived.reshape(STN, TM, SPECTRA + 1, 2, LANES))


def fringe_tables():
    lag = np.arange(1, HALF + 1)
    fine = 2.0 * np.pi * ((np.arange(LANES)[:, None] * lag) % C) / C
    coarse = 2.0 * np.pi * ((np.arange(CB)[:, None] * lag) % CB) / CB
    period = 2.0 * np.pi * ((np.arange(PERIODS)[:, None] * np.arange(PERIODS)) % PERIODS)
    period = period / PERIODS
    factor = 1.0 / math.sqrt(PERIODS * C)
    flip = np.eye(HALF)[::-1]
    return [
        np.ascontiguousarray(table, np.float32)
        for table in (
            np.concatenate([np.cos(fine), np.sin(fine)], axis=1),
            np.stack([np.cos(coarse), np.sin(coarse)]),
            np.stack([np.cos(period), np.sin(period)]) * factor,
            flip,
        )
    ]


def fringe_kernel(z_ref, fine_ref, coarse_ref, period_ref, flip_ref, out_ref):
    fine = fine_ref[...]
    re = jnp.dot(z_ref[0], fine, precision=HIGHEST, preferred_element_type=jnp.float32)
    im = jnp.dot(z_ref[1], fine, precision=HIGHEST, preferred_element_type=jnp.float32)
    parts = [[], [], [], []]
    for p in range(PERIODS):
        sums = [jnp.zeros((8, LANES), jnp.float32)] * 4
        for g in range(CB // 8):
            at = slice(p * CB + g * 8, p * CB + g * 8 + 8)
            re_cos, re_sin = re[at, :HALF], re[at, HALF:]
            im_cos, im_sin = im[at, :HALF], im[at, HALF:]
            cosine = coarse_ref[0, g * 8 : g * 8 + 8, :]
            sine = coarse_ref[1, g * 8 : g * 8 + 8, :]
            plus_re, plus_im = re_cos + im_sin, im_cos - re_sin
            minus_re, minus_im = re_cos - im_sin, im_cos + re_sin
            terms = (
                cosine * minus_re - sine * minus_im,
                cosine * minus_im + sine * minus_re,
                cosine * plus_re + sine * plus_im,
                cosine * plus_im - sine * plus_re,
            )
            sums = [total + term for total, term in zip(sums, terms)]
        for part, total in zip(parts, sums):
            part.append(total)
    minus_re, minus_im, plus_re, plus_im = (group_sums(part, 8) for part in parts)
    reversed_ = jnp.dot(
        jnp.concatenate([minus_re, minus_im]),
        flip_ref[...],
        precision=HIGHEST,
        preferred_element_type=jnp.float32,
    )
    real = jnp.concatenate([reversed_[:8], plus_re], axis=1)
    imag = jnp.concatenate([reversed_[8:], plus_im], axis=1)
    cosine, sine = period_ref[0], period_ref[1]

    def turn(a, b):
        return jnp.dot(a, b, precision=HIGHEST, preferred_element_type=jnp.float32)

    out_ref[0, 0] = turn(cosine, real) + turn(sine, imag)
    out_ref[1, 0] = turn(cosine, imag) - turn(sine, real)


def fringed(normed):
    return pl.pallas_call(
        fringe_kernel,
        in_specs=[pl.BlockSpec(memory_space=pltpu.VMEM)] * 5,
        out_specs=pl.BlockSpec(memory_space=pltpu.VMEM),
        out_shape=jax.ShapeDtypeStruct((2, 1, PERIODS, LAGS), jnp.float32),
        compiler_params=pltpu.CompilerParams(vmem_limit_bytes=32 * 2**20),
        name="fringe",
    )(normed, *fringe_tables())


def per_device(spectra, flags, poly_index, delay_model, partner_order):
    axes = ("stn", "tm")
    first = (lax.axis_index("tm") * K).astype(jnp.int32).reshape(1)
    chunks = rotated_chunks(spectra, flags, poly_index, delay_model, first)
    arrived = lax.all_to_all(chunks, axes, split_axis=0, concat_axis=0, tiled=True)
    rows = correlated(partner_order, arrived)
    owned = lax.all_to_all(rows, axes, split_axis=0, concat_axis=0, tiled=True)
    return fringed(jnp.moveaxis(owned, 1, 0))


def solution(mesh):
    return jax.shard_map(
        per_device,
        mesh=mesh,
        in_specs=(
            P("stn", None, "tm", None, None),
            P("stn", None, "tm", None),
            P("stn", None, "tm"),
            P(),
            P(),
        ),
        out_specs=P(None, ("stn", "tm"), None, None),
        check_vma=False,
    )
```

time: 104 us -> 86.4 us (0.83)
  blocking collectives: 79.6 us -> 71 us
  Pallas kernels: 18.5 us -> 11.6 us
  local copies, waits for them, and re-layouts: 5.02 us -> 3.39 us
    all_to_all x1, blocking collectives: 57 us -> 48.7 us  [per_device(): lax.all_to_all(chunks, axes, split_axis=0, concat_axis=0, tiled=True)]
    pallas_call x1, Pallas kernels: 8.85 us -> 3.87 us  [rotated_chunks(): pl.pallas_call(rotate_kernel, in_specs=[pl.BlockSpec(memory_space=pltpu.S...]
    reshape x1 -> x0, local copies, waits for them, and re-layouts: 2.24 us -> none  [rotated_chunks(): tiles = spectra.reshape(2, PERIODS, 2 * K, C)]
    pallas_call x1, Pallas kernels: 8.01 us -> 6.1 us  [correlated(): pl.pallas_call(correlate_kernel, in_specs=[pl.BlockSpec(memory_space=pltp...]
    unnamed x12 -> x18, local copies, waits for them, and re-layouts: 2.76 us -> 3.37 us
where the time goes in v2:
time: 86.4 us; the launch traced here: 86.1 us
  blocking collectives  71 us (82%)
  Pallas kernels  11.6 us (13%)
  local copies, waits for them, and re-layouts  3.39 us (4%)
    all_to_all x1, blocking collectives, per_device(): lax.all_to_all(chunks, axes, split_axis=0, concat_axis=0, tiled=True)  48.7 us
    all_to_all x1, blocking collectives, per_device(): owned = lax.all_to_all(rows, axes, split_axis=0, concat_axis=0, tiled=True)  22.4 us
    pallas_call x1, Pallas kernels, correlated(): pl.pallas_call(correlate_kernel, in_specs=[pl.BlockSpec(memory_space=pltp...  6.1 us
    pallas_call x1, Pallas kernels, rotated_chunks(): pl.pallas_call(rotate_kernel, in_specs=[pl.BlockSpec(memory_space=pltpu.S...  3.87 us
    unnamed x18, local copies, waits for them, and re-layouts  3.37 us

profile of v2, /device:TPU:1, one launch (start us, length us, event | category | flops | bytes accessed | tf_op | source)
XLA Modules:
  0.0 86.1 jit_solution(220259915060374617)
XLA Ops:
  0.0 0.0 copy-start
  0.0 1.2 %copy-done = bf16[2,8,4,2,4096]{4,3,2,1,0:T(2,128)(2,1)S(1)} copy-done((bf16[2,8,4,2,4096]{4,3,2,1,0:T(2,128)(2,1)S(1)}, bf16[2,8,4,2,4096]{4,3,2,1,0:T(2,128)(2,1)}, u32[]{:S(2)}) %copy-start) | copy-done | bytes 1048600
  1.2 0.0 copy-start.3
  1.2 0.8 copy-done.3
  2.0 0.0 copy-start.6
  2.0 0.7 copy-done.6
  2.7 0.0 copy-start.7
  2.7 0.7 copy-done.7
  3.4 3.9 %rotate.1 = bf16[256,9,2,128]{3,2,1,0:T(2,128)(2,1)S(1)} custom-call(s32[1]{0:T(128)} %bitcast.first_ref, s32[2,4,8]{2,1,0:T(4,128)S(1)} %bitcast.9, f32[3,64]{1,0:T(4,128)S(1)} %bitcast.10, s32[2,8,4,32]{3,2,1,0:T(4,128)S(1)} %copy-done.3, bf16[2,8,4,2,4096]{4,3,2,1,0:T(2,128)(2,1)S(1)} %copy-done), custom_call_target="tpu_custom_call" | custom-call | tf_op jit(solution)/shard_map/rotate/pallas_call | solution.py:113
  7.2 0.0 copy-start.8
  7.2 48.7 %all_to_all.10 = bf16[256,9,2,128]{3,2,1,0:T(2,128)(2,1)S(1)} all-to-all(bf16[256,9,2,128]{3,2,1,0:T(2,128)(2,1)S(1)} %rotate.1), channel_id=1, replica_groups=mesh['stn'=8,'tm'=32] {'stn','tm'}, dimensions={0} | all-to-all | bytes 2359296 | tf_op jit(solution)/shard_map/all_to_all | solution.py:366
  55.9 0.0 copy-done.8
  55.9 0.0 copy-start.1
  55.9 0.0 copy-start.2
  55.9 0.0 copy-start.4
  55.9 0.0 copy-start.5
  55.9 6.1 %correlate.1 = f32[256,2,128]{2,1,0:T(2,128)S(1)} custom-call(s32[16]{0:T(128)S(1)} %copy-done.8, bf16[8,32,9,2,128]{4,3,2,1,0:T(2,128)(2,1)S(1)} %bitcast.7), custom_call_target="tpu_custom_call" | custom-call | tf_op jit(solution)/shard_map/correlate/pallas_call | solution.py:270
  62.0 22.4 %all_to_all.11 = f32[256,2,128]{2,1,0:T(2,128)S(1)} all-to-all(f32[256,2,128]{2,1,0:T(2,128)S(1)} %correlate.1), channel_id=1, replica_groups=mesh['stn'=8,'tm'=32] {'stn','tm'}, dimensions={0} | all-to-all | bytes 524288 | tf_op jit(solution)/shard_map/all_to_all | solution.py:368
  84.4 0.0 copy-done.1
  84.4 0.0 copy-done.2
  84.5 0.0 copy-done.4
  84.5 0.0 copy-done.5
  84.5 1.6 %fringe.1 = f32[2,1,8,256]{3,2,1,0:T(8,128)} custom-call(f32[2,256,128]{2,1,0:T(8,128)S(1)} %bitcast.8, f32[128,256]{1,0:T(8,128)S(1)} %copy-done.1, f32[2,32,128]{2,1,0:T(8,128)S(1)} %copy-done.4, f32[2,8,8]{2,1,0:T(8,128)S(1)} %copy-done.5, f32[128,128]{1,0:T(8,128)S(1)} %copy-done.2), custom_call_target="tpu_custom_call" | custom-call | tf_op jit(solution)/shard_map/fringe/pallas_call | solution.py:352
  (1 shorter events, 0.0 us)
Async XLA Ops:
  0.0 1.2 %copy-start = (bf16[2,8,4,2,4096]{4,3,2,1,0:T(2,128)(2,1)S(1)}, bf16[2,8,4,2,4096]{4,3,2,1,0:T(2,128)(2,1)}, u32[]{:S(2)}) copy-start(bf16[2,8,4,2,4096]{4,3,2,1,0:T(2,128)(2,1)} %x_hbm.1) | copy-start | bytes 3145732
  1.2 0.8 copy-start.3
  2.0 0.7 copy-start.6
  2.7 0.7 copy-start.7
  7.2 48.7 %copy-start.8 = (s32[16]{0:T(128)S(1)}, s32[16]{0:T(128)}, u32[]{:S(2)}) copy-start(s32[16]{0:T(128)} %order_ref.1) | copy-start | bytes 196
  55.9 28.5 %copy-start.1 = (f32[128,256]{1,0:T(8,128)S(1)}, f32[128,256]{1,0:T(8,128)}, u32[]{:S(2)}) copy-start(f32[128,256]{1,0:T(8,128)} %constant.14.clone.fine_ref) | copy-start | bytes 393220
  55.9 28.5 %copy-start.2 = (f32[128,128]{1,0:T(8,128)S(1)}, f32[128,128]{1,0:T(8,128)}, u32[]{:S(2)}) copy-start(f32[128,128]{1,0:T(8,128)} %constant.17.clone.flip_ref) | copy-start | bytes 196612
  55.9 28.5 %copy-start.4 = (f32[2,32,128]{2,1,0:T(8,128)S(1)}, f32[2,32,128]{2,1,0:T(8,128)}, u32[]{:S(2)}) copy-start(f32[2,32,128]{2,1,0:T(8,128)} %constant.15.clone.coarse_ref) | copy-start | bytes 98308
  55.9 28.5 %copy-start.5 = (f32[2,8,8]{2,1,0:T(8,128)S(1)}, f32[2,8,8]{2,1,0:T(8,128)}, u32[]{:S(2)}) copy-start(f32[2,8,8]{2,1,0:T(8,128)} %constant.16.clone.period_ref) | copy-start | bytes 1540

commit v3 on v2

--- a/solution.py
+++ b/solution.py
@@ -6,6 +6,7 @@
 from jax import lax
 from jax.experimental import pallas as pl
 from jax.experimental.pallas import tpu as pltpu
+from jax.sharding import Mesh
 from jax.sharding import PartitionSpec as P
 
 S = 16
@@ -15,7 +16,9 @@
 SPP = 128
 CB = 32
 STN = 8
-TM = 32
+QUARTERS = 4
+UNITS = 8
+ITEMS = 4
 K = 4
 SPECTRA = 2 * K
 LANES = 128
@@ -158,13 +161,7 @@
     return stage[0]
 
 
-def pair_scales(y_ref):
-    lane = lanes_of((TM, LANES))
-    seen = jnp.zeros((TM, LANES), jnp.float32)
-    for n in range(STN):
-        seen = jnp.where(
-            lane // SPECTRA == n, y_ref[n, :, SPECTRA].astype(jnp.float32)[:, 0, :], seen
-        )
+def pair_counts(seen):
     seen = seen.astype(jnp.bfloat16)
     together = lax.dot_general(
         seen, seen, (((0,), (0,)), ((), ())), preferred_element_type=jnp.float32
@@ -173,97 +170,121 @@
     together = jnp.where(i % K == j % K, together, 0.0).astype(jnp.bfloat16)
     partner = jnp.where(i // K == j, 1.0, 0.0).astype(jnp.bfloat16)
     summed = jnp.dot(together, partner, preferred_element_type=jnp.float32)
-    a, b = rows_of((STN * 8, LANES)), lanes_of((STN * 8, LANES))
-    station = jnp.where(a // 4 == b // K, 1.0, 0.0).astype(jnp.bfloat16)
-    counts = jnp.dot(
-        station, summed.astype(jnp.bfloat16), preferred_element_type=jnp.float32
-    )
-    return 1.0 / jnp.sqrt(jnp.maximum(counts, 1.0))
-
-
-def correlate_kernel(order_ref, y_ref, out_ref, mine_ref, theirs_ref, crossed_ref, scales, place_ref):
+    station = jnp.where(rows_of((S, LANES)) == lanes_of((S, LANES)) // K, 1.0, 0.0)
+    return jnp.dot(
+        station.astype(jnp.bfloat16),
+        summed.astype(jnp.bfloat16),
+        preferred_element_type=jnp.float32,
+    )
+
+
+PAIRS = [(n, m) for n in range(STN) for m in range(n, STN)]
+
+
+def correlate_kernel(order_ref, y_ref, out_ref, mine_ref, theirs_ref, crossed_ref, tiles, counts, place_ref):
     for j in range(S):
         place_ref[order_ref[j]] = j
     row = rows_of((8, LANES))
-    scales[...] = pair_scales(y_ref)
-
-    def unpack(t, carry):
-        for n in range(STN):
-            x = y_ref[n, t, 0:SPECTRA].reshape(2 * SPECTRA, LANES).astype(jnp.float32)
-            re, im = x[:SPECTRA], x[SPECTRA:]
-            total, gap = re + im, im - re
-            for part, value in enumerate((re, im, total)):
-                mine_ref[n, part, t] = value
-            for part, value in enumerate((total, gap)):
-                theirs_ref[n, part, t] = value
-            for part, value in enumerate((re, total, gap)):
-                crossed_ref[n, part, t] = pltpu.roll(value, 4, 0)
-        return carry
-
-    lax.fori_loop(0, TM, unpack, 0)
-    conjugate = jnp.where(row % 2 == 0, 1.0, -1.0)
+    lane = lanes_of((8, LANES))
     zero = jnp.zeros((8, LANES), jnp.float32)
 
-    def finish(n, m, sums):
+    def finish(n, m, item, sums):
         values = []
         for number, (first, second, third) in enumerate((sums[:3], sums[3:])):
             real = first + third
             imag = zero if n == m and number == 0 else first - second
             values += [real, imag]
         tile = group_sums(values, 4)
-        scale = scales[n * 8 : n * 8 + 8, :]
-        even = jnp.broadcast_to(scale[:, 2 * m : 2 * m + 1], (8, LANES))
-        odd = jnp.broadcast_to(scale[:, 2 * m + 1 : 2 * m + 2], (8, LANES))
-        tile = tile * jnp.where((row < 2) | (row >= 6), even, odd)
-        other = tile * conjugate
-        for pair in range(4):
-            h = pair // 2
+        if n == m:
+            left = tile - tile.astype(jnp.bfloat16).astype(jnp.float32)
+            tile = jnp.where(row % 4 == 1, pltpu.roll(left, 1, 0), tile)
+        tiles[PAIRS.index((n, m)), item] = tile
+
+    def one_item(item, carry):
+        seen = zero
+        for n in range(STN):
+            for u in range(UNITS):
+                x = y_ref[n, u, item, 0:SPECTRA].reshape(2 * SPECTRA, LANES)
+                x = x.astype(jnp.float32)
+                re, im = x[:SPECTRA], x[SPECTRA:]
+                total, gap = re + im, im - re
+                for part, value in enumerate((re, im, total)):
+                    mine_ref[n, part, u] = value
+                theirs_ref[n, u] = gap
+                for part, value in enumerate((re, total, gap)):
+                    crossed_ref[n, part, u] = pltpu.roll(value, 4, 0)
+            weight = y_ref[n, :, item, SPECTRA].astype(jnp.float32)[:, 0, :]
+            seen = jnp.where(lane // SPECTRA == n, weight, seen)
+        counts[item] = pair_counts(seen)
+        for block_n in range(0, STN, 2):
+            for block_m in range(block_n, STN, 2):
+                pairs = [
+                    (n, m)
+                    for n in range(block_n, block_n + 2)
+                    for m in range(block_m, block_m + 2)
+                    if n <= m
+                ]
+                sums = {pair: None for pair in pairs}
+                for u in range(UNITS):
+                    mine = {
+                        n: [mine_ref[n, part, u] for part in range(3)]
+                        for n in range(block_n, block_n + 2)
+                    }
+                    theirs = {
+                        m: [
+                            mine_ref[m, 0, u],
+                            mine_ref[m, 2, u],
+                            theirs_ref[m, u],
+                            *(crossed_ref[m, part, u] for part in range(3)),
+                        ]
+                        for m in range(block_m, block_m + 2)
+                    }
+                    for n, m in pairs:
+                        re, im, both = mine[n]
+                        terms = [
+                            f * o
+                            for f, o in zip((both, re, im, both, re, im), theirs[m])
+                        ]
+                        old = sums[n, m]
+                        sums[n, m] = (
+                            terms if old is None else [x + y for x, y in zip(old, terms)]
+                        )
+                for n, m in pairs:
+                    finish(n, m, item, sums[n, m])
+        return carry
+
+    lax.fori_loop(0, ITEMS, one_item, 0)
+    conjugate = jnp.where(row % 2 == 0, 1.0, -1.0)
+    upper, inner = row < 4, row % 4 < 2
+    for number, (n, m) in enumerate(PAIRS):
+        t = [tiles[number, item] for item in range(ITEMS)]
+        halves = (
+            [jnp.where(upper, t[i], pltpu.roll(t[i + 2], 4, 0)) for i in range(2)],
+            [jnp.where(upper, pltpu.roll(t[i], 4, 0), t[i + 2]) for i in range(2)],
+        )
+        for h, (x, y) in enumerate(halves):
+            same = jnp.where(inner, x, pltpu.roll(y, 2, 0))
+            crossed = jnp.where(inner, pltpu.roll(x, 6, 0), y)
             a = 2 * n + h
-            b = 2 * m + (h if pair % 2 == 0 else 1 - h)
-            at = slice(2 * pair, 2 * pair + 2)
-            out_ref[a * S + place_ref[b]] = tile[at]
-            if n != m:
-                out_ref[b * S + place_ref[a]] = other[at]
-
-    for block_n in range(0, STN, 2):
-        for block_m in range(block_n, STN, 2):
-            pairs = [
-                (n, m)
-                for n in range(block_n, block_n + 2)
-                for m in range(block_m, block_m + 2)
-                if n <= m
-            ]
-
-            def add(t, sums, pairs=pairs, block_n=block_n, block_m=block_m):
-                mine = {
-                    n: [mine_ref[n, part, t] for part in range(3)]
-                    for n in range(block_n, block_n + 2)
-                }
-                theirs = {
-                    m: [
-                        mine_ref[m, 0, t],
-                        theirs_ref[m, 0, t],
-                        theirs_ref[m, 1, t],
-                        *(crossed_ref[m, part, t] for part in range(3)),
-                    ]
-                    for m in range(block_m, block_m + 2)
-                }
-                result = []
-                for (n, m), total in zip(pairs, sums):
-                    re, im, both = mine[n]
-                    factors = (both, re, im, both, re, im)
-                    result.append(
-                        tuple(
-                            t0 + f * o for t0, f, o in zip(total, factors, theirs[m])
-                        )
+            for b, value in ((2 * m + h, same), (2 * m + 1 - h, crossed)):
+                out_ref[a * S + place_ref[b], 0:ITEMS] = value.astype(
+                    jnp.bfloat16
+                ).reshape(ITEMS, 2, LANES)
+                if n != m:
+                    out_ref[b * S + place_ref[a], 0:ITEMS] = (
+                        (value * conjugate).astype(jnp.bfloat16).reshape(ITEMS, 2, LANES)
                     )
-                return tuple(result)
-
-            sums = lax.fori_loop(
-                0, TM, add, tuple((zero,) * 6 for _ in pairs), unroll=4
-            )
-            for (n, m), total in zip(pairs, sums):
-                finish(n, m, total)
+    group = lanes_of((S, LANES)) // (LANES // ITEMS)
+    for b in range(S):
+        seen = jnp.zeros((S, LANES), jnp.float32)
+        for item in range(ITEMS):
+            column = jnp.broadcast_to(counts[item, :, b : b + 1], (S, LANES))
+            seen = jnp.where(group == item, column, seen)
+        at = place_ref[b]
+        for a in range(S):
+            out_ref[a * S + at, ITEMS] = jnp.broadcast_to(
+                seen[a : a + 1], (2, LANES)
+            ).astype(jnp.bfloat16)
 
 
 def correlated(order, arrived):
@@ -274,17 +295,18 @@
             pl.BlockSpec(memory_space=pltpu.VMEM),
         ],
         out_specs=pl.BlockSpec(memory_space=pltpu.VMEM),
-        out_shape=jax.ShapeDtypeStruct((S * S, 2, LANES), jnp.float32),
+        out_shape=jax.ShapeDtypeStruct((S * S, ITEMS + 1, 2, LANES), jnp.bfloat16),
         scratch_shapes=[
-            pltpu.VMEM((STN, 3, TM, 8, LANES), jnp.float32),
-            pltpu.VMEM((STN, 2, TM, 8, LANES), jnp.float32),
-            pltpu.VMEM((STN, 3, TM, 8, LANES), jnp.float32),
-            pltpu.VMEM((STN * 8, LANES), jnp.float32),
+            pltpu.VMEM((STN, 3, UNITS, 8, LANES), jnp.float32),
+            pltpu.VMEM((STN, UNITS, 8, LANES), jnp.float32),
+            pltpu.VMEM((STN, 3, UNITS, 8, LANES), jnp.float32),
+            pltpu.VMEM((len(PAIRS), ITEMS, 8, LANES), jnp.float32),
+            pltpu.VMEM((ITEMS, S, LANES), jnp.float32),
             pltpu.SMEM((S,), jnp.int32),
         ],
-        compiler_params=pltpu.CompilerParams(vmem_limit_bytes=48 * 2**20),
+        compiler_params=pltpu.CompilerParams(vmem_limit_bytes=32 * 2**20),
         name="correlate",
-    )(order, arrived.reshape(STN, TM, SPECTRA + 1, 2, LANES))
+    )(order, arrived.reshape(STN, UNITS, ITEMS, SPECTRA + 1, 2, LANES))
 
 
 def fringe_tables():
@@ -306,10 +328,44 @@
     ]
 
 
-def fringe_kernel(z_ref, fine_ref, coarse_ref, period_ref, flip_ref, out_ref):
+def fringe_kernel(
+    row_ref, order_ref, z_ref, fine_ref, coarse_ref, period_ref, flip_ref, out_ref, sums, scales
+):
+    for p in range(PERIODS):
+        for u in range(UNITS):
+            parts = [
+                z_ref[p, quarter, u, 0:ITEMS].reshape(2 * ITEMS, LANES).astype(jnp.float32)
+                for quarter in range(QUARTERS)
+            ]
+            at = (p * UNITS + u) * 2 * ITEMS
+            sums[at : at + 2 * ITEMS] = (parts[0] + parts[1]) + (parts[2] + parts[3])
+        counts = sum(
+            z_ref[p, quarter, :, ITEMS].astype(jnp.float32)[:, 0, :]
+            for quarter in range(QUARTERS)
+        )
+        scale = 1.0 / jnp.sqrt(jnp.maximum(counts, 1.0))
+        for item in range(ITEMS):
+            at = item * (LANES // ITEMS)
+            scales[pl.ds(p * CB + item, UNITS, stride=ITEMS), :] = jnp.broadcast_to(
+                scale[:, at : at + 1], (UNITS, LANES)
+            )
+    alone = order_ref[row_ref[0] % S] == row_ref[0] // S
+    left = jnp.where(alone, 1.0, 0.0)
+    first = sums[pl.ds(0, PERIODS * CB, stride=2), :]
+    second = sums[pl.ds(1, PERIODS * CB, stride=2), :]
     fine = fine_ref[...]
-    re = jnp.dot(z_ref[0], fine, precision=HIGHEST, preferred_element_type=jnp.float32)
-    im = jnp.dot(z_ref[1], fine, precision=HIGHEST, preferred_element_type=jnp.float32)
+    re = jnp.dot(
+        (first + left * second) * scales[...],
+        fine,
+        precision=HIGHEST,
+        preferred_element_type=jnp.float32,
+    )
+    im = jnp.dot(
+        (second * (1.0 - left)) * scales[...],
+        fine,
+        precision=HIGHEST,
+        preferred_element_type=jnp.float32,
+    )
     parts = [[], [], [], []]
     for p in range(PERIODS):
         sums = [jnp.zeros((8, LANES), jnp.float32)] * 4
@@ -348,38 +404,55 @@
     out_ref[1, 0] = turn(cosine, imag) - turn(sine, real)
 
 
-def fringed(normed):
+def fringed(row, order, owned):
     return pl.pallas_call(
         fringe_kernel,
-        in_specs=[pl.BlockSpec(memory_space=pltpu.VMEM)] * 5,
+        in_specs=[pl.BlockSpec(memory_space=pltpu.SMEM)] * 2
+        + [pl.BlockSpec(memory_space=pltpu.VMEM)] * 5,
         out_specs=pl.BlockSpec(memory_space=pltpu.VMEM),
         out_shape=jax.ShapeDtypeStruct((2, 1, PERIODS, LAGS), jnp.float32),
+        scratch_shapes=[
+            pltpu.VMEM((PERIODS * CB * 2, LANES), jnp.float32),
+            pltpu.VMEM((PERIODS * CB, LANES), jnp.float32),
+        ],
         compiler_params=pltpu.CompilerParams(vmem_limit_bytes=32 * 2**20),
         name="fringe",
-    )(normed, *fringe_tables())
+    )(
+        row,
+        order,
+        owned.reshape(PERIODS, QUARTERS, UNITS, ITEMS + 1, 2, LANES),
+        *fringe_tables(),
+    )
 
 
 def per_device(spectra, flags, poly_index, delay_model, partner_order):
-    axes = ("stn", "tm")
-    first = (lax.axis_index("tm") * K).astype(jnp.int32).reshape(1)
-    chunks = rotated_chunks(spectra, flags, poly_index, delay_model, first)
-    arrived = lax.all_to_all(chunks, axes, split_axis=0, concat_axis=0, tiled=True)
+    plane = ("stn", "unit")
+    everyone = ("stn", "quarter", "unit")
+    shard = lax.axis_index(("quarter", "unit")).astype(jnp.int32)
+    row = lax.axis_index(everyone).astype(jnp.int32)
+    chunks = rotated_chunks(spectra, flags, poly_index, delay_model, (shard * K).reshape(1))
+    chunks = chunks.reshape(STN * UNITS, ITEMS * (SPECTRA + 1), 2, LANES)
+    arrived = lax.all_to_all(chunks, plane, split_axis=0, concat_axis=0, tiled=True)
     rows = correlated(partner_order, arrived)
-    owned = lax.all_to_all(rows, axes, split_axis=0, concat_axis=0, tiled=True)
-    return fringed(jnp.moveaxis(owned, 1, 0))
+    owned = lax.all_to_all(rows, everyone, split_axis=0, concat_axis=0, tiled=True)
+    return fringed(row.reshape(1), partner_order, owned)
 
 
 def solution(mesh):
+    finer = Mesh(
+        mesh.devices.reshape(STN, QUARTERS, UNITS), ("stn", "quarter", "unit")
+    )
+    time = ("quarter", "unit")
     return jax.shard_map(
         per_device,
-        mesh=mesh,
+        mesh=finer,
         in_specs=(
-            P("stn", None, "tm", None, None),
-            P("stn", None, "tm", None),
-            P("stn", None, "tm"),
+            P("stn", None, time, None, None),
+            P("stn", None, time, None),
+            P("stn", None, time),
             P(),
             P(),
         ),
-        out_specs=P(None, ("stn", "tm"), None, None),
+        out_specs=P(None, ("stn", "quarter", "unit"), None, None),
         check_vma=False,
     )

time: 86.4 us -> 79.8 us (0.924)
  blocking collectives: 71 us -> 29.5 us
  waiting for transfers between devices: 0 us -> 23.7 us
  starting transfers between devices: 0 us -> 10.4 us
  Pallas kernels: 11.6 us -> 12.5 us
    all_to_all x2 -> x1, blocking collectives: 71 us -> 29.5 us  [per_device(): lax.all_to_all(chunks, plane, split_axis=0, concat_axis=0, tiled=True)]
    all_to_all x0 -> x1, waiting for transfers between devices: none -> 23.7 us  [per_device(): lax.all_to_all(rows, everyone, split_axis=0, concat_axis=0, tiled=True)]
    all_to_all x0 -> x1, starting transfers between devices: none -> 10.4 us  [per_device(): lax.all_to_all(rows, everyone, split_axis=0, concat_axis=0, tiled=True)]
    pallas_call x1, Pallas kernels: 1.64 us -> 2.81 us  [fringed(): pl.pallas_call(fringe_kernel, in_specs=[pl.BlockSpec(memory_space=pltpu.S...]
  transfers between devices with their start and end apart: 0 -> 1, of which waited for: 0 -> 1; matrix products, arithmetic and copies ran while one was open for 0% -> 0% of each run, Pallas kernels for 0% -> 0%
where the time goes in v3:
time: 79.8 us; the launch traced here: 79.5 us
  blocking collectives  29.5 us (37%)
  waiting for transfers between devices  23.7 us (30%)
  Pallas kernels  12.5 us (16%)
  starting transfers between devices  10.4 us (13%)
  local copies, waits for them, and re-layouts  3.37 us (4%)
    all_to_all x1, blocking collectives, per_device(): lax.all_to_all(chunks, plane, split_axis=0, concat_axis=0, tiled=True)  29.5 us
    all_to_all x1, waiting for transfers between devices, per_device(): lax.all_to_all(rows, everyone, split_axis=0, concat_axis=0, tiled=True)  23.7 us
    all_to_all x1, starting transfers between devices, per_device(): lax.all_to_all(rows, everyone, split_axis=0, concat_axis=0, tiled=True)  10.4 us
    pallas_call x1, Pallas kernels, correlated(): pl.pallas_call(correlate_kernel, in_specs=[pl.BlockSpec(memory_space=pltp...  5.78 us
    pallas_call x1, Pallas kernels, rotated_chunks(): pl.pallas_call(rotate_kernel, in_specs=[pl.BlockSpec(memory_space=pltpu.S...  3.87 us
    unnamed x18, local copies, waits for them, and re-layouts  3.37 us
    pallas_call x1, Pallas kernels, fringed(): pl.pallas_call(fringe_kernel, in_specs=[pl.BlockSpec(memory_space=pltpu.S...  2.81 us
  transfers between devices with their start and end apart: 1, of which 1 were waited for; matrix products, arithmetic and copies ran while one was open for 0% of the time, Pallas kernels for 0%

profile of v3, /device:TPU:1, one launch (start us, length us, event | category | flops | bytes accessed | tf_op | source)
XLA Modules:
  0.0 79.5 jit_solution(9490273834366701428)
XLA Ops:
  0.0 0.0 copy-start
  0.0 1.2 %copy-done = bf16[2,8,4,2,4096]{4,3,2,1,0:T(2,128)(2,1)S(1)} copy-done((bf16[2,8,4,2,4096]{4,3,2,1,0:T(2,128)(2,1)S(1)}, bf16[2,8,4,2,4096]{4,3,2,1,0:T(2,128)(2,1)}, u32[]{:S(2)}) %copy-start) | copy-done | bytes 1048600
  1.2 0.0 copy-start.3
  1.2 0.8 copy-done.3
  2.0 0.0 copy-start.6
  2.0 0.7 copy-done.6
  2.7 0.0 copy-start.7
  2.7 0.7 copy-done.7
  3.4 3.9 %rotate.1 = bf16[256,9,2,128]{3,2,1,0:T(2,128)(2,1)S(1)} custom-call(s32[1]{0:T(128)} %bitcast.1.first_ref, s32[2,4,8]{2,1,0:T(4,128)S(1)} %bitcast.10, f32[3,64]{1,0:T(4,128)S(1)} %bitcast.11, s32[2,8,4,32]{3,2,1,0:T(4,128)S(1)} %copy-done.3, bf16[2,8,4,2,4096]{4,3,2,1,0:T(2,128)(2,1)S(1)} %copy-done), custom_call_target="tpu_custom_call" | custom-call | tf_op jit(solution)/shard_map/rotate/pallas_call | solution.py:116
  7.2 0.0 copy-start.8
  7.2 29.5 %all_to_all.10 = bf16[64,36,2,128]{3,2,1,0:T(2,128)(2,1)S(1)} all-to-all(bf16[64,36,2,128]{3,2,1,0:T(2,128)(2,1)S(1)} %bitcast.7), channel_id=1, replica_groups=mesh['stn'=8,'quarter'=4,'unit'=8] {'stn','unit'}, dimensions={0} | all-to-all | bytes 2359296 | tf_op jit(solution)/shard_map/all_to_all | solution.py:435
  36.7 0.0 copy-done.8
  36.7 0.0 copy-start.1
  36.7 0.0 copy-start.2
  36.7 0.0 copy-start.4
  36.7 0.0 copy-start.5
  36.7 5.8 %correlate.1 = bf16[256,5,2,128]{3,2,1,0:T(2,128)(2,1)} custom-call(s32[16]{0:T(128)S(1)} %copy-done.8, bf16[8,8,4,9,2,128]{5,4,3,2,1,0:T(2,128)(2,1)S(1)} %bitcast.8), custom_call_target="tpu_custom_call" | custom-call | tf_op jit(solution)/shard_map/correlate/pallas_call | solution.py:291
  42.5 10.4 %all-to-all-start.1 = ((bf16[256,5,2,128]{3,2,1,0:T(2,128)(2,1)}), bf16[256,5,2,128]{3,2,1,0:T(2,128)(2,1)S(1)}, u32[]{:S(2)}, u32[]{:S(2)}) async-start(bf16[256,5,2,128]{3,2,1,0:T(2,128)(2,1)} %correlate.1), calls=%async_computation.1 | async-start | bytes 1310720 | tf_op jit(solution)/shard_map/all_to_all | solution.py:437
  53.0 23.7 %all-to-all-done.1 = bf16[256,5,2,128]{3,2,1,0:T(2,128)(2,1)S(1)} async-done(((bf16[256,5,2,128]{3,2,1,0:T(2,128)(2,1)}), bf16[256,5,2,128]{3,2,1,0:T(2,128)(2,1)S(1)}, u32[]{:S(2)}, u32[]{:S(2)}) %all-to-all-start.1) | async-done | bytes 655392 | tf_op jit(solution)/shard_map/all_to_all | solution.py:437
  76.7 0.0 copy-done.1
  76.7 0.0 copy-done.2
  76.7 0.0 copy-done.4
  76.7 0.0 copy-done.5
  76.7 2.8 %fringe.1 = f32[2,1,8,256]{3,2,1,0:T(8,128)} custom-call(s32[1]{0:T(128)} %bitcast.row_ref, s32[16]{0:T(128)S(1)} %copy-done.8, bf16[8,4,8,5,2,128]{5,4,3,2,1,0:T(2,128)(2,1)S(1)} %bitcast.9, f32[128,256]{1,0:T(8,128)S(1)} %copy-done.1, f32[2,32,128]{2,1,0:T(8,128)S(1)} %copy-done.4, f32[2,8,8]{2,1,0:T(8,128)S(1)} %copy-done.5, f32[128,128]{1,0:T(8,128)S(1)} %copy-done.2), custom_call_target="tpu_custom_call" | custom-call | tf_op jit(solution)/shard_map/fringe/pallas_call | solution.py:408
Async XLA Ops:
  0.0 1.2 %copy-start = (bf16[2,8,4,2,4096]{4,3,2,1,0:T(2,128)(2,1)S(1)}, bf16[2,8,4,2,4096]{4,3,2,1,0:T(2,128)(2,1)}, u32[]{:S(2)}) copy-start(bf16[2,8,4,2,4096]{4,3,2,1,0:T(2,128)(2,1)} %x_hbm.1) | copy-start | bytes 3145732
  1.2 0.8 copy-start.3
  2.0 0.7 copy-start.6
  2.7 0.7 copy-start.7
  7.2 29.5 %copy-start.8 = (s32[16]{0:T(128)S(1)}, s32[16]{0:T(128)}, u32[]{:S(2)}) copy-start(s32[16]{0:T(128)} %order_ref.3) | copy-start | bytes 196
  36.7 40.0 %copy-start.1 = (f32[128,256]{1,0:T(8,128)S(1)}, f32[128,256]{1,0:T(8,128)}, u32[]{:S(2)}) copy-start(f32[128,256]{1,0:T(8,128)} %constant.26.clone.fine_ref) | copy-start | bytes 393220
  36.7 40.0 %copy-start.2 = (f32[128,128]{1,0:T(8,128)S(1)}, f32[128,128]{1,0:T(8,128)}, u32[]{:S(2)}) copy-start(f32[128,128]{1,0:T(8,128)} %constant.29.clone.flip_ref) | copy-start | bytes 196612
  36.7 40.0 %copy-start.4 = (f32[2,32,128]{2,1,0:T(8,128)S(1)}, f32[2,32,128]{2,1,0:T(8,128)}, u32[]{:S(2)}) copy-start(f32[2,32,128]{2,1,0:T(8,128)} %constant.27.clone.coarse_ref) | copy-start | bytes 98308
  36.7 40.0 %copy-start.5 = (f32[2,8,8]{2,1,0:T(8,128)S(1)}, f32[2,8,8]{2,1,0:T(8,128)}, u32[]{:S(2)}) copy-start(f32[2,8,8]{2,1,0:T(8,128)} %constant.28.clone.period_ref) | copy-start | bytes 1540
  42.5 34.2 %all-to-all-start.1 = ((bf16[256,5,2,128]{3,2,1,0:T(2,128)(2,1)}), bf16[256,5,2,128]{3,2,1,0:T(2,128)(2,1)S(1)}, u32[]{:S(2)}, u32[]{:S(2)}) async-start(bf16[256,5,2,128]{3,2,1,0:T(2,128)(2,1)} %correlate.1), calls=%async_computation.1 | async-start | bytes 1310720 | tf_op jit(solution)/shard_map/all_to_all | solution.py:437

commit v4 on v3

--- a/solution.py
+++ b/solution.py
@@ -20,6 +20,7 @@
 UNITS = 8
 ITEMS = 4
 K = 4
+NPOLY = 64
 SPECTRA = 2 * K
 LANES = 128
 HALF = LAGS // 2
@@ -34,12 +35,41 @@
     return lax.broadcasted_iota(jnp.int32, shape, len(shape) - 1)
 
 
-def rotate_kernel(first_ref, poly_ref, model_ref, flags_ref, x_hbm, out_ref, x_ref, turned_re, turned_im, sems):
+def in_hbm(array):
+    return pltpu.with_memory_space_constraint(array, pltpu.HBM)
+
+
+def rotate_kernel(
+    first_ref,
+    poly_hbm,
+    model_hbm,
+    flags_hbm,
+    x_hbm,
+    out_ref,
+    poly_ref,
+    model_ref,
+    flags_ref,
+    x_ref,
+    turned_re,
+    turned_im,
+    sems,
+    small_sems,
+):
     def fetch(p):
         return pltpu.make_async_copy(x_hbm.at[:, p], x_ref.at[p], sems.at[p])
 
+    small = [
+        pltpu.make_async_copy(source, target, small_sems.at[number])
+        for number, (source, target) in enumerate(
+            ((poly_hbm, poly_ref), (model_hbm, model_ref), (flags_hbm, flags_ref))
+        )
+    ]
+    for copy in small:
+        copy.start()
     for p in range(PERIODS):
         fetch(p).start()
+    for copy in small:
+        copy.wait()
     row = rows_of((8, LANES))
     lane = lanes_of((8, LANES))
     across = jnp.zeros((8, LANES), jnp.float32)
@@ -115,24 +145,29 @@
 def rotated_chunks(spectra, flags, poly_index, delay_model, first):
     return pl.pallas_call(
         rotate_kernel,
-        in_specs=[
-            pl.BlockSpec(memory_space=pltpu.SMEM),
-            pl.BlockSpec(memory_space=pltpu.SMEM),
-            pl.BlockSpec(memory_space=pltpu.SMEM),
-            pl.BlockSpec(memory_space=pltpu.VMEM),
-            pl.BlockSpec(memory_space=pltpu.HBM),
-        ],
+        in_specs=[pl.BlockSpec(memory_space=pltpu.SMEM)]
+        + [pl.BlockSpec(memory_space=pltpu.HBM)] * 4,
         out_specs=pl.BlockSpec(memory_space=pltpu.VMEM),
         out_shape=jax.ShapeDtypeStruct((PERIODS * CB, SPECTRA + 1, 2, LANES), jnp.bfloat16),
         scratch_shapes=[
+            pltpu.SMEM((2, K, PERIODS), jnp.int32),
+            pltpu.SMEM((3, NPOLY), jnp.float32),
+            pltpu.VMEM((2, PERIODS, K, CB), jnp.int32),
             pltpu.VMEM((PERIODS, 2, K, 2, C), jnp.bfloat16),
             pltpu.VMEM((2, CB * SPECTRA, LANES), jnp.float32),
             pltpu.VMEM((2, CB * SPECTRA, LANES), jnp.float32),
             pltpu.SemaphoreType.DMA((PERIODS,)),
+            pltpu.SemaphoreType.DMA((3,)),
         ],
         compiler_params=pltpu.CompilerParams(vmem_limit_bytes=32 * 2**20),
         name="rotate",
-    )(first, poly_index.transpose(0, 2, 1), delay_model.T, flags, spectra)
+    )(
+        first,
+        in_hbm(poly_index.transpose(0, 2, 1)),
+        in_hbm(delay_model.T),
+        in_hbm(flags),
+        in_hbm(spectra),
+    )
 
 
 def group_sums(values, group):

time: 79.8 us -> 76.2 us (0.955)
  local copies, waits for them, and re-layouts: 3.37 us -> 0.02 us
    unnamed x18 -> x10, local copies, waits for them, and re-layouts: 3.37 us -> 0.02 us
where the time goes in v4:
time: 76.2 us; the launch traced here: 76 us
  blocking collectives  29.5 us (39%)
  waiting for transfers between devices  23.7 us (31%)
  Pallas kernels  12.3 us (16%)
  starting transfers between devices  10.4 us (14%)
    all_to_all x1, blocking collectives, per_device(): lax.all_to_all(chunks, plane, split_axis=0, concat_axis=0, tiled=True)  29.5 us
    all_to_all x1, waiting for transfers between devices, per_device(): lax.all_to_all(rows, everyone, split_axis=0, concat_axis=0, tiled=True)  23.7 us
    all_to_all x1, starting transfers between devices, per_device(): lax.all_to_all(rows, everyone, split_axis=0, concat_axis=0, tiled=True)  10.4 us
    pallas_call x1, Pallas kernels, correlated(): pl.pallas_call(correlate_kernel, in_specs=[pl.BlockSpec(memory_space=pltp...  5.77 us
    pallas_call x1, Pallas kernels, rotated_chunks(): pl.pallas_call(rotate_kernel, in_specs=[pl.BlockSpec(memory_space=pltpu.S...  3.74 us
    pallas_call x1, Pallas kernels, fringed(): pl.pallas_call(fringe_kernel, in_specs=[pl.BlockSpec(memory_space=pltpu.S...  2.81 us
  transfers between devices with their start and end apart: 1, of which 1 were waited for; matrix products, arithmetic and copies ran while one was open for 0% of the time, Pallas kernels for 0%

profile of v4, /device:TPU:1, one launch (start us, length us, event | category | flops | bytes accessed | tf_op | source)
XLA Modules:
  0.0 76.0 jit_solution(8101174907606201436)
XLA Ops:
  0.0 3.7 %rotate.1 = bf16[256,9,2,128]{3,2,1,0:T(2,128)(2,1)S(1)} custom-call(s32[1]{0:T(128)} %bitcast.1.first_ref, s32[2,4,8]{2,1,0:T(4,128)} %bitcast.10, f32[3,64]{1,0:T(4,128)} %bitcast.11, s32[2,8,4,32]{3,2,1,0:T(4,128)} %flags_hbm.1, bf16[2,8,4,2,4096]{4,3,2,1,0:T(2,128)(2,1)} %x_hbm.1), custom_call_target="tpu_custom_call" | custom-call | tf_op jit(solution)/shard_map/rotate/pallas_call | solution.py:146
  3.7 0.0 copy-start.4
  3.8 29.5 %all_to_all.10 = bf16[64,36,2,128]{3,2,1,0:T(2,128)(2,1)S(1)} all-to-all(bf16[64,36,2,128]{3,2,1,0:T(2,128)(2,1)S(1)} %bitcast.7), channel_id=1, replica_groups=mesh['stn'=8,'quarter'=4,'unit'=8] {'stn','unit'}, dimensions={0} | all-to-all | bytes 2359296 | tf_op jit(solution)/shard_map/all_to_all | solution.py:470
  33.2 0.0 copy-done.4
  33.2 0.0 copy-start
  33.2 0.0 copy-start.1
  33.2 0.0 copy-start.2
  33.2 0.0 copy-start.3
  33.3 5.8 %correlate.1 = bf16[256,5,2,128]{3,2,1,0:T(2,128)(2,1)} custom-call(s32[16]{0:T(128)S(1)} %copy-done.4, bf16[8,8,4,9,2,128]{5,4,3,2,1,0:T(2,128)(2,1)S(1)} %bitcast.8), custom_call_target="tpu_custom_call" | custom-call | tf_op jit(solution)/shard_map/correlate/pallas_call | solution.py:326
  39.0 10.4 %all-to-all-start.1 = ((bf16[256,5,2,128]{3,2,1,0:T(2,128)(2,1)}), bf16[256,5,2,128]{3,2,1,0:T(2,128)(2,1)S(1)}, u32[]{:S(2)}, u32[]{:S(2)}) async-start(bf16[256,5,2,128]{3,2,1,0:T(2,128)(2,1)} %correlate.1), calls=%async_computation.1 | async-start | bytes 1310720 | tf_op jit(solution)/shard_map/all_to_all | solution.py:472
  49.5 23.7 %all-to-all-done.1 = bf16[256,5,2,128]{3,2,1,0:T(2,128)(2,1)S(1)} async-done(((bf16[256,5,2,128]{3,2,1,0:T(2,128)(2,1)}), bf16[256,5,2,128]{3,2,1,0:T(2,128)(2,1)S(1)}, u32[]{:S(2)}, u32[]{:S(2)}) %all-to-all-start.1) | async-done | bytes 655392 | tf_op jit(solution)/shard_map/all_to_all | solution.py:472
  73.2 0.0 copy-done
  73.2 0.0 copy-done.1
  73.2 0.0 copy-done.2
  73.2 0.0 copy-done.3
  73.2 2.8 %fringe.1 = f32[2,1,8,256]{3,2,1,0:T(8,128)} custom-call(s32[1]{0:T(128)} %bitcast.row_ref, s32[16]{0:T(128)S(1)} %copy-done.4, bf16[8,4,8,5,2,128]{5,4,3,2,1,0:T(2,128)(2,1)S(1)} %bitcast.9, f32[128,256]{1,0:T(8,128)S(1)} %copy-done, f32[2,32,128]{2,1,0:T(8,128)S(1)} %copy-done.2, f32[2,8,8]{2,1,0:T(8,128)S(1)} %copy-done.3, f32[128,128]{1,0:T(8,128)S(1)} %copy-done.1), custom_call_target="tpu_custom_call" | custom-call | tf_op jit(solution)/shard_map/fringe/pallas_call | solution.py:443
Async XLA Ops:
  3.7 29.5 %copy-start.4 = (s32[16]{0:T(128)S(1)}, s32[16]{0:T(128)}, u32[]{:S(2)}) copy-start(s32[16]{0:T(128)} %order_ref.3) | copy-start | bytes 196
  33.2 40.0 %copy-start = (f32[128,256]{1,0:T(8,128)S(1)}, f32[128,256]{1,0:T(8,128)}, u32[]{:S(2)}) copy-start(f32[128,256]{1,0:T(8,128)} %constant.26.clone.fine_ref) | copy-start | bytes 393220
  33.2 40.0 %copy-start.1 = (f32[128,128]{1,0:T(8,128)S(1)}, f32[128,128]{1,0:T(8,128)}, u32[]{:S(2)}) copy-start(f32[128,128]{1,0:T(8,128)} %constant.29.clone.flip_ref) | copy-start | bytes 196612
  33.2 40.0 %copy-start.2 = (f32[2,32,128]{2,1,0:T(8,128)S(1)}, f32[2,32,128]{2,1,0:T(8,128)}, u32[]{:S(2)}) copy-start(f32[2,32,128]{2,1,0:T(8,128)} %constant.27.clone.coarse_ref) | copy-start | bytes 98308
  33.2 40.0 %copy-start.3 = (f32[2,8,8]{2,1,0:T(8,128)S(1)}, f32[2,8,8]{2,1,0:T(8,128)}, u32[]{:S(2)}) copy-start(f32[2,8,8]{2,1,0:T(8,128)} %constant.28.clone.period_ref) | copy-start | bytes 1540
  39.0 34.2 %all-to-all-start.1 = ((bf16[256,5,2,128]{3,2,1,0:T(2,128)(2,1)}), bf16[256,5,2,128]{3,2,1,0:T(2,128)(2,1)S(1)}, u32[]{:S(2)}, u32[]{:S(2)}) async-start(bf16[256,5,2,128]{3,2,1,0:T(2,128)(2,1)} %correlate.1), calls=%async_computation.1 | async-start | bytes 1310720 | tf_op jit(solution)/shard_map/all_to_all | solution.py:472

commit v5 on v4

--- a/solution.py
+++ b/solution.py
@@ -2,6 +2,7 @@
 
 import jax
 import jax.numpy as jnp
+import ml_dtypes
 import numpy as np
 from jax import lax
 from jax.experimental import pallas as pl
@@ -22,9 +23,12 @@
 K = 4
 NPOLY = 64
 SPECTRA = 2 * K
+TILES = ITEMS * SPECTRA + 1
 LANES = 128
 HALF = LAGS // 2
 HIGHEST = lax.Precision.HIGHEST
+COSINE = [(-1) ** n * (2 * math.pi) ** (2 * n) / math.factorial(2 * n) for n in range(10)]
+SINE = [(-1) ** n * (2 * math.pi) ** (2 * n + 1) / math.factorial(2 * n + 1) for n in range(10)]
 
 
 def rows_of(shape):
@@ -35,12 +39,25 @@
     return lax.broadcasted_iota(jnp.int32, shape, len(shape) - 1)
 
 
+def turn(delay, index, whole):
+    turns = delay * index.astype(jnp.float32) * (1.0 / whole)
+    turns = turns - jnp.round(turns)
+    square = turns * turns
+    cosine = jnp.full_like(square, COSINE[-1])
+    for coefficient in COSINE[-2::-1]:
+        cosine = cosine * square + coefficient
+    sine = jnp.full_like(square, SINE[-1])
+    for coefficient in SINE[-2::-1]:
+        sine = sine * square + coefficient
+    return cosine, sine * turns
+
+
 def in_hbm(array):
     return pltpu.with_memory_space_constraint(array, pltpu.HBM)
 
 
 def rotate_kernel(
-    first_ref,
+    place_ref,
     poly_hbm,
     model_hbm,
     flags_hbm,
@@ -79,7 +96,7 @@
         for s in range(2):
             for k in range(K):
                 index = poly_ref[s, k, p]
-                time = p * SPP + first_ref[0] + k
+                time = p * SPP + place_ref[0] % (QUARTERS * UNITS) * K + k
                 moment = time.astype(jnp.float32) * (1.0 / (PERIODS * SPP))
                 delay = (
                     model_ref[0, index]
@@ -89,9 +106,7 @@
                 column = jnp.where(row == s * K + k, delay, column)
                 across = jnp.where(lane == p * SPECTRA + s * K + k, delay, across)
         down.append(column)
-    fine = [d * (lane.astype(jnp.float32) * (math.pi / C)) for d in down]
-    fine_cos = [jnp.cos(f) for f in fine]
-    fine_sin = [jnp.sin(f) for f in fine]
+    fine_cos, fine_sin = zip(*(turn(column, lane, 2 * C) for column in down))
     weight = 1.0 - flags_ref[...].reshape(2 * PERIODS * K, CB).astype(jnp.float32)
     weight = weight.astype(jnp.bfloat16)
     source = rows_of((2 * PERIODS * K, LANES))
@@ -110,13 +125,17 @@
     coarse_weight = spread(
         jnp.where(target == source_p * SPECTRA + spectrum, 1.0, 0.0)
     )
-    block = rows_of((CB, LANES)).astype(jnp.float32)
-    coarse = jnp.tile(across, (CB // 8, 1)) * (block * (math.pi * LANES / C))
-    coarse_cos = coarse_weight * jnp.cos(coarse)
-    coarse_sin = coarse_weight * jnp.sin(coarse)
+    block = rows_of((CB, LANES))
+    cosine, sine = turn(jnp.tile(across, (CB // 8, 1)), block, 2 * CB)
+    coarse_cos = coarse_weight * cosine
+    coarse_sin = coarse_weight * sine
+    held = block % ITEMS == lanes_of((CB, LANES)) // (LANES // ITEMS)
+    merge = rows_of((UNITS, CB)) == lanes_of((UNITS, CB)) // ITEMS
+    merge = jnp.where(merge, 1.0, 0.0).astype(jnp.bfloat16)
     for p in range(PERIODS):
         mark = jnp.where((source_p == p) & (target % SPECTRA == spectrum), 1.0, 0.0)
-        sent = spread(mark).astype(jnp.bfloat16)
+        sent = jnp.where(held, spread(mark), 0.0).astype(jnp.bfloat16)
+        sent = jnp.dot(merge, sent, preferred_element_type=jnp.float32).astype(jnp.bfloat16)
         fetch(p).wait()
         for s in range(2):
             for k in range(K):
@@ -136,19 +155,22 @@
         for q in range(CB):
             at = slice(q * SPECTRA, (q + 1) * SPECTRA)
             both = jnp.concatenate([turned_re[p % 2, at], turned_im[p % 2, at]])
-            out_ref[p * CB + q, 0:SPECTRA] = both.astype(jnp.bfloat16).reshape(SPECTRA, 2, LANES)
-        out_ref[p * CB : (p + 1) * CB, SPECTRA] = jnp.broadcast_to(
-            sent[:, None, :], (CB, 2, LANES)
-        )
-
-
-def rotated_chunks(spectra, flags, poly_index, delay_model, first):
+            tile = q % ITEMS * SPECTRA
+            out_ref[p * UNITS + q // ITEMS, tile : tile + SPECTRA] = both.astype(
+                jnp.bfloat16
+            ).reshape(SPECTRA, 2, LANES)
+        out_ref[p * UNITS : (p + 1) * UNITS, TILES - 1] = jnp.broadcast_to(
+            sent[:, None, :], (UNITS, 2, LANES)
+        )
+
+
+def rotated_chunks(spectra, flags, poly_index, delay_model, place):
     return pl.pallas_call(
         rotate_kernel,
         in_specs=[pl.BlockSpec(memory_space=pltpu.SMEM)]
         + [pl.BlockSpec(memory_space=pltpu.HBM)] * 4,
         out_specs=pl.BlockSpec(memory_space=pltpu.VMEM),
-        out_shape=jax.ShapeDtypeStruct((PERIODS * CB, SPECTRA + 1, 2, LANES), jnp.bfloat16),
+        out_shape=jax.ShapeDtypeStruct((PERIODS * UNITS, TILES, 2, LANES), jnp.bfloat16),
         scratch_shapes=[
             pltpu.SMEM((2, K, PERIODS), jnp.int32),
             pltpu.SMEM((3, NPOLY), jnp.float32),
@@ -162,7 +184,7 @@
         compiler_params=pltpu.CompilerParams(vmem_limit_bytes=32 * 2**20),
         name="rotate",
     )(
-        first,
+        place,
         in_hbm(poly_index.transpose(0, 2, 1)),
         in_hbm(delay_model.T),
         in_hbm(flags),
@@ -196,27 +218,10 @@
     return stage[0]
 
 
-def pair_counts(seen):
-    seen = seen.astype(jnp.bfloat16)
-    together = lax.dot_general(
-        seen, seen, (((0,), (0,)), ((), ())), preferred_element_type=jnp.float32
-    )
-    i, j = rows_of((LANES, LANES)), lanes_of((LANES, LANES))
-    together = jnp.where(i % K == j % K, together, 0.0).astype(jnp.bfloat16)
-    partner = jnp.where(i // K == j, 1.0, 0.0).astype(jnp.bfloat16)
-    summed = jnp.dot(together, partner, preferred_element_type=jnp.float32)
-    station = jnp.where(rows_of((S, LANES)) == lanes_of((S, LANES)) // K, 1.0, 0.0)
-    return jnp.dot(
-        station.astype(jnp.bfloat16),
-        summed.astype(jnp.bfloat16),
-        preferred_element_type=jnp.float32,
-    )
-
-
 PAIRS = [(n, m) for n in range(STN) for m in range(n, STN)]
 
 
-def correlate_kernel(order_ref, y_ref, out_ref, mine_ref, theirs_ref, crossed_ref, tiles, counts, place_ref):
+def correlate_kernel(order_ref, y_ref, out_ref, mine_ref, theirs_ref, crossed_ref, tiles, place_ref):
     for j in range(S):
         place_ref[order_ref[j]] = j
     row = rows_of((8, LANES))
@@ -235,11 +240,21 @@
             tile = jnp.where(row % 4 == 1, pltpu.roll(left, 1, 0), tile)
         tiles[PAIRS.index((n, m)), item] = tile
 
+    weights = [
+        y_ref[n, :, TILES - 1].astype(jnp.float32)[:, 0, :] for n in range(STN)
+    ]
+    swapped = [pltpu.roll(weight, K, 1) for weight in weights]
+    products = [weights[n] * weights[m] for n, m in PAIRS]
+    products += [weights[n] * swapped[m] for n, m in PAIRS]
+    counts = [group_sums(products[i : i + 8], 8) for i in range(0, len(products), 8)]
+
+    def count_row(number):
+        return counts[number // 8][number % 8 : number % 8 + 1]
+
     def one_item(item, carry):
-        seen = zero
         for n in range(STN):
             for u in range(UNITS):
-                x = y_ref[n, u, item, 0:SPECTRA].reshape(2 * SPECTRA, LANES)
+                x = y_ref[n, u, pl.ds(item * SPECTRA, SPECTRA)].reshape(2 * SPECTRA, LANES)
                 x = x.astype(jnp.float32)
                 re, im = x[:SPECTRA], x[SPECTRA:]
                 total, gap = re + im, im - re
@@ -248,9 +263,6 @@
                 theirs_ref[n, u] = gap
                 for part, value in enumerate((re, total, gap)):
                     crossed_ref[n, part, u] = pltpu.roll(value, 4, 0)
-            weight = y_ref[n, :, item, SPECTRA].astype(jnp.float32)[:, 0, :]
-            seen = jnp.where(lane // SPECTRA == n, weight, seen)
-        counts[item] = pair_counts(seen)
         for block_n in range(0, STN, 2):
             for block_m in range(block_n, STN, 2):
                 pairs = [
@@ -309,17 +321,17 @@
                     out_ref[b * S + place_ref[a], 0:ITEMS] = (
                         (value * conjugate).astype(jnp.bfloat16).reshape(ITEMS, 2, LANES)
                     )
-    group = lanes_of((S, LANES)) // (LANES // ITEMS)
-    for b in range(S):
-        seen = jnp.zeros((S, LANES), jnp.float32)
-        for item in range(ITEMS):
-            column = jnp.broadcast_to(counts[item, :, b : b + 1], (S, LANES))
-            seen = jnp.where(group == item, column, seen)
-        at = place_ref[b]
-        for a in range(S):
-            out_ref[a * S + at, ITEMS] = jnp.broadcast_to(
-                seen[a : a + 1], (2, LANES)
-            ).astype(jnp.bfloat16)
+        def put(stations, row_of_counts):
+            pair_of_rows = jnp.broadcast_to(row_of_counts, (2, LANES)).astype(jnp.bfloat16)
+            for a, b in stations:
+                out_ref[a * S + place_ref[b], ITEMS] = pair_of_rows
+
+        same, crossed = count_row(number), count_row(len(PAIRS) + number)
+        put([(2 * n + h, 2 * m + h) for h in range(2)], same)
+        put([(2 * n + h, 2 * m + 1 - h) for h in range(2)], crossed)
+        if n != m:
+            put([(2 * m + h, 2 * n + h) for h in range(2)], same)
+            put([(2 * m + 1 - h, 2 * n + h) for h in range(2)], pltpu.roll(crossed, K, 1))
 
 
 def correlated(order, arrived):
@@ -336,12 +348,11 @@
             pltpu.VMEM((STN, UNITS, 8, LANES), jnp.float32),
             pltpu.VMEM((STN, 3, UNITS, 8, LANES), jnp.float32),
             pltpu.VMEM((len(PAIRS), ITEMS, 8, LANES), jnp.float32),
-            pltpu.VMEM((ITEMS, S, LANES), jnp.float32),
             pltpu.SMEM((S,), jnp.int32),
         ],
         compiler_params=pltpu.CompilerParams(vmem_limit_bytes=32 * 2**20),
         name="correlate",
-    )(order, arrived.reshape(STN, UNITS, ITEMS, SPECTRA + 1, 2, LANES))
+    )(order, arrived.reshape(STN, UNITS, TILES, 2, LANES))
 
 
 def fringe_tables():
@@ -352,10 +363,12 @@
     period = period / PERIODS
     factor = 1.0 / math.sqrt(PERIODS * C)
     flip = np.eye(HALF)[::-1]
-    return [
+    fine = np.concatenate([np.cos(fine), np.sin(fine)], axis=1).astype(np.float32)
+    high = fine.astype(ml_dtypes.bfloat16)
+    low = (fine - high.astype(np.float32)).astype(ml_dtypes.bfloat16)
+    return [np.concatenate([high, high, low])] + [
         np.ascontiguousarray(table, np.float32)
         for table in (
-            np.concatenate([np.cos(fine), np.sin(fine)], axis=1),
             np.stack([np.cos(coarse), np.sin(coarse)]),
             np.stack([np.cos(period), np.sin(period)]) * factor,
             flip,
@@ -364,7 +377,7 @@
 
 
 def fringe_kernel(
-    row_ref, order_ref, z_ref, fine_ref, coarse_ref, period_ref, flip_ref, out_ref, sums, scales
+    place_ref, order_ref, z_ref, fine_ref, coarse_ref, period_ref, flip_ref, out_ref, sums, scales, seen
 ):
     for p in range(PERIODS):
         for u in range(UNITS):
@@ -374,33 +387,39 @@
             ]
             at = (p * UNITS + u) * 2 * ITEMS
             sums[at : at + 2 * ITEMS] = (parts[0] + parts[1]) + (parts[2] + parts[3])
-        counts = sum(
+        seen[p * UNITS : (p + 1) * UNITS] = sum(
             z_ref[p, quarter, :, ITEMS].astype(jnp.float32)[:, 0, :]
             for quarter in range(QUARTERS)
         )
-        scale = 1.0 / jnp.sqrt(jnp.maximum(counts, 1.0))
-        for item in range(ITEMS):
-            at = item * (LANES // ITEMS)
-            scales[pl.ds(p * CB + item, UNITS, stride=ITEMS), :] = jnp.broadcast_to(
-                scale[:, at : at + 1], (UNITS, LANES)
-            )
-    alone = order_ref[row_ref[0] % S] == row_ref[0] // S
+    source, target = rows_of((LANES, LANES)), lanes_of((LANES, LANES))
+    wide = LANES // ITEMS
+    spectrum = place_ref[0] // S % 2
+    added = (source // wide == target // wide) & (source % wide // K == 4 + spectrum)
+    counts = jnp.dot(
+        seen[...].astype(jnp.bfloat16),
+        jnp.where(added, 1.0, 0.0).astype(jnp.bfloat16),
+        preferred_element_type=jnp.float32,
+    )
+    scale = 1.0 / jnp.sqrt(jnp.maximum(counts, 1.0))
+    for item in range(ITEMS):
+        scales[pl.ds(item, PERIODS * UNITS, stride=ITEMS), :] = jnp.broadcast_to(
+            scale[:, item * wide : item * wide + 1], (PERIODS * UNITS, LANES)
+        )
+    alone = order_ref[place_ref[0] % S] == place_ref[0] // S
     left = jnp.where(alone, 1.0, 0.0)
     first = sums[pl.ds(0, PERIODS * CB, stride=2), :]
     second = sums[pl.ds(1, PERIODS * CB, stride=2), :]
-    fine = fine_ref[...]
-    re = jnp.dot(
-        (first + left * second) * scales[...],
-        fine,
-        precision=HIGHEST,
+    values = jnp.concatenate(
+        [(first + left * second) * scales[...], (second * (1.0 - left)) * scales[...]]
+    )
+    high = values.astype(jnp.bfloat16)
+    low = (values - high.astype(jnp.float32)).astype(jnp.bfloat16)
+    both = jnp.dot(
+        jnp.concatenate([high, low, high], axis=1),
+        fine_ref[...],
         preferred_element_type=jnp.float32,
     )
-    im = jnp.dot(
-        (second * (1.0 - left)) * scales[...],
-        fine,
-        precision=HIGHEST,
-        preferred_element_type=jnp.float32,
-    )
+    re, im = both[: PERIODS * CB], both[PERIODS * CB :]
     parts = [[], [], [], []]
     for p in range(PERIODS):
         sums = [jnp.zeros((8, LANES), jnp.float32)] * 4
@@ -439,7 +458,7 @@
     out_ref[1, 0] = turn(cosine, imag) - turn(sine, real)
 
 
-def fringed(row, order, owned):
+def fringed(place, order, owned):
     return pl.pallas_call(
         fringe_kernel,
         in_specs=[pl.BlockSpec(memory_space=pltpu.SMEM)] * 2
@@ -449,11 +468,12 @@
         scratch_shapes=[
             pltpu.VMEM((PERIODS * CB * 2, LANES), jnp.float32),
             pltpu.VMEM((PERIODS * CB, LANES), jnp.float32),
+            pltpu.VMEM((PERIODS * UNITS, LANES), jnp.float32),
         ],
         compiler_params=pltpu.CompilerParams(vmem_limit_bytes=32 * 2**20),
         name="fringe",
     )(
-        row,
+        place,
         order,
         owned.reshape(PERIODS, QUARTERS, UNITS, ITEMS + 1, 2, LANES),
         *fringe_tables(),
@@ -463,14 +483,13 @@
 def per_device(spectra, flags, poly_index, delay_model, partner_order):
     plane = ("stn", "unit")
     everyone = ("stn", "quarter", "unit")
-    shard = lax.axis_index(("quarter", "unit")).astype(jnp.int32)
     row = lax.axis_index(everyone).astype(jnp.int32)
-    chunks = rotated_chunks(spectra, flags, poly_index, delay_model, (shard * K).reshape(1))
-    chunks = chunks.reshape(STN * UNITS, ITEMS * (SPECTRA + 1), 2, LANES)
+    place = row.reshape(1)
+    chunks = rotated_chunks(spectra, flags, poly_index, delay_model, place)
     arrived = lax.all_to_all(chunks, plane, split_axis=0, concat_axis=0, tiled=True)
     rows = correlated(partner_order, arrived)
     owned = lax.all_to_all(rows, everyone, split_axis=0, concat_axis=0, tiled=True)
-    return fringed(row.reshape(1), partner_order, owned)
+    return fringed(place, partner_order, owned)
 
 
 def solution(mesh):

time: 76.2 us -> 73.6 us (0.966)
  blocking collectives: 29.5 us -> 62.4 us
  waiting for transfers between devices: 23.7 us -> 0 us
  starting transfers between devices: 10.4 us -> 0 us
  Pallas kernels: 12.3 us -> 10.9 us
    all_to_all x0 -> x1, blocking collectives: none -> 34 us  [per_device(): lax.all_to_all(rows, everyone, split_axis=0, concat_axis=0, tiled=True)]
    all_to_all x1 -> x0, waiting for transfers between devices: 23.7 us -> none  [per_device(): lax.all_to_all(rows, everyone, split_axis=0, concat_axis=0, tiled=True)]
    all_to_all x1 -> x0, starting transfers between devices: 10.4 us -> none  [per_device(): lax.all_to_all(rows, everyone, split_axis=0, concat_axis=0, tiled=True)]
    all_to_all x1, blocking collectives: 29.5 us -> 28.4 us  [per_device(): lax.all_to_all(chunks, plane, split_axis=0, concat_axis=0, tiled=True)]
    pallas_call x1, Pallas kernels: 5.77 us -> 4.76 us  [correlated(): pl.pallas_call(correlate_kernel, in_specs=[pl.BlockSpec(memory_space=pltp...]
  transfers between devices with their start and end apart: 1 -> 0, of which waited for: 1 -> 0; matrix products, arithmetic and copies ran while one was open for 0% -> 0% of each run, Pallas kernels for 0% -> 0%
where the time goes in v5:
time: 73.6 us; the launch traced here: 73.4 us
  blocking collectives  62.4 us (85%)
  Pallas kernels  10.9 us (15%)
    all_to_all x1, blocking collectives, per_device(): lax.all_to_all(rows, everyone, split_axis=0, concat_axis=0, tiled=True)  34 us
    all_to_all x1, blocking collectives, per_device(): lax.all_to_all(chunks, plane, split_axis=0, concat_axis=0, tiled=True)  28.4 us
    pallas_call x1, Pallas kernels, correlated(): pl.pallas_call(correlate_kernel, in_specs=[pl.BlockSpec(memory_space=pltp...  4.76 us
    pallas_call x1, Pallas kernels, rotated_chunks(): pl.pallas_call(rotate_kernel, in_specs=[pl.BlockSpec(memory_space=pltpu.S...  3.71 us
    pallas_call x1, Pallas kernels, fringed(): pl.pallas_call(fringe_kernel, in_specs=[pl.BlockSpec(memory_space=pltpu.S...  2.46 us

profile of v5, /device:TPU:1, one launch (start us, length us, event | category | flops | bytes accessed | tf_op | source)
XLA Modules:
  0.0 73.4 jit_solution(8083622679403278303)
XLA Ops:
  0.0 3.7 %rotate.1 = bf16[64,33,2,128]{3,2,1,0:T(2,128)(2,1)S(1)} custom-call(s32[1]{0:T(128)} %bitcast.place_ref, s32[2,4,8]{2,1,0:T(4,128)} %bitcast.7, f32[3,64]{1,0:T(4,128)} %bitcast.8, s32[2,8,4,32]{3,2,1,0:T(4,128)} %flags_hbm.1, bf16[2,8,4,2,4096]{4,3,2,1,0:T(2,128)(2,1)} %x_hbm.1), custom_call_target="tpu_custom_call" | custom-call | tf_op jit(solution)/shard_map/rotate/pallas_call | solution.py:168
  3.7 0.0 copy-start.4
  3.7 28.4 %all_to_all.10 = bf16[64,33,2,128]{3,2,1,0:T(2,128)(2,1)S(1)} all-to-all(bf16[64,33,2,128]{3,2,1,0:T(2,128)(2,1)S(1)} %rotate.1), channel_id=1, replica_groups=mesh['stn'=8,'quarter'=4,'unit'=8] {'stn','unit'}, dimensions={0} | all-to-all | bytes 2162688 | tf_op jit(solution)/shard_map/all_to_all | solution.py:489
  32.2 0.0 copy-done.4
  32.2 4.8 %correlate.1 = bf16[256,5,2,128]{3,2,1,0:T(2,128)(2,1)S(1)} custom-call(s32[16]{0:T(128)S(1)} %copy-done.4, bf16[8,8,33,2,128]{4,3,2,1,0:T(2,128)(2,1)S(1)} %bitcast.5), custom_call_target="tpu_custom_call" | custom-call | tf_op jit(solution)/shard_map/correlate/pallas_call | solution.py:338
  36.9 0.0 copy-start
  36.9 0.0 copy-start.1
  37.0 0.0 copy-start.2
  37.0 0.0 copy-start.3
  37.0 34.0 %all_to_all.11 = bf16[256,5,2,128]{3,2,1,0:T(2,128)(2,1)S(1)} all-to-all(bf16[256,5,2,128]{3,2,1,0:T(2,128)(2,1)S(1)} %correlate.1), channel_id=1, replica_groups=mesh['stn'=8,'quarter'=4,'unit'=8] {'stn','quarter','unit'}, dimensions={0} | all-to-all | bytes 1310720 | tf_op jit(solution)/shard_map/all_to_all | solution.py:491
  70.9 0.0 copy-done
  70.9 0.0 copy-done.1
  70.9 0.0 copy-done.2
  70.9 0.0 copy-done.3
  71.0 2.5 %fringe.1 = f32[2,1,8,256]{3,2,1,0:T(8,128)} custom-call(s32[1]{0:T(128)} %bitcast.place_ref, s32[16]{0:T(128)S(1)} %copy-done.4, bf16[8,4,8,5,2,128]{5,4,3,2,1,0:T(2,128)(2,1)S(1)} %bitcast.6, bf16[384,256]{1,0:T(8,128)(2,1)S(1)} %copy-done, f32[2,32,128]{2,1,0:T(8,128)S(1)} %copy-done.2, f32[2,8,8]{2,1,0:T(8,128)S(1)} %copy-done.3, f32[128,128]{1,0:T(8,128)S(1)} %copy-done.1), custom_call_target="tpu_custom_call" | custom-call | tf_op jit(solution)/shard_map/fringe/pallas_call | solution.py:462
Async XLA Ops:
  3.7 28.4 %copy-start.4 = (s32[16]{0:T(128)S(1)}, s32[16]{0:T(128)}, u32[]{:S(2)}) copy-start(s32[16]{0:T(128)} %order_ref.3) | copy-start | bytes 196
  36.9 34.0 %copy-start = (bf16[384,256]{1,0:T(8,128)(2,1)S(1)}, bf16[384,256]{1,0:T(8,128)(2,1)}, u32[]{:S(2)}) copy-start(bf16[384,256]{1,0:T(8,128)(2,1)} %constant.24.clone.fine_ref) | copy-start | bytes 589828
  36.9 34.0 %copy-start.1 = (f32[128,128]{1,0:T(8,128)S(1)}, f32[128,128]{1,0:T(8,128)}, u32[]{:S(2)}) copy-start(f32[128,128]{1,0:T(8,128)} %constant.27.clone.flip_ref) | copy-start | bytes 196612
  37.0 34.0 %copy-start.2 = (f32[2,32,128]{2,1,0:T(8,128)S(1)}, f32[2,32,128]{2,1,0:T(8,128)}, u32[]{:S(2)}) copy-start(f32[2,32,128]{2,1,0:T(8,128)} %constant.25.clone.coarse_ref) | copy-start | bytes 98308
  37.0 34.0 %copy-start.3 = (f32[2,8,8]{2,1,0:T(8,128)S(1)}, f32[2,8,8]{2,1,0:T(8,128)}, u32[]{:S(2)}) copy-start(f32[2,8,8]{2,1,0:T(8,128)} %constant.26.clone.period_ref) | copy-start | bytes 1540

commit v6 on v5

--- a/solution.py
+++ b/solution.py
@@ -70,21 +70,17 @@
     turned_re,
     turned_im,
     sems,
-    small_sems,
 ):
-    def fetch(p):
-        return pltpu.make_async_copy(x_hbm.at[:, p], x_ref.at[p], sems.at[p])
-
     small = [
-        pltpu.make_async_copy(source, target, small_sems.at[number])
+        pltpu.make_async_copy(source, target, sems.at[number])
         for number, (source, target) in enumerate(
             ((poly_hbm, poly_ref), (model_hbm, model_ref), (flags_hbm, flags_ref))
         )
     ]
     for copy in small:
         copy.start()
-    for p in range(PERIODS):
-        fetch(p).start()
+    fetch = pltpu.make_async_copy(x_hbm, x_ref, sems.at[3])
+    fetch.start()
     for copy in small:
         copy.wait()
     row = rows_of((8, LANES))
@@ -136,11 +132,12 @@
         mark = jnp.where((source_p == p) & (target % SPECTRA == spectrum), 1.0, 0.0)
         sent = jnp.where(held, spread(mark), 0.0).astype(jnp.bfloat16)
         sent = jnp.dot(merge, sent, preferred_element_type=jnp.float32).astype(jnp.bfloat16)
-        fetch(p).wait()
+        if p == 0:
+            fetch.wait()
         for s in range(2):
             for k in range(K):
                 r = s * K + k
-                x = x_ref[p, s, k].astype(jnp.float32)
+                x = x_ref[s, p, k].astype(jnp.float32)
                 re = x[0:1].reshape(CB, LANES)
                 im = x[1:2].reshape(CB, LANES)
                 at = p * SPECTRA + r
@@ -175,11 +172,10 @@
             pltpu.SMEM((2, K, PERIODS), jnp.int32),
             pltpu.SMEM((3, NPOLY), jnp.float32),
             pltpu.VMEM((2, PERIODS, K, CB), jnp.int32),
-            pltpu.VMEM((PERIODS, 2, K, 2, C), jnp.bfloat16),
+            pltpu.VMEM((2, PERIODS, K, 2, C), jnp.bfloat16),
             pltpu.VMEM((2, CB * SPECTRA, LANES), jnp.float32),
             pltpu.VMEM((2, CB * SPECTRA, LANES), jnp.float32),
-            pltpu.SemaphoreType.DMA((PERIODS,)),
-            pltpu.SemaphoreType.DMA((3,)),
+            pltpu.SemaphoreType.DMA((4,)),
         ],
         compiler_params=pltpu.CompilerParams(vmem_limit_bytes=32 * 2**20),
         name="rotate",
@@ -261,8 +257,9 @@
                 for part, value in enumerate((re, im, total)):
                     mine_ref[n, part, u] = value
                 theirs_ref[n, u] = gap
-                for part, value in enumerate((re, total, gap)):
-                    crossed_ref[n, part, u] = pltpu.roll(value, 4, 0)
+                re, im = pltpu.roll(re, 4, 0), pltpu.roll(im, 4, 0)
+                for part, value in enumerate((re, re + im, im - re)):
+                    crossed_ref[n, part, u] = value
         for block_n in range(0, STN, 2):
             for block_m in range(block_n, STN, 2):
                 pairs = [

time: 73.6 us -> 72.6 us (0.986)
  Pallas kernels: 10.9 us -> 9.99 us
    pallas_call x1, Pallas kernels: 3.71 us -> 2.74 us  [rotated_chunks(): pl.pallas_call(rotate_kernel, in_specs=[pl.BlockSpec(memory_space=pltpu.S...]
where the time goes in v6:
time: 72.6 us; the launch traced here: 72.5 us
  blocking collectives  62.4 us (86%)
  Pallas kernels  9.99 us (14%)
    all_to_all x1, blocking collectives, per_device(): lax.all_to_all(rows, everyone, split_axis=0, concat_axis=0, tiled=True)  34 us
    all_to_all x1, blocking collectives, per_device(): lax.all_to_all(chunks, plane, split_axis=0, concat_axis=0, tiled=True)  28.4 us
    pallas_call x1, Pallas kernels, correlated(): pl.pallas_call(correlate_kernel, in_specs=[pl.BlockSpec(memory_space=pltp...  4.79 us
    pallas_call x1, Pallas kernels, rotated_chunks(): pl.pallas_call(rotate_kernel, in_specs=[pl.BlockSpec(memory_space=pltpu.S...  2.74 us
    pallas_call x1, Pallas kernels, fringed(): pl.pallas_call(fringe_kernel, in_specs=[pl.BlockSpec(memory_space=pltpu.S...  2.46 us

profile of v6, /device:TPU:1, one launch (start us, length us, event | category | flops | bytes accessed | tf_op | source)
XLA Modules:
  0.0 72.5 jit_solution(11932115289118886482)
XLA Ops:
  0.0 2.7 %rotate.1 = bf16[64,33,2,128]{3,2,1,0:T(2,128)(2,1)S(1)} custom-call(s32[1]{0:T(128)} %bitcast.place_ref, s32[2,4,8]{2,1,0:T(4,128)} %bitcast.7, f32[3,64]{1,0:T(4,128)} %bitcast.8, s32[2,8,4,32]{3,2,1,0:T(4,128)} %flags_hbm.1, bf16[2,8,4,2,4096]{4,3,2,1,0:T(2,128)(2,1)} %x_hbm.1), custom_call_target="tpu_custom_call" | custom-call | tf_op jit(solution)/shard_map/rotate/pallas_call | solution.py:165
  2.8 0.0 copy-start.4
  2.8 28.4 %all_to_all.10 = bf16[64,33,2,128]{3,2,1,0:T(2,128)(2,1)S(1)} all-to-all(bf16[64,33,2,128]{3,2,1,0:T(2,128)(2,1)S(1)} %rotate.1), channel_id=1, replica_groups=mesh['stn'=8,'quarter'=4,'unit'=8] {'stn','unit'}, dimensions={0} | all-to-all | bytes 2162688 | tf_op jit(solution)/shard_map/all_to_all | solution.py:486
  31.2 0.0 copy-done.4
  31.2 4.8 %correlate.1 = bf16[256,5,2,128]{3,2,1,0:T(2,128)(2,1)S(1)} custom-call(s32[16]{0:T(128)S(1)} %copy-done.4, bf16[8,8,33,2,128]{4,3,2,1,0:T(2,128)(2,1)S(1)} %bitcast.5), custom_call_target="tpu_custom_call" | custom-call | tf_op jit(solution)/shard_map/correlate/pallas_call | solution.py:335
  36.0 0.0 copy-start
  36.0 0.0 copy-start.1
  36.0 0.0 copy-start.2
  36.0 0.0 copy-start.3
  36.0 34.0 %all_to_all.11 = bf16[256,5,2,128]{3,2,1,0:T(2,128)(2,1)S(1)} all-to-all(bf16[256,5,2,128]{3,2,1,0:T(2,128)(2,1)S(1)} %correlate.1), channel_id=1, replica_groups=mesh['stn'=8,'quarter'=4,'unit'=8] {'stn','quarter','unit'}, dimensions={0} | all-to-all | bytes 1310720 | tf_op jit(solution)/shard_map/all_to_all | solution.py:488
  70.0 0.0 copy-done
  70.0 0.0 copy-done.1
  70.0 0.0 copy-done.2
  70.0 0.0 copy-done.3
  70.0 2.5 %fringe.1 = f32[2,1,8,256]{3,2,1,0:T(8,128)} custom-call(s32[1]{0:T(128)} %bitcast.place_ref, s32[16]{0:T(128)S(1)} %copy-done.4, bf16[8,4,8,5,2,128]{5,4,3,2,1,0:T(2,128)(2,1)S(1)} %bitcast.6, bf16[384,256]{1,0:T(8,128)(2,1)S(1)} %copy-done, f32[2,32,128]{2,1,0:T(8,128)S(1)} %copy-done.2, f32[2,8,8]{2,1,0:T(8,128)S(1)} %copy-done.3, f32[128,128]{1,0:T(8,128)S(1)} %copy-done.1), custom_call_target="tpu_custom_call" | custom-call | tf_op jit(solution)/shard_map/fringe/pallas_call | solution.py:459
Async XLA Ops:
  2.8 28.4 %copy-start.4 = (s32[16]{0:T(128)S(1)}, s32[16]{0:T(128)}, u32[]{:S(2)}) copy-start(s32[16]{0:T(128)} %order_ref.3) | copy-start | bytes 196
  36.0 34.0 %copy-start = (bf16[384,256]{1,0:T(8,128)(2,1)S(1)}, bf16[384,256]{1,0:T(8,128)(2,1)}, u32[]{:S(2)}) copy-start(bf16[384,256]{1,0:T(8,128)(2,1)} %constant.24.clone.fine_ref) | copy-start | bytes 589828
  36.0 34.0 %copy-start.1 = (f32[128,128]{1,0:T(8,128)S(1)}, f32[128,128]{1,0:T(8,128)}, u32[]{:S(2)}) copy-start(f32[128,128]{1,0:T(8,128)} %constant.27.clone.flip_ref) | copy-start | bytes 196612
  36.0 34.0 %copy-start.2 = (f32[2,32,128]{2,1,0:T(8,128)S(1)}, f32[2,32,128]{2,1,0:T(8,128)}, u32[]{:S(2)}) copy-start(f32[2,32,128]{2,1,0:T(8,128)} %constant.25.clone.coarse_ref) | copy-start | bytes 98308
  36.0 34.0 %copy-start.3 = (f32[2,8,8]{2,1,0:T(8,128)S(1)}, f32[2,8,8]{2,1,0:T(8,128)}, u32[]{:S(2)}) copy-start(f32[2,8,8]{2,1,0:T(8,128)} %constant.26.clone.period_ref) | copy-start | bytes 1540

commit v7 on v6

--- a/solution.py
+++ b/solution.py
@@ -217,7 +217,7 @@
 PAIRS = [(n, m) for n in range(STN) for m in range(n, STN)]
 
 
-def correlate_kernel(order_ref, y_ref, out_ref, mine_ref, theirs_ref, crossed_ref, tiles, place_ref):
+def correlate_kernel(order_ref, y_ref, out_ref, mine_ref, crossed_ref, tiles, place_ref):
     for j in range(S):
         place_ref[order_ref[j]] = j
     row = rows_of((8, LANES))
@@ -225,11 +225,11 @@
     zero = jnp.zeros((8, LANES), jnp.float32)
 
     def finish(n, m, item, sums):
-        values = []
-        for number, (first, second, third) in enumerate((sums[:3], sums[3:])):
-            real = first + third
-            imag = zero if n == m and number == 0 else first - second
-            values += [real, imag]
+        if n == m:
+            values = [sums[0] + sums[1], zero]
+        else:
+            values = [sums[0] + sums[2], sums[0] - sums[1]]
+        values += [sums[-3] + sums[-1], sums[-3] - sums[-2]]
         tile = group_sums(values, 4)
         if n == m:
             left = tile - tile.astype(jnp.bfloat16).astype(jnp.float32)
@@ -240,12 +240,13 @@
         y_ref[n, :, TILES - 1].astype(jnp.float32)[:, 0, :] for n in range(STN)
     ]
     swapped = [pltpu.roll(weight, K, 1) for weight in weights]
-    products = [weights[n] * weights[m] for n, m in PAIRS]
-    products += [weights[n] * swapped[m] for n, m in PAIRS]
-    counts = [group_sums(products[i : i + 8], 8) for i in range(0, len(products), 8)]
-
-    def count_row(number):
-        return counts[number // 8][number % 8 : number % 8 + 1]
+    products = []
+    for n, m in PAIRS:
+        products += [weights[n] * weights[m], weights[n] * swapped[m]]
+    counts = [
+        group_sums(products[i : i + 8], 8).astype(jnp.bfloat16)
+        for i in range(0, len(products), 8)
+    ]
 
     def one_item(item, carry):
         for n in range(STN):
@@ -253,43 +254,37 @@
                 x = y_ref[n, u, pl.ds(item * SPECTRA, SPECTRA)].reshape(2 * SPECTRA, LANES)
                 x = x.astype(jnp.float32)
                 re, im = x[:SPECTRA], x[SPECTRA:]
-                total, gap = re + im, im - re
-                for part, value in enumerate((re, im, total)):
+                for part, value in enumerate((re, im)):
                     mine_ref[n, part, u] = value
-                theirs_ref[n, u] = gap
-                re, im = pltpu.roll(re, 4, 0), pltpu.roll(im, 4, 0)
-                for part, value in enumerate((re, re + im, im - re)):
-                    crossed_ref[n, part, u] = value
+                    crossed_ref[n, part, u] = pltpu.roll(value, 4, 0)
         for block_n in range(0, STN, 2):
-            for block_m in range(block_n, STN, 2):
+            for block_m in range(block_n - block_n % 2, STN, 2):
                 pairs = [
                     (n, m)
                     for n in range(block_n, block_n + 2)
                     for m in range(block_m, block_m + 2)
                     if n <= m
                 ]
-                sums = {pair: None for pair in pairs}
+                sums = {}
                 for u in range(UNITS):
-                    mine = {
-                        n: [mine_ref[n, part, u] for part in range(3)]
-                        for n in range(block_n, block_n + 2)
-                    }
-                    theirs = {
-                        m: [
-                            mine_ref[m, 0, u],
-                            mine_ref[m, 2, u],
-                            theirs_ref[m, u],
-                            *(crossed_ref[m, part, u] for part in range(3)),
-                        ]
-                        for m in range(block_m, block_m + 2)
-                    }
+                    mine, theirs = {}, {}
+                    for n in range(block_n, block_n + 2):
+                        re, im = mine_ref[n, 0, u], mine_ref[n, 1, u]
+                        mine[n] = re, im, re + im
+                    for m in range(block_m, block_m + 2):
+                        for number, ref in enumerate((mine_ref, crossed_ref)):
+                            re, im = ref[m, 0, u], ref[m, 1, u]
+                            theirs[m, number] = re, re + im, im - re
                     for n, m in pairs:
                         re, im, both = mine[n]
-                        terms = [
-                            f * o
-                            for f, o in zip((both, re, im, both, re, im), theirs[m])
-                        ]
-                        old = sums[n, m]
+                        terms = []
+                        for number in range(2):
+                            their_re, their_both, their_gap = theirs[m, number]
+                            if n == m and not number:
+                                terms += [re * re, im * im]
+                            else:
+                                terms += [both * their_re, re * their_both, im * their_gap]
+                        old = sums.get((n, m))
                         sums[n, m] = (
                             terms if old is None else [x + y for x, y in zip(old, terms)]
                         )
@@ -318,17 +313,13 @@
                     out_ref[b * S + place_ref[a], 0:ITEMS] = (
                         (value * conjugate).astype(jnp.bfloat16).reshape(ITEMS, 2, LANES)
                     )
-        def put(stations, row_of_counts):
-            pair_of_rows = jnp.broadcast_to(row_of_counts, (2, LANES)).astype(jnp.bfloat16)
-            for a, b in stations:
+        pair_of_rows = counts[number // 4][number % 4 * 2 : number % 4 * 2 + 2]
+        for h in range(2):
+            for other in range(2):
+                a, b = 2 * n + h, 2 * m + other
                 out_ref[a * S + place_ref[b], ITEMS] = pair_of_rows
-
-        same, crossed = count_row(number), count_row(len(PAIRS) + number)
-        put([(2 * n + h, 2 * m + h) for h in range(2)], same)
-        put([(2 * n + h, 2 * m + 1 - h) for h in range(2)], crossed)
-        if n != m:
-            put([(2 * m + h, 2 * n + h) for h in range(2)], same)
-            put([(2 * m + 1 - h, 2 * n + h) for h in range(2)], pltpu.roll(crossed, K, 1))
+                if n != m:
+                    out_ref[b * S + place_ref[a], ITEMS] = pair_of_rows
 
 
 def correlated(order, arrived):
@@ -341,9 +332,8 @@
         out_specs=pl.BlockSpec(memory_space=pltpu.VMEM),
         out_shape=jax.ShapeDtypeStruct((S * S, ITEMS + 1, 2, LANES), jnp.bfloat16),
         scratch_shapes=[
-            pltpu.VMEM((STN, 3, UNITS, 8, LANES), jnp.float32),
-            pltpu.VMEM((STN, UNITS, 8, LANES), jnp.float32),
-            pltpu.VMEM((STN, 3, UNITS, 8, LANES), jnp.float32),
+            pltpu.VMEM((STN, 2, UNITS, 8, LANES), jnp.float32),
+            pltpu.VMEM((STN, 2, UNITS, 8, LANES), jnp.float32),
             pltpu.VMEM((len(PAIRS), ITEMS, 8, LANES), jnp.float32),
             pltpu.SMEM((S,), jnp.int32),
         ],
@@ -376,6 +366,9 @@
 def fringe_kernel(
     place_ref, order_ref, z_ref, fine_ref, coarse_ref, period_ref, flip_ref, out_ref, sums, scales, seen
 ):
+    mine, partner = place_ref[0] // S, order_ref[place_ref[0] % S]
+    crossed = mine % 2 != partner % 2
+    spectrum = jnp.where(mine // 2 <= partner // 2, mine % 2, partner % 2)
     for p in range(PERIODS):
         for u in range(UNITS):
             parts = [
@@ -384,13 +377,14 @@
             ]
             at = (p * UNITS + u) * 2 * ITEMS
             sums[at : at + 2 * ITEMS] = (parts[0] + parts[1]) + (parts[2] + parts[3])
-        seen[p * UNITS : (p + 1) * UNITS] = sum(
-            z_ref[p, quarter, :, ITEMS].astype(jnp.float32)[:, 0, :]
-            for quarter in range(QUARTERS)
+        counts = sum(
+            z_ref[p, quarter, :, ITEMS].astype(jnp.float32) for quarter in range(QUARTERS)
+        )
+        seen[p * UNITS : (p + 1) * UNITS] = jnp.where(
+            crossed, counts[:, 1, :], counts[:, 0, :]
         )
     source, target = rows_of((LANES, LANES)), lanes_of((LANES, LANES))
     wide = LANES // ITEMS
-    spectrum = place_ref[0] // S % 2
     added = (source // wide == target // wide) & (source % wide // K == 4 + spectrum)
     counts = jnp.dot(
         seen[...].astype(jnp.bfloat16),
@@ -402,8 +396,7 @@
         scales[pl.ds(item, PERIODS * UNITS, stride=ITEMS), :] = jnp.broadcast_to(
             scale[:, item * wide : item * wide + 1], (PERIODS * UNITS, LANES)
         )
-    alone = order_ref[place_ref[0] % S] == place_ref[0] // S
-    left = jnp.where(alone, 1.0, 0.0)
+    left = jnp.where(mine == partner, 1.0, 0.0)
     first = sums[pl.ds(0, PERIODS * CB, stride=2), :]
     second = sums[pl.ds(1, PERIODS * CB, stride=2), :]
     values = jnp.concatenate(

time: 72.6 us -> 72.1 us (level)
  no operation moved by 1% of the time
where the time goes in v7:
time: 72.1 us; the launch traced here: 71.9 us
  blocking collectives  62.4 us (87%)
  Pallas kernels  9.41 us (13%)
    all_to_all x1, blocking collectives, per_device(): lax.all_to_all(rows, everyone, split_axis=0, concat_axis=0, tiled=True)  34 us
    all_to_all x1, blocking collectives, per_device(): lax.all_to_all(chunks, plane, split_axis=0, concat_axis=0, tiled=True)  28.4 us
    pallas_call x1, Pallas kernels, correlated(): pl.pallas_call(correlate_kernel, in_specs=[pl.BlockSpec(memory_space=pltp...  4.19 us
    pallas_call x1, Pallas kernels, rotated_chunks(): pl.pallas_call(rotate_kernel, in_specs=[pl.BlockSpec(memory_space=pltpu.S...  2.74 us
    pallas_call x1, Pallas kernels, fringed(): pl.pallas_call(fringe_kernel, in_specs=[pl.BlockSpec(memory_space=pltpu.S...  2.48 us

profile of v7, /device:TPU:1, one launch (start us, length us, event | category | flops | bytes accessed | tf_op | source)
XLA Modules:
  0.0 71.9 jit_solution(16225800434382496315)
XLA Ops:
  0.0 2.7 %rotate.1 = bf16[64,33,2,128]{3,2,1,0:T(2,128)(2,1)S(1)} custom-call(s32[1]{0:T(128)} %bitcast.place_ref, s32[2,4,8]{2,1,0:T(4,128)} %bitcast.7, f32[3,64]{1,0:T(4,128)} %bitcast.8, s32[2,8,4,32]{3,2,1,0:T(4,128)} %flags_hbm.1, bf16[2,8,4,2,4096]{4,3,2,1,0:T(2,128)(2,1)} %x_hbm.1), custom_call_target="tpu_custom_call" | custom-call | tf_op jit(solution)/shard_map/rotate/pallas_call | solution.py:165
  2.8 0.0 copy-start.4
  2.8 28.4 %all_to_all.10 = bf16[64,33,2,128]{3,2,1,0:T(2,128)(2,1)S(1)} all-to-all(bf16[64,33,2,128]{3,2,1,0:T(2,128)(2,1)S(1)} %rotate.1), channel_id=1, replica_groups=mesh['stn'=8,'quarter'=4,'unit'=8] {'stn','unit'}, dimensions={0} | all-to-all | bytes 2162688 | tf_op jit(solution)/shard_map/all_to_all | solution.py:479
  31.2 0.0 copy-done.4
  31.2 4.2 %correlate.1 = bf16[256,5,2,128]{3,2,1,0:T(2,128)(2,1)S(1)} custom-call(s32[16]{0:T(128)S(1)} %copy-done.4, bf16[8,8,33,2,128]{4,3,2,1,0:T(2,128)(2,1)S(1)} %bitcast.5), custom_call_target="tpu_custom_call" | custom-call | tf_op jit(solution)/shard_map/correlate/pallas_call | solution.py:326
  35.4 0.0 copy-start
  35.4 0.0 copy-start.1
  35.4 0.0 copy-start.2
  35.4 0.0 copy-start.3
  35.4 34.0 %all_to_all.11 = bf16[256,5,2,128]{3,2,1,0:T(2,128)(2,1)S(1)} all-to-all(bf16[256,5,2,128]{3,2,1,0:T(2,128)(2,1)S(1)} %correlate.1), channel_id=1, replica_groups=mesh['stn'=8,'quarter'=4,'unit'=8] {'stn','quarter','unit'}, dimensions={0} | all-to-all | bytes 1310720 | tf_op jit(solution)/shard_map/all_to_all | solution.py:481
  69.4 0.0 copy-done
  69.4 0.0 copy-done.1
  69.4 0.0 copy-done.2
  69.4 0.0 copy-done.3
  69.4 2.5 %fringe.1 = f32[2,1,8,256]{3,2,1,0:T(8,128)} custom-call(s32[1]{0:T(128)} %bitcast.place_ref, s32[16]{0:T(128)S(1)} %copy-done.4, bf16[8,4,8,5,2,128]{5,4,3,2,1,0:T(2,128)(2,1)S(1)} %bitcast.6, bf16[384,256]{1,0:T(8,128)(2,1)S(1)} %copy-done, f32[2,32,128]{2,1,0:T(8,128)S(1)} %copy-done.2, f32[2,8,8]{2,1,0:T(8,128)S(1)} %copy-done.3, f32[128,128]{1,0:T(8,128)S(1)} %copy-done.1), custom_call_target="tpu_custom_call" | custom-call | tf_op jit(solution)/shard_map/fringe/pallas_call | solution.py:452
Async XLA Ops:
  2.8 28.4 %copy-start.4 = (s32[16]{0:T(128)S(1)}, s32[16]{0:T(128)}, u32[]{:S(2)}) copy-start(s32[16]{0:T(128)} %order_ref.3) | copy-start | bytes 196
  35.4 34.0 %copy-start = (bf16[384,256]{1,0:T(8,128)(2,1)S(1)}, bf16[384,256]{1,0:T(8,128)(2,1)}, u32[]{:S(2)}) copy-start(bf16[384,256]{1,0:T(8,128)(2,1)} %constant.24.clone.fine_ref) | copy-start | bytes 589828
  35.4 34.0 %copy-start.1 = (f32[128,128]{1,0:T(8,128)S(1)}, f32[128,128]{1,0:T(8,128)}, u32[]{:S(2)}) copy-start(f32[128,128]{1,0:T(8,128)} %constant.27.clone.flip_ref) | copy-start | bytes 196612
  35.4 34.0 %copy-start.2 = (f32[2,32,128]{2,1,0:T(8,128)S(1)}, f32[2,32,128]{2,1,0:T(8,128)}, u32[]{:S(2)}) copy-start(f32[2,32,128]{2,1,0:T(8,128)} %constant.25.clone.coarse_ref) | copy-start | bytes 98308
  35.4 34.0 %copy-start.3 = (f32[2,8,8]{2,1,0:T(8,128)S(1)}, f32[2,8,8]{2,1,0:T(8,128)}, u32[]{:S(2)}) copy-start(f32[2,8,8]{2,1,0:T(8,128)} %constant.26.clone.period_ref) | copy-start | bytes 1540

commit v8 on v7

--- a/solution.py
+++ b/solution.py
@@ -27,6 +27,8 @@
 LANES = 128
 HALF = LAGS // 2
 HIGHEST = lax.Precision.HIGHEST
+WIDE = LANES // ITEMS
+TERMS = WIDE - 1
 COSINE = [(-1) ** n * (2 * math.pi) ** (2 * n) / math.factorial(2 * n) for n in range(10)]
 SINE = [(-1) ** n * (2 * math.pi) ** (2 * n + 1) / math.factorial(2 * n + 1) for n in range(10)]
 
@@ -217,7 +219,17 @@
 PAIRS = [(n, m) for n in range(STN) for m in range(n, STN)]
 
 
-def correlate_kernel(order_ref, y_ref, out_ref, mine_ref, crossed_ref, tiles, place_ref):
+def three_passes(values, table):
+    high = values.astype(jnp.bfloat16)
+    low = (values - high.astype(jnp.float32)).astype(jnp.bfloat16)
+    return jnp.dot(
+        jnp.concatenate([high, low, high], axis=1),
+        table,
+        preferred_element_type=jnp.float32,
+    )
+
+
+def correlate_kernel(order_ref, y_ref, terms_ref, out_ref, mine_ref, crossed_ref, tiles, place_ref):
     for j in range(S):
         place_ref[order_ref[j]] = j
     row = rows_of((8, LANES))
@@ -231,22 +243,26 @@
             values = [sums[0] + sums[2], sums[0] - sums[1]]
         values += [sums[-3] + sums[-1], sums[-3] - sums[-2]]
         tile = group_sums(values, 4)
-        if n == m:
-            left = tile - tile.astype(jnp.bfloat16).astype(jnp.float32)
-            tile = jnp.where(row % 4 == 1, pltpu.roll(left, 1, 0), tile)
-        tiles[PAIRS.index((n, m)), item] = tile
+        tiles[item, pl.ds(PAIRS.index((n, m)) * 8, 8)] = tile
 
     weights = [
         y_ref[n, :, TILES - 1].astype(jnp.float32)[:, 0, :] for n in range(STN)
     ]
     swapped = [pltpu.roll(weight, K, 1) for weight in weights]
-    products = []
+    counts = []
     for n, m in PAIRS:
-        products += [weights[n] * weights[m], weights[n] * swapped[m]]
-    counts = [
-        group_sums(products[i : i + 8], 8).astype(jnp.bfloat16)
-        for i in range(0, len(products), 8)
-    ]
+        same, other = weights[n] * weights[m], weights[n] * swapped[m]
+        counts.append(group_sums([same, zero, other, zero] * 2, 8))
+    counts = jnp.concatenate(counts)
+    at = rows_of(counts.shape) % 8 // 4
+    counts = jnp.where(lanes_of(counts.shape) % WIDE // K == 4 + at, counts, 0.0)
+    i, j = rows_of((LANES, LANES)), lanes_of((LANES, LANES))
+    last = jnp.where(j == i // WIDE * WIDE + TERMS, 1.0, 0.0)
+    counts = jnp.dot(
+        counts.astype(jnp.bfloat16),
+        last.astype(jnp.bfloat16),
+        preferred_element_type=jnp.float32,
+    )
 
     def one_item(item, carry):
         for n in range(STN):
@@ -294,32 +310,19 @@
 
     lax.fori_loop(0, ITEMS, one_item, 0)
     conjugate = jnp.where(row % 2 == 0, 1.0, -1.0)
-    upper, inner = row < 4, row % 4 < 2
+    total = counts
+    for item in range(ITEMS):
+        total = total + three_passes(tiles[item], terms_ref[item])
     for number, (n, m) in enumerate(PAIRS):
-        t = [tiles[number, item] for item in range(ITEMS)]
-        halves = (
-            [jnp.where(upper, t[i], pltpu.roll(t[i + 2], 4, 0)) for i in range(2)],
-            [jnp.where(upper, pltpu.roll(t[i], 4, 0), t[i + 2]) for i in range(2)],
-        )
-        for h, (x, y) in enumerate(halves):
-            same = jnp.where(inner, x, pltpu.roll(y, 2, 0))
-            crossed = jnp.where(inner, pltpu.roll(x, 6, 0), y)
-            a = 2 * n + h
-            for b, value in ((2 * m + h, same), (2 * m + 1 - h, crossed)):
-                out_ref[a * S + place_ref[b], 0:ITEMS] = value.astype(
-                    jnp.bfloat16
-                ).reshape(ITEMS, 2, LANES)
-                if n != m:
-                    out_ref[b * S + place_ref[a], 0:ITEMS] = (
-                        (value * conjugate).astype(jnp.bfloat16).reshape(ITEMS, 2, LANES)
-                    )
-        pair_of_rows = counts[number // 4][number % 4 * 2 : number % 4 * 2 + 2]
-        for h in range(2):
-            for other in range(2):
-                a, b = 2 * n + h, 2 * m + other
-                out_ref[a * S + place_ref[b], ITEMS] = pair_of_rows
-                if n != m:
-                    out_ref[b * S + place_ref[a], ITEMS] = pair_of_rows
+        value = total[number * 8 : number * 8 + 8]
+        other = value * conjugate
+        for pair in range(4):
+            h = pair // 2
+            a, b = 2 * n + h, 2 * m + (h if pair % 2 == 0 else 1 - h)
+            at = slice(2 * pair, 2 * pair + 2)
+            out_ref[a * S + place_ref[b]] = value[at]
+            if n != m:
+                out_ref[b * S + place_ref[a]] = other[at]
 
 
 def correlated(order, arrived):
@@ -328,93 +331,89 @@
         in_specs=[
             pl.BlockSpec(memory_space=pltpu.SMEM),
             pl.BlockSpec(memory_space=pltpu.VMEM),
+            pl.BlockSpec(memory_space=pltpu.VMEM),
         ],
         out_specs=pl.BlockSpec(memory_space=pltpu.VMEM),
-        out_shape=jax.ShapeDtypeStruct((S * S, ITEMS + 1, 2, LANES), jnp.bfloat16),
+        out_shape=jax.ShapeDtypeStruct((S * S, 2, LANES), jnp.float32),
         scratch_shapes=[
             pltpu.VMEM((STN, 2, UNITS, 8, LANES), jnp.float32),
             pltpu.VMEM((STN, 2, UNITS, 8, LANES), jnp.float32),
-            pltpu.VMEM((len(PAIRS), ITEMS, 8, LANES), jnp.float32),
+            pltpu.VMEM((ITEMS, len(PAIRS) * 8, LANES), jnp.float32),
             pltpu.SMEM((S,), jnp.int32),
         ],
         compiler_params=pltpu.CompilerParams(vmem_limit_bytes=32 * 2**20),
         name="correlate",
-    )(order, arrived.reshape(STN, UNITS, TILES, 2, LANES))
+    )(order, arrived.reshape(STN, UNITS, TILES, 2, LANES), term_tables())
+
+
+def split_table(table):
+    high = table.astype(np.float32).astype(ml_dtypes.bfloat16)
+    low = (table - high.astype(np.float64)).astype(np.float32).astype(ml_dtypes.bfloat16)
+    return np.concatenate([high, high, low])
+
+
+CENTRE = (LANES - 1) / 2
+
+
+def term_tables():
+    x = (np.arange(LANES) - CENTRE) / CENTRE
+    table = np.cos(np.arccos(x)[:, None] * np.arange(TERMS))
+    placed = np.zeros((ITEMS, LANES, LANES))
+    for item in range(ITEMS):
+        placed[item, :, item * WIDE : item * WIDE + TERMS] = table
+    return np.stack([split_table(each) for each in placed])
 
 
 def fringe_tables():
     lag = np.arange(1, HALF + 1)
-    fine = 2.0 * np.pi * ((np.arange(LANES)[:, None] * lag) % C) / C
-    coarse = 2.0 * np.pi * ((np.arange(CB)[:, None] * lag) % CB) / CB
+    z = 2.0 * np.pi * CENTRE * lag / C
+    points = 2.0 * np.pi * np.arange(256) / 256
+    order = np.arange(TERMS)
+    bessel = np.cos(
+        order[:, None, None] * points - z[:, None] * np.sin(points)
+    ).mean(axis=2)
+    series = np.where(order == 0, 1, 2)[:, None] * np.array([1, -1j, -1, 1j])[order % 4][:, None] * bessel
+    fine = np.zeros((LANES, HALF), np.complex128)
+    for item in range(ITEMS):
+        turned = np.exp(-2j * np.pi * ((CENTRE + item * LANES) * lag % C) / C)
+        fine[item * WIDE : item * WIDE + TERMS] = series * turned
+    unit = 2.0 * np.pi * ((np.arange(UNITS)[:, None] * lag) % UNITS) / UNITS
     period = 2.0 * np.pi * ((np.arange(PERIODS)[:, None] * np.arange(PERIODS)) % PERIODS)
     period = period / PERIODS
     factor = 1.0 / math.sqrt(PERIODS * C)
-    flip = np.eye(HALF)[::-1]
-    fine = np.concatenate([np.cos(fine), np.sin(fine)], axis=1).astype(np.float32)
-    high = fine.astype(ml_dtypes.bfloat16)
-    low = (fine - high.astype(np.float32)).astype(ml_dtypes.bfloat16)
-    return [np.concatenate([high, high, low])] + [
+    return [split_table(np.concatenate([fine.real, -fine.imag], axis=1))] + [
         np.ascontiguousarray(table, np.float32)
         for table in (
-            np.stack([np.cos(coarse), np.sin(coarse)]),
+            np.stack([np.cos(unit), np.sin(unit)]),
             np.stack([np.cos(period), np.sin(period)]) * factor,
-            flip,
+            np.eye(HALF)[::-1],
         )
     ]
 
 
-def fringe_kernel(
-    place_ref, order_ref, z_ref, fine_ref, coarse_ref, period_ref, flip_ref, out_ref, sums, scales, seen
-):
-    mine, partner = place_ref[0] // S, order_ref[place_ref[0] % S]
-    crossed = mine % 2 != partner % 2
-    spectrum = jnp.where(mine // 2 <= partner // 2, mine % 2, partner % 2)
-    for p in range(PERIODS):
-        for u in range(UNITS):
-            parts = [
-                z_ref[p, quarter, u, 0:ITEMS].reshape(2 * ITEMS, LANES).astype(jnp.float32)
-                for quarter in range(QUARTERS)
-            ]
-            at = (p * UNITS + u) * 2 * ITEMS
-            sums[at : at + 2 * ITEMS] = (parts[0] + parts[1]) + (parts[2] + parts[3])
-        counts = sum(
-            z_ref[p, quarter, :, ITEMS].astype(jnp.float32) for quarter in range(QUARTERS)
-        )
-        seen[p * UNITS : (p + 1) * UNITS] = jnp.where(
-            crossed, counts[:, 1, :], counts[:, 0, :]
-        )
-    source, target = rows_of((LANES, LANES)), lanes_of((LANES, LANES))
-    wide = LANES // ITEMS
-    added = (source // wide == target // wide) & (source % wide // K == 4 + spectrum)
+def fringe_kernel(z_ref, fine_ref, coarse_ref, period_ref, flip_ref, out_ref):
+    sums = [
+        sum(z_ref[p, quarter] for quarter in range(QUARTERS)) for p in range(PERIODS)
+    ]
+    real = jnp.concatenate([each[:, 0, :] for each in sums])
+    imag = jnp.concatenate([each[:, 1, :] for each in sums])
+    i, j = rows_of((LANES, LANES)), lanes_of((LANES, LANES))
+    spread = jnp.where(i == j // WIDE * WIDE + TERMS, 1.0, 0.0).astype(jnp.bfloat16)
     counts = jnp.dot(
-        seen[...].astype(jnp.bfloat16),
-        jnp.where(added, 1.0, 0.0).astype(jnp.bfloat16),
+        jnp.where(lanes_of(real.shape) % WIDE == TERMS, real, 0.0).astype(jnp.bfloat16),
+        spread,
         preferred_element_type=jnp.float32,
     )
     scale = 1.0 / jnp.sqrt(jnp.maximum(counts, 1.0))
-    for item in range(ITEMS):
-        scales[pl.ds(item, PERIODS * UNITS, stride=ITEMS), :] = jnp.broadcast_to(
-            scale[:, item * wide : item * wide + 1], (PERIODS * UNITS, LANES)
-        )
-    left = jnp.where(mine == partner, 1.0, 0.0)
-    first = sums[pl.ds(0, PERIODS * CB, stride=2), :]
-    second = sums[pl.ds(1, PERIODS * CB, stride=2), :]
-    values = jnp.concatenate(
-        [(first + left * second) * scales[...], (second * (1.0 - left)) * scales[...]]
-    )
-    high = values.astype(jnp.bfloat16)
-    low = (values - high.astype(jnp.float32)).astype(jnp.bfloat16)
-    both = jnp.dot(
-        jnp.concatenate([high, low, high], axis=1),
-        fine_ref[...],
-        preferred_element_type=jnp.float32,
-    )
-    re, im = both[: PERIODS * CB], both[PERIODS * CB :]
+    both = three_passes(
+        jnp.concatenate([real * scale, imag * scale]), fine_ref[...]
+    )
+    re, im = both[: PERIODS * UNITS], both[PERIODS * UNITS :]
     parts = [[], [], [], []]
     for p in range(PERIODS):
         sums = [jnp.zeros((8, LANES), jnp.float32)] * 4
-        for g in range(CB // 8):
-            at = slice(p * CB + g * 8, p * CB + g * 8 + 8)
+        for g in range(1):
+            at = slice(p * UNITS, p * UNITS + UNITS)
             re_cos, re_sin = re[at, :HALF], re[at, HALF:]
             im_cos, im_sin = im[at, :HALF], im[at, HALF:]
             cosine = coarse_ref[0, g * 8 : g * 8 + 8, :]
@@ -448,26 +447,15 @@
     out_ref[1, 0] = turn(cosine, imag) - turn(sine, real)
 
 
-def fringed(place, order, owned):
+def fringed(owned):
     return pl.pallas_call(
         fringe_kernel,
-        in_specs=[pl.BlockSpec(memory_space=pltpu.SMEM)] * 2
-        + [pl.BlockSpec(memory_space=pltpu.VMEM)] * 5,
+        in_specs=[pl.BlockSpec(memory_space=pltpu.VMEM)] * 5,
         out_specs=pl.BlockSpec(memory_space=pltpu.VMEM),
         out_shape=jax.ShapeDtypeStruct((2, 1, PERIODS, LAGS), jnp.float32),
-        scratch_shapes=[
-            pltpu.VMEM((PERIODS * CB * 2, LANES), jnp.float32),
-            pltpu.VMEM((PERIODS * CB, LANES), jnp.float32),
-            pltpu.VMEM((PERIODS * UNITS, LANES), jnp.float32),
-        ],
         compiler_params=pltpu.CompilerParams(vmem_limit_bytes=32 * 2**20),
         name="fringe",
-    )(
-        place,
-        order,
-        owned.reshape(PERIODS, QUARTERS, UNITS, ITEMS + 1, 2, LANES),
-        *fringe_tables(),
-    )
+    )(owned.reshape(PERIODS, QUARTERS, UNITS, 2, LANES), *fringe_tables())
 
 
 def per_device(spectra, flags, poly_index, delay_model, partner_order):
@@ -479,7 +467,7 @@
     arrived = lax.all_to_all(chunks, plane, split_axis=0, concat_axis=0, tiled=True)
     rows = correlated(partner_order, arrived)
     owned = lax.all_to_all(rows, everyone, split_axis=0, concat_axis=0, tiled=True)
-    return fringed(place, partner_order, owned)
+    return fringed(owned)
 
 
 def solution(mesh):

time: 72.1 us -> 63.1 us (0.88)
  blocking collectives: 62.4 us -> 54.4 us
  Pallas kernels: 9.41 us -> 8.42 us
    all_to_all x1, blocking collectives: 34 us -> 25.8 us  [per_device(): lax.all_to_all(rows, everyone, split_axis=0, concat_axis=0, tiled=True)]
    pallas_call x1, Pallas kernels: 2.48 us -> 1.4 us  [fringed(): pl.pallas_call(fringe_kernel, in_specs=[pl.BlockSpec(memory_space=pltpu.V...]
where the time goes in v8:
time: 63.1 us; the launch traced here: 62.9 us
  blocking collectives  54.4 us (86%)
  Pallas kernels  8.42 us (13%)
    all_to_all x1, blocking collectives, per_device(): lax.all_to_all(chunks, plane, split_axis=0, concat_axis=0, tiled=True)  28.6 us
    all_to_all x1, blocking collectives, per_device(): lax.all_to_all(rows, everyone, split_axis=0, concat_axis=0, tiled=True)  25.8 us
    pallas_call x1, Pallas kernels, correlated(): pl.pallas_call(correlate_kernel, in_specs=[pl.BlockSpec(memory_space=pltp...  4.28 us
    pallas_call x1, Pallas kernels, rotated_chunks(): pl.pallas_call(rotate_kernel, in_specs=[pl.BlockSpec(memory_space=pltpu.S...  2.74 us
    pallas_call x1, Pallas kernels, fringed(): pl.pallas_call(fringe_kernel, in_specs=[pl.BlockSpec(memory_space=pltpu.V...  1.4 us

profile of v8, /device:TPU:1, one launch (start us, length us, event | category | flops | bytes accessed | tf_op | source)
XLA Modules:
  0.0 62.9 jit_solution(2873515908630923827)
XLA Ops:
  0.0 2.7 %rotate.1 = bf16[64,33,2,128]{3,2,1,0:T(2,128)(2,1)S(1)} custom-call(s32[1]{0:T(128)} %bitcast.place_ref, s32[2,4,8]{2,1,0:T(4,128)} %bitcast.7, f32[3,64]{1,0:T(4,128)} %bitcast.8, s32[2,8,4,32]{3,2,1,0:T(4,128)} %flags_hbm.1, bf16[2,8,4,2,4096]{4,3,2,1,0:T(2,128)(2,1)} %x_hbm.1), custom_call_target="tpu_custom_call" | custom-call | tf_op jit(solution)/shard_map/rotate/pallas_call | solution.py:167
  2.8 0.0 copy-start
  2.8 0.0 copy-start.5
  2.8 28.6 %all_to_all.10 = bf16[64,33,2,128]{3,2,1,0:T(2,128)(2,1)S(1)} all-to-all(bf16[64,33,2,128]{3,2,1,0:T(2,128)(2,1)S(1)} %rotate.1), channel_id=1, replica_groups=mesh['stn'=8,'quarter'=4,'unit'=8] {'stn','unit'}, dimensions={0} | all-to-all | bytes 2162688 | tf_op jit(solution)/shard_map/all_to_all | solution.py:467
  31.3 0.0 copy-done
  31.3 0.0 copy-done.5
  31.3 0.0 copy-start.1
  31.3 0.0 copy-start.2
  31.4 0.0 copy-start.3
  31.4 0.0 copy-start.4
  31.4 4.3 %correlate.1 = f32[256,2,128]{2,1,0:T(2,128)S(1)} custom-call(s32[16]{0:T(128)S(1)} %copy-done.5, bf16[8,8,33,2,128]{4,3,2,1,0:T(2,128)(2,1)S(1)} %bitcast.5, bf16[4,384,128]{2,1,0:T(8,128)(2,1)S(1)} %copy-done), custom_call_target="tpu_custom_call" | custom-call | tf_op jit(solution)/shard_map/correlate/pallas_call | solution.py:329
  35.7 25.8 %all_to_all.11 = f32[256,2,128]{2,1,0:T(2,128)S(1)} all-to-all(f32[256,2,128]{2,1,0:T(2,128)S(1)} %correlate.1), channel_id=1, replica_groups=mesh['stn'=8,'quarter'=4,'unit'=8] {'stn','quarter','unit'}, dimensions={0} | all-to-all | bytes 524288 | tf_op jit(solution)/shard_map/all_to_all | solution.py:469
  61.5 0.0 copy-done.1
  61.5 0.0 copy-done.2
  61.5 0.0 copy-done.3
  61.5 0.0 copy-done.4
  61.5 1.4 %fringe.1 = f32[2,1,8,256]{3,2,1,0:T(8,128)} custom-call(f32[8,4,8,2,128]{4,3,2,1,0:T(2,128)S(1)} %bitcast.6, bf16[384,256]{1,0:T(8,128)(2,1)S(1)} %copy-done.1, f32[2,8,128]{2,1,0:T(8,128)S(1)} %copy-done.4, f32[2,8,8]{2,1,0:T(8,128)S(1)} %copy-done.3, f32[128,128]{1,0:T(8,128)S(1)} %copy-done.2), custom_call_target="tpu_custom_call" | custom-call | tf_op jit(solution)/shard_map/fringe/pallas_call | solution.py:451
Async XLA Ops:
  2.8 28.6 %copy-start = (bf16[4,384,128]{2,1,0:T(8,128)(2,1)S(1)}, bf16[4,384,128]{2,1,0:T(8,128)(2,1)}, u32[]{:S(2)}) copy-start(bf16[4,384,128]{2,1,0:T(8,128)(2,1)} %constant.26.clone.terms_ref) | copy-start | bytes 1179652
  2.8 28.6 %copy-start.5 = (s32[16]{0:T(128)S(1)}, s32[16]{0:T(128)}, u32[]{:S(2)}) copy-start(s32[16]{0:T(128)} %order_ref.1) | copy-start | bytes 196
  31.3 30.1 %copy-start.1 = (bf16[384,256]{1,0:T(8,128)(2,1)S(1)}, bf16[384,256]{1,0:T(8,128)(2,1)}, u32[]{:S(2)}) copy-start(bf16[384,256]{1,0:T(8,128)(2,1)} %constant.27.clone.fine_ref) | copy-start | bytes 589828
  31.3 30.1 %copy-start.2 = (f32[128,128]{1,0:T(8,128)S(1)}, f32[128,128]{1,0:T(8,128)}, u32[]{:S(2)}) copy-start(f32[128,128]{1,0:T(8,128)} %constant.30.clone.flip_ref) | copy-start | bytes 196612
  31.4 30.1 %copy-start.3 = (f32[2,8,8]{2,1,0:T(8,128)S(1)}, f32[2,8,8]{2,1,0:T(8,128)}, u32[]{:S(2)}) copy-start(f32[2,8,8]{2,1,0:T(8,128)} %constant.29.clone.period_ref) | copy-start | bytes 1540
  31.4 30.1 %copy-start.4 = (f32[2,8,128]{2,1,0:T(8,128)S(1)}, f32[2,8,128]{2,1,0:T(8,128)}, u32[]{:S(2)}) copy-start(f32[2,8,128]{2,1,0:T(8,128)} %constant.28.clone.coarse_ref) | copy-start | bytes 24580

commit v9 on v8

--- a/solution.py
+++ b/solution.py
@@ -315,7 +315,11 @@
         total = total + three_passes(tiles[item], terms_ref[item])
     for number, (n, m) in enumerate(PAIRS):
         value = total[number * 8 : number * 8 + 8]
-        other = value * conjugate
+        if n == m:
+            left = value - value.astype(jnp.bfloat16).astype(jnp.float32)
+            value = jnp.where(row % 4 == 1, pltpu.roll(left, 1, 0), value)
+        other = (value * conjugate).astype(jnp.bfloat16)
+        value = value.astype(jnp.bfloat16)
         for pair in range(4):
             h = pair // 2
             a, b = 2 * n + h, 2 * m + (h if pair % 2 == 0 else 1 - h)
@@ -334,7 +338,7 @@
             pl.BlockSpec(memory_space=pltpu.VMEM),
         ],
         out_specs=pl.BlockSpec(memory_space=pltpu.VMEM),
-        out_shape=jax.ShapeDtypeStruct((S * S, 2, LANES), jnp.float32),
+        out_shape=jax.ShapeDtypeStruct((S * S, 2, LANES), jnp.bfloat16),
         scratch_shapes=[
             pltpu.VMEM((STN, 2, UNITS, 8, LANES), jnp.float32),
             pltpu.VMEM((STN, 2, UNITS, 8, LANES), jnp.float32),
@@ -391,12 +395,16 @@
     ]
 
 
-def fringe_kernel(z_ref, fine_ref, coarse_ref, period_ref, flip_ref, out_ref):
+def fringe_kernel(place_ref, order_ref, z_ref, fine_ref, coarse_ref, period_ref, flip_ref, out_ref):
     sums = [
-        sum(z_ref[p, quarter] for quarter in range(QUARTERS)) for p in range(PERIODS)
+        sum(z_ref[p, quarter].astype(jnp.float32) for quarter in range(QUARTERS))
+        for p in range(PERIODS)
     ]
     real = jnp.concatenate([each[:, 0, :] for each in sums])
     imag = jnp.concatenate([each[:, 1, :] for each in sums])
+    alone = order_ref[place_ref[0] % S] == place_ref[0] // S
+    left = jnp.where(alone, 1.0, 0.0)
+    real, imag = real + left * imag, (1.0 - left) * imag
     i, j = rows_of((LANES, LANES)), lanes_of((LANES, LANES))
     spread = jnp.where(i == j // WIDE * WIDE + TERMS, 1.0, 0.0).astype(jnp.bfloat16)
     counts = jnp.dot(
@@ -447,15 +455,21 @@
     out_ref[1, 0] = turn(cosine, imag) - turn(sine, real)
 
 
-def fringed(owned):
+def fringed(place, order, owned):
     return pl.pallas_call(
         fringe_kernel,
-        in_specs=[pl.BlockSpec(memory_space=pltpu.VMEM)] * 5,
+        in_specs=[pl.BlockSpec(memory_space=pltpu.SMEM)] * 2
+        + [pl.BlockSpec(memory_space=pltpu.VMEM)] * 5,
         out_specs=pl.BlockSpec(memory_space=pltpu.VMEM),
         out_shape=jax.ShapeDtypeStruct((2, 1, PERIODS, LAGS), jnp.float32),
         compiler_params=pltpu.CompilerParams(vmem_limit_bytes=32 * 2**20),
         name="fringe",
-    )(owned.reshape(PERIODS, QUARTERS, UNITS, 2, LANES), *fringe_tables())
+    )(
+        place,
+        order,
+        owned.reshape(PERIODS, QUARTERS, UNITS, 2, LANES),
+        *fringe_tables(),
+    )
 
 
 def per_device(spectra, flags, poly_index, delay_model, partner_order):
@@ -467,7 +481,7 @@
     arrived = lax.all_to_all(chunks, plane, split_axis=0, concat_axis=0, tiled=True)
     rows = correlated(partner_order, arrived)
     owned = lax.all_to_all(rows, everyone, split_axis=0, concat_axis=0, tiled=True)
-    return fringed(owned)
+    return fringed(place, partner_order, owned)
 
 
 def solution(mesh):

time: 63.1 us -> 61 us (0.967)
  blocking collectives: 54.4 us -> 51.8 us
    all_to_all x1, blocking collectives: 25.8 us -> 23.2 us  [per_device(): lax.all_to_all(rows, everyone, split_axis=0, concat_axis=0, tiled=True)]
where the time goes in v9:
time: 61 us; the launch traced here: 60.9 us
  blocking collectives  51.8 us (85%)
  Pallas kernels  9.03 us (15%)
    all_to_all x1, blocking collectives, per_device(): lax.all_to_all(chunks, plane, split_axis=0, concat_axis=0, tiled=True)  28.6 us
    all_to_all x1, blocking collectives, per_device(): lax.all_to_all(rows, everyone, split_axis=0, concat_axis=0, tiled=True)  23.2 us
    pallas_call x1, Pallas kernels, correlated(): pl.pallas_call(correlate_kernel, in_specs=[pl.BlockSpec(memory_space=pltp...  4.29 us
    pallas_call x1, Pallas kernels, rotated_chunks(): pl.pallas_call(rotate_kernel, in_specs=[pl.BlockSpec(memory_space=pltpu.S...  2.74 us
    pallas_call x1, Pallas kernels, fringed(): pl.pallas_call(fringe_kernel, in_specs=[pl.BlockSpec(memory_space=pltpu.S...  2 us

profile of v9, /device:TPU:1, one launch (start us, length us, event | category | flops | bytes accessed | tf_op | source)
XLA Modules:
  0.0 60.9 jit_solution(14973469866931008137)
XLA Ops:
  0.0 2.7 %rotate.1 = bf16[64,33,2,128]{3,2,1,0:T(2,128)(2,1)S(1)} custom-call(s32[1]{0:T(128)} %bitcast.place_ref, s32[2,4,8]{2,1,0:T(4,128)} %bitcast.7, f32[3,64]{1,0:T(4,128)} %bitcast.8, s32[2,8,4,32]{3,2,1,0:T(4,128)} %flags_hbm.1, bf16[2,8,4,2,4096]{4,3,2,1,0:T(2,128)(2,1)} %x_hbm.1), custom_call_target="tpu_custom_call" | custom-call | tf_op jit(solution)/shard_map/rotate/pallas_call | solution.py:167
  2.8 0.0 copy-start
  2.8 0.0 copy-start.5
  2.8 28.6 %all_to_all.10 = bf16[64,33,2,128]{3,2,1,0:T(2,128)(2,1)S(1)} all-to-all(bf16[64,33,2,128]{3,2,1,0:T(2,128)(2,1)S(1)} %rotate.1), channel_id=1, replica_groups=mesh['stn'=8,'quarter'=4,'unit'=8] {'stn','unit'}, dimensions={0} | all-to-all | bytes 2162688 | tf_op jit(solution)/shard_map/all_to_all | solution.py:481
  31.3 0.0 copy-start.1
  31.3 0.0 copy-start.2
  31.3 0.0 copy-start.3
  31.3 0.0 copy-start.4
  31.4 0.0 copy-done
  31.4 0.0 copy-done.5
  31.4 4.3 %correlate.1 = bf16[256,2,128]{2,1,0:T(2,128)(2,1)S(1)} custom-call(s32[16]{0:T(128)S(1)} %copy-done.5, bf16[8,8,33,2,128]{4,3,2,1,0:T(2,128)(2,1)S(1)} %bitcast.5, bf16[4,384,128]{2,1,0:T(8,128)(2,1)S(1)} %copy-done), custom_call_target="tpu_custom_call" | custom-call | tf_op jit(solution)/shard_map/correlate/pallas_call | solution.py:333
  35.7 23.2 %all_to_all.11 = bf16[256,2,128]{2,1,0:T(2,128)(2,1)S(1)} all-to-all(bf16[256,2,128]{2,1,0:T(2,128)(2,1)S(1)} %correlate.1), channel_id=1, replica_groups=mesh['stn'=8,'quarter'=4,'unit'=8] {'stn','quarter','unit'}, dimensions={0} | all-to-all | bytes 262144 | tf_op jit(solution)/shard_map/all_to_all | solution.py:483
  58.9 0.0 copy-done.1
  58.9 0.0 copy-done.2
  58.9 0.0 copy-done.3
  58.9 0.0 copy-done.4
  58.9 2.0 %fringe.1 = f32[2,1,8,256]{3,2,1,0:T(8,128)} custom-call(s32[1]{0:T(128)} %bitcast.place_ref, s32[16]{0:T(128)S(1)} %copy-done.5, bf16[8,4,8,2,128]{4,3,2,1,0:T(2,128)(2,1)S(1)} %bitcast.6, bf16[384,256]{1,0:T(8,128)(2,1)S(1)} %copy-done.1, f32[2,8,128]{2,1,0:T(8,128)S(1)} %copy-done.4, f32[2,8,8]{2,1,0:T(8,128)S(1)} %copy-done.3, f32[128,128]{1,0:T(8,128)S(1)} %copy-done.2), custom_call_target="tpu_custom_call" | custom-call | tf_op jit(solution)/shard_map/fringe/pallas_call | solution.py:459
Async XLA Ops:
  2.8 28.6 %copy-start = (bf16[4,384,128]{2,1,0:T(8,128)(2,1)S(1)}, bf16[4,384,128]{2,1,0:T(8,128)(2,1)}, u32[]{:S(2)}) copy-start(bf16[4,384,128]{2,1,0:T(8,128)(2,1)} %constant.26.clone.terms_ref) | copy-start | bytes 1179652
  2.8 28.6 %copy-start.5 = (s32[16]{0:T(128)S(1)}, s32[16]{0:T(128)}, u32[]{:S(2)}) copy-start(s32[16]{0:T(128)} %order_ref.3) | copy-start | bytes 196
  31.3 27.5 %copy-start.1 = (bf16[384,256]{1,0:T(8,128)(2,1)S(1)}, bf16[384,256]{1,0:T(8,128)(2,1)}, u32[]{:S(2)}) copy-start(bf16[384,256]{1,0:T(8,128)(2,1)} %constant.27.clone.fine_ref) | copy-start | bytes 589828
  31.3 27.5 %copy-start.2 = (f32[128,128]{1,0:T(8,128)S(1)}, f32[128,128]{1,0:T(8,128)}, u32[]{:S(2)}) copy-start(f32[128,128]{1,0:T(8,128)} %constant.30.clone.flip_ref) | copy-start | bytes 196612
  31.3 27.5 %copy-start.3 = (f32[2,8,8]{2,1,0:T(8,128)S(1)}, f32[2,8,8]{2,1,0:T(8,128)}, u32[]{:S(2)}) copy-start(f32[2,8,8]{2,1,0:T(8,128)} %constant.29.clone.period_ref) | copy-start | bytes 1540
  31.3 27.5 %copy-start.4 = (f32[2,8,128]{2,1,0:T(8,128)S(1)}, f32[2,8,128]{2,1,0:T(8,128)}, u32[]{:S(2)}) copy-start(f32[2,8,128]{2,1,0:T(8,128)} %constant.28.clone.coarse_ref) | copy-start | bytes 24580

commit v10 on v9

--- a/solution.py
+++ b/solution.py
@@ -317,7 +317,8 @@
         value = total[number * 8 : number * 8 + 8]
         if n == m:
             left = value - value.astype(jnp.bfloat16).astype(jnp.float32)
-            value = jnp.where(row % 4 == 1, pltpu.roll(left, 1, 0), value)
+            left = jnp.where(lane % WIDE == TERMS, 1.0, pltpu.roll(left, 1, 0))
+            value = jnp.where(row % 4 == 1, left, value)
         other = (value * conjugate).astype(jnp.bfloat16)
         value = value.astype(jnp.bfloat16)
         for pair in range(4):
@@ -395,23 +396,23 @@
     ]
 
 
-def fringe_kernel(place_ref, order_ref, z_ref, fine_ref, coarse_ref, period_ref, flip_ref, out_ref):
+def fringe_kernel(z_ref, fine_ref, coarse_ref, period_ref, flip_ref, out_ref):
     sums = [
         sum(z_ref[p, quarter].astype(jnp.float32) for quarter in range(QUARTERS))
         for p in range(PERIODS)
     ]
     real = jnp.concatenate([each[:, 0, :] for each in sums])
     imag = jnp.concatenate([each[:, 1, :] for each in sums])
-    alone = order_ref[place_ref[0] % S] == place_ref[0] // S
-    left = jnp.where(alone, 1.0, 0.0)
-    real, imag = real + left * imag, (1.0 - left) * imag
     i, j = rows_of((LANES, LANES)), lanes_of((LANES, LANES))
     spread = jnp.where(i == j // WIDE * WIDE + TERMS, 1.0, 0.0).astype(jnp.bfloat16)
-    counts = jnp.dot(
-        jnp.where(lanes_of(real.shape) % WIDE == TERMS, real, 0.0).astype(jnp.bfloat16),
+    marks = jnp.concatenate([real, imag])
+    marks = jnp.dot(
+        jnp.where(lanes_of(marks.shape) % WIDE == TERMS, marks, 0.0).astype(jnp.bfloat16),
         spread,
         preferred_element_type=jnp.float32,
     )
+    counts, alone = marks[: PERIODS * UNITS], marks[PERIODS * UNITS :] > 0.5
+    real, imag = jnp.where(alone, real + imag, real), jnp.where(alone, 0.0, imag)
     scale = 1.0 / jnp.sqrt(jnp.maximum(counts, 1.0))
     both = three_passes(
         jnp.concatenate([real * scale, imag * scale]), fine_ref[...]
@@ -455,18 +456,15 @@
     out_ref[1, 0] = turn(cosine, imag) - turn(sine, real)
 
 
-def fringed(place, order, owned):
+def fringed(owned):
     return pl.pallas_call(
         fringe_kernel,
-        in_specs=[pl.BlockSpec(memory_space=pltpu.SMEM)] * 2
-        + [pl.BlockSpec(memory_space=pltpu.VMEM)] * 5,
+        in_specs=[pl.BlockSpec(memory_space=pltpu.VMEM)] * 5,
         out_specs=pl.BlockSpec(memory_space=pltpu.VMEM),
         out_shape=jax.ShapeDtypeStruct((2, 1, PERIODS, LAGS), jnp.float32),
         compiler_params=pltpu.CompilerParams(vmem_limit_bytes=32 * 2**20),
         name="fringe",
     )(
-        place,
-        order,
         owned.reshape(PERIODS, QUARTERS, UNITS, 2, LANES),
         *fringe_tables(),
     )
@@ -481,7 +479,7 @@
     arrived = lax.all_to_all(chunks, plane, split_axis=0, concat_axis=0, tiled=True)
     rows = correlated(partner_order, arrived)
     owned = lax.all_to_all(rows, everyone, split_axis=0, concat_axis=0, tiled=True)
-    return fringed(place, partner_order, owned)
+    return fringed(owned)
 
 
 def solution(mesh):

time: 61 us -> 60.5 us (level)
  no operation moved by 1% of the time
where the time goes in v10:
time: 60.5 us; the launch traced here: 60.3 us
  blocking collectives  51.8 us (86%)
  Pallas kernels  8.48 us (14%)
    all_to_all x1, blocking collectives, per_device(): lax.all_to_all(chunks, plane, split_axis=0, concat_axis=0, tiled=True)  28.6 us
    all_to_all x1, blocking collectives, per_device(): lax.all_to_all(rows, everyone, split_axis=0, concat_axis=0, tiled=True)  23.2 us
    pallas_call x1, Pallas kernels, correlated(): pl.pallas_call(correlate_kernel, in_specs=[pl.BlockSpec(memory_space=pltp...  4.29 us
    pallas_call x1, Pallas kernels, rotated_chunks(): pl.pallas_call(rotate_kernel, in_specs=[pl.BlockSpec(memory_space=pltpu.S...  2.74 us
    pallas_call x1, Pallas kernels, fringed(): pl.pallas_call(fringe_kernel, in_specs=[pl.BlockSpec(memory_space=pltpu.V...  1.44 us

profile of v10, /device:TPU:1, one launch (start us, length us, event | category | flops | bytes accessed | tf_op | source)
XLA Modules:
  0.0 60.3 jit_solution(14766165379266632547)
XLA Ops:
  0.0 2.7 %rotate.1 = bf16[64,33,2,128]{3,2,1,0:T(2,128)(2,1)S(1)} custom-call(s32[1]{0:T(128)} %bitcast.place_ref, s32[2,4,8]{2,1,0:T(4,128)} %bitcast.7, f32[3,64]{1,0:T(4,128)} %bitcast.8, s32[2,8,4,32]{3,2,1,0:T(4,128)} %flags_hbm.1, bf16[2,8,4,2,4096]{4,3,2,1,0:T(2,128)(2,1)} %x_hbm.1), custom_call_target="tpu_custom_call" | custom-call | tf_op jit(solution)/shard_map/rotate/pallas_call | solution.py:167
  2.8 0.0 copy-start
  2.8 0.0 copy-start.5
  2.8 28.6 %all_to_all.10 = bf16[64,33,2,128]{3,2,1,0:T(2,128)(2,1)S(1)} all-to-all(bf16[64,33,2,128]{3,2,1,0:T(2,128)(2,1)S(1)} %rotate.1), channel_id=1, replica_groups=mesh['stn'=8,'quarter'=4,'unit'=8] {'stn','unit'}, dimensions={0} | all-to-all | bytes 2162688 | tf_op jit(solution)/shard_map/all_to_all | solution.py:479
  31.3 0.0 copy-start.1
  31.3 0.0 copy-start.2
  31.3 0.0 copy-start.3
  31.3 0.0 copy-start.4
  31.4 0.0 copy-done
  31.4 0.0 copy-done.5
  31.4 4.3 %correlate.1 = bf16[256,2,128]{2,1,0:T(2,128)(2,1)S(1)} custom-call(s32[16]{0:T(128)S(1)} %copy-done.5, bf16[8,8,33,2,128]{4,3,2,1,0:T(2,128)(2,1)S(1)} %bitcast.5, bf16[4,384,128]{2,1,0:T(8,128)(2,1)S(1)} %copy-done), custom_call_target="tpu_custom_call" | custom-call | tf_op jit(solution)/shard_map/correlate/pallas_call | solution.py:334
  35.7 23.2 %all_to_all.11 = bf16[256,2,128]{2,1,0:T(2,128)(2,1)S(1)} all-to-all(bf16[256,2,128]{2,1,0:T(2,128)(2,1)S(1)} %correlate.1), channel_id=1, replica_groups=mesh['stn'=8,'quarter'=4,'unit'=8] {'stn','quarter','unit'}, dimensions={0} | all-to-all | bytes 262144 | tf_op jit(solution)/shard_map/all_to_all | solution.py:481
  58.9 0.0 copy-done.1
  58.9 0.0 copy-done.2
  58.9 0.0 copy-done.3
  58.9 0.0 copy-done.4
  58.9 1.4 %fringe.1 = f32[2,1,8,256]{3,2,1,0:T(8,128)} custom-call(bf16[8,4,8,2,128]{4,3,2,1,0:T(2,128)(2,1)S(1)} %bitcast.6, bf16[384,256]{1,0:T(8,128)(2,1)S(1)} %copy-done.1, f32[2,8,128]{2,1,0:T(8,128)S(1)} %copy-done.4, f32[2,8,8]{2,1,0:T(8,128)S(1)} %copy-done.3, f32[128,128]{1,0:T(8,128)S(1)} %copy-done.2), custom_call_target="tpu_custom_call" | custom-call | tf_op jit(solution)/shard_map/fringe/pallas_call | solution.py:460
Async XLA Ops:
  2.8 28.6 %copy-start = (bf16[4,384,128]{2,1,0:T(8,128)(2,1)S(1)}, bf16[4,384,128]{2,1,0:T(8,128)(2,1)}, u32[]{:S(2)}) copy-start(bf16[4,384,128]{2,1,0:T(8,128)(2,1)} %constant.26.clone.terms_ref) | copy-start | bytes 1179652
  2.8 28.6 %copy-start.5 = (s32[16]{0:T(128)S(1)}, s32[16]{0:T(128)}, u32[]{:S(2)}) copy-start(s32[16]{0:T(128)} %order_ref.1) | copy-start | bytes 196
  31.3 27.5 %copy-start.1 = (bf16[384,256]{1,0:T(8,128)(2,1)S(1)}, bf16[384,256]{1,0:T(8,128)(2,1)}, u32[]{:S(2)}) copy-start(bf16[384,256]{1,0:T(8,128)(2,1)} %constant.27.clone.fine_ref) | copy-start | bytes 589828
  31.3 27.5 %copy-start.2 = (f32[128,128]{1,0:T(8,128)S(1)}, f32[128,128]{1,0:T(8,128)}, u32[]{:S(2)}) copy-start(f32[128,128]{1,0:T(8,128)} %constant.30.clone.flip_ref) | copy-start | bytes 196612
  31.3 27.5 %copy-start.3 = (f32[2,8,8]{2,1,0:T(8,128)S(1)}, f32[2,8,8]{2,1,0:T(8,128)}, u32[]{:S(2)}) copy-start(f32[2,8,8]{2,1,0:T(8,128)} %constant.29.clone.period_ref) | copy-start | bytes 1540
  31.3 27.5 %copy-start.4 = (f32[2,8,128]{2,1,0:T(8,128)S(1)}, f32[2,8,128]{2,1,0:T(8,128)}, u32[]{:S(2)}) copy-start(f32[2,8,128]{2,1,0:T(8,128)} %constant.28.clone.coarse_ref) | copy-start | bytes 24580

commit v11 on v10

--- a/solution.py
+++ b/solution.py
@@ -310,9 +310,9 @@
 
     lax.fori_loop(0, ITEMS, one_item, 0)
     conjugate = jnp.where(row % 2 == 0, 1.0, -1.0)
-    total = counts
-    for item in range(ITEMS):
-        total = total + three_passes(tiles[item], terms_ref[item])
+    total = counts + three_passes(
+        jnp.concatenate([tiles[item] for item in range(ITEMS)], axis=1), terms_ref[...]
+    )
     for number, (n, m) in enumerate(PAIRS):
         value = total[number * 8 : number * 8 + 8]
         if n == m:
@@ -366,7 +366,7 @@
     placed = np.zeros((ITEMS, LANES, LANES))
     for item in range(ITEMS):
         placed[item, :, item * WIDE : item * WIDE + TERMS] = table
-    return np.stack([split_table(each) for each in placed])
+    return split_table(placed.reshape(ITEMS * LANES, LANES))
 
 
 def fringe_tables():

time: 60.5 us -> 60.5 us (level)
  no operation moved by 1% of the time
where the time goes in v11:
time: 60.5 us; the launch traced here: 60.4 us
  blocking collectives  51.8 us (86%)
  Pallas kernels  8.51 us (14%)
    all_to_all x1, blocking collectives, per_device(): lax.all_to_all(chunks, plane, split_axis=0, concat_axis=0, tiled=True)  28.6 us
    all_to_all x1, blocking collectives, per_device(): lax.all_to_all(rows, everyone, split_axis=0, concat_axis=0, tiled=True)  23.2 us
    pallas_call x1, Pallas kernels, correlated(): pl.pallas_call(correlate_kernel, in_specs=[pl.BlockSpec(memory_space=pltp...  4.32 us
    pallas_call x1, Pallas kernels, rotated_chunks(): pl.pallas_call(rotate_kernel, in_specs=[pl.BlockSpec(memory_space=pltpu.S...  2.74 us
    pallas_call x1, Pallas kernels, fringed(): pl.pallas_call(fringe_kernel, in_specs=[pl.BlockSpec(memory_space=pltpu.V...  1.44 us

profile of v11, /device:TPU:1, one launch (start us, length us, event | category | flops | bytes accessed | tf_op | source)
XLA Modules:
  0.0 60.4 jit_solution(1404214505248773392)
XLA Ops:
  0.0 2.7 %rotate.1 = bf16[64,33,2,128]{3,2,1,0:T(2,128)(2,1)S(1)} custom-call(s32[1]{0:T(128)} %bitcast.place_ref, s32[2,4,8]{2,1,0:T(4,128)} %bitcast.7, f32[3,64]{1,0:T(4,128)} %bitcast.8, s32[2,8,4,32]{3,2,1,0:T(4,128)} %flags_hbm.1, bf16[2,8,4,2,4096]{4,3,2,1,0:T(2,128)(2,1)} %x_hbm.1), custom_call_target="tpu_custom_call" | custom-call | tf_op jit(solution)/shard_map/rotate/pallas_call | solution.py:167
  2.8 0.0 copy-start
  2.8 0.0 copy-start.5
  2.8 28.6 %all_to_all.10 = bf16[64,33,2,128]{3,2,1,0:T(2,128)(2,1)S(1)} all-to-all(bf16[64,33,2,128]{3,2,1,0:T(2,128)(2,1)S(1)} %rotate.1), channel_id=1, replica_groups=mesh['stn'=8,'quarter'=4,'unit'=8] {'stn','unit'}, dimensions={0} | all-to-all | bytes 2162688 | tf_op jit(solution)/shard_map/all_to_all | solution.py:479
  31.3 0.0 copy-start.1
  31.3 0.0 copy-start.2
  31.3 0.0 copy-start.3
  31.3 0.0 copy-start.4
  31.4 0.0 copy-done
  31.4 0.0 copy-done.5
  31.4 4.3 %correlate.1 = bf16[256,2,128]{2,1,0:T(2,128)(2,1)S(1)} custom-call(s32[16]{0:T(128)S(1)} %copy-done.5, bf16[8,8,33,2,128]{4,3,2,1,0:T(2,128)(2,1)S(1)} %bitcast.5, bf16[1536,128]{1,0:T(8,128)(2,1)S(1)} %copy-done), custom_call_target="tpu_custom_call" | custom-call | tf_op jit(solution)/shard_map/correlate/pallas_call | solution.py:334
  35.7 23.2 %all_to_all.11 = bf16[256,2,128]{2,1,0:T(2,128)(2,1)S(1)} all-to-all(bf16[256,2,128]{2,1,0:T(2,128)(2,1)S(1)} %correlate.1), channel_id=1, replica_groups=mesh['stn'=8,'quarter'=4,'unit'=8] {'stn','quarter','unit'}, dimensions={0} | all-to-all | bytes 262144 | tf_op jit(solution)/shard_map/all_to_all | solution.py:481
  58.9 0.0 copy-done.1
  58.9 0.0 copy-done.2
  58.9 0.0 copy-done.3
  58.9 0.0 copy-done.4
  58.9 1.4 %fringe.1 = f32[2,1,8,256]{3,2,1,0:T(8,128)} custom-call(bf16[8,4,8,2,128]{4,3,2,1,0:T(2,128)(2,1)S(1)} %bitcast.6, bf16[384,256]{1,0:T(8,128)(2,1)S(1)} %copy-done.1, f32[2,8,128]{2,1,0:T(8,128)S(1)} %copy-done.4, f32[2,8,8]{2,1,0:T(8,128)S(1)} %copy-done.3, f32[128,128]{1,0:T(8,128)S(1)} %copy-done.2), custom_call_target="tpu_custom_call" | custom-call | tf_op jit(solution)/shard_map/fringe/pallas_call | solution.py:460
Async XLA Ops:
  2.8 28.6 %copy-start = (bf16[1536,128]{1,0:T(8,128)(2,1)S(1)}, bf16[1536,128]{1,0:T(8,128)(2,1)}, u32[]{:S(2)}) copy-start(bf16[1536,128]{1,0:T(8,128)(2,1)} %constant.26.clone.terms_ref) | copy-start | bytes 1179652
  2.8 28.6 %copy-start.5 = (s32[16]{0:T(128)S(1)}, s32[16]{0:T(128)}, u32[]{:S(2)}) copy-start(s32[16]{0:T(128)} %order_ref.1) | copy-start | bytes 196
  31.3 27.6 %copy-start.1 = (bf16[384,256]{1,0:T(8,128)(2,1)S(1)}, bf16[384,256]{1,0:T(8,128)(2,1)}, u32[]{:S(2)}) copy-start(bf16[384,256]{1,0:T(8,128)(2,1)} %constant.27.clone.fine_ref) | copy-start | bytes 589828
  31.3 27.6 %copy-start.2 = (f32[128,128]{1,0:T(8,128)S(1)}, f32[128,128]{1,0:T(8,128)}, u32[]{:S(2)}) copy-start(f32[128,128]{1,0:T(8,128)} %constant.30.clone.flip_ref) | copy-start | bytes 196612
  31.3 27.6 %copy-start.3 = (f32[2,8,8]{2,1,0:T(8,128)S(1)}, f32[2,8,8]{2,1,0:T(8,128)}, u32[]{:S(2)}) copy-start(f32[2,8,8]{2,1,0:T(8,128)} %constant.29.clone.period_ref) | copy-start | bytes 1540
  31.3 27.6 %copy-start.4 = (f32[2,8,128]{2,1,0:T(8,128)S(1)}, f32[2,8,128]{2,1,0:T(8,128)}, u32[]{:S(2)}) copy-start(f32[2,8,128]{2,1,0:T(8,128)} %constant.28.clone.coarse_ref) | copy-start | bytes 24580
